TPU v7x, 32 devices: a whole 2x2x4 slice. The times are simulated.
32 devices in a mesh: region: 16 (over z, x, core), level: 2 (over y).
Axes of the slice: x: 2, y: 2, z: 4, core: 2. Of those that a mesh axis runs over, the one named last changes fastest.
Arguments:
- prior_samples: bfloat16 [256, 16, 24576], P('region', 'level'), may hold values from -6 to 6
- measured_site: int32 [8192], P('region'), may hold values from 0 to 24575
- measured_datum: float32 [8192], P('region'), may hold values from -6 to 6
- inverse_variance: float32 [8192], P('region'), may hold values from 0.5 to 8
- active_slots: int32 [16], P('region'), may hold values from 256 to 512
- cutoff_distance: int32 [16], P('region'), may hold values from 128 to 256
Outputs:
- analysis: bfloat16 [256, 16, 24576], P('region', 'level')
Inputs may be any that keep to these rules, and one draw needn't show every extreme that they name: measured_site[o] = level * 1536 + cell within its region, for a level below 16. Slots of region r at or past active_slots[r] are empty and are ignored.
All inputs are finite; a program needn't handle non-finite values.
Results may differ from a plain program's by a relative error of at most 0.00115.
The roundings to bfloat16 on the way count: a program that leaves them out, or rounds other values in their place, can miss the bound.
Values may be sent and summed in bfloat16 or wider, within the bound.
No kernel may reach another device: no remote copies, remote signals or barrier semaphores. Data moves between devices by JAX's collectives and lax.ppermute only.
A program may use at most 256 MiB of HBM per device.

v0:
```python
import functools

import jax
import jax.numpy as jnp
from jax import lax
from jax.experimental import pallas as pl
from jax.experimental.pallas import tpu as pltpu
from jax.sharding import PartitionSpec as P


COARSE = 6
SPACING = 256
NS_ITERS = 5
HALVES = 2
LANES = 128

inflation = 1.1


def gather_kernel(cell_ref, level_ref, fields_ref, out_ref):
    members, tiers, cells = fields_ref.shape
    slots = cell_ref.shape[-1]
    rows = lax.broadcasted_iota(jnp.int32, (cells, slots), 0)
    chosen = jnp.where(rows == cell_ref[0], 1.0, 0.0).astype(jnp.bfloat16)
    fields = fields_ref[...].reshape(members * tiers, cells)
    found = jnp.dot(fields, chosen, preferred_element_type=jnp.float32)
    found = found.reshape(members, tiers, slots)
    tier = lax.broadcasted_iota(jnp.int32, (members, tiers, slots), 1)
    found = jnp.where(tier == level_ref[...], found, 0.0)
    out_ref[0] = jnp.sum(found, axis=1).astype(jnp.bfloat16)


def gather_observed(prior, cell, level):
    members, tiers, total = prior.shape
    regions, _, slots = cell.shape
    cells = total // regions
    return pl.pallas_call(
        gather_kernel,
        grid=(regions,),
        in_specs=[
            pl.BlockSpec((1, 1, slots), lambda r: (r, 0, 0)),
            pl.BlockSpec((1, 1, slots), lambda r: (r, 0, 0)),
            pl.BlockSpec((members, tiers, cells), lambda r: (0, 0, r)),
        ],
        out_specs=pl.BlockSpec((1, members, slots), lambda r: (r, 0, 0)),
        out_shape=jax.ShapeDtypeStruct((regions, members, slots), jnp.bfloat16),
        name="gather_observed",
    )(cell, level, prior)


def copy_all(pairs, semaphore):
    copies = [pltpu.make_async_copy(a, b, semaphore.at[i]) for i, (a, b) in enumerate(pairs)]
    for copy in copies:
        copy.start()
    for copy in copies:
        copy.wait()


def moved(kernel, where, operands, out_shape, count, aliases=None):
    anywhere = pl.BlockSpec(memory_space=pl.ANY)
    several = isinstance(out_shape, list)
    return pl.pallas_call(
        kernel,
        in_specs=[pl.BlockSpec(memory_space=pltpu.SMEM)] + [anywhere] * len(operands),
        out_specs=[anywhere] * len(out_shape) if several else anywhere,
        out_shape=out_shape,
        scratch_shapes=[pltpu.SemaphoreType.DMA((count,))],
        input_output_aliases=aliases or {},
    )(where, *operands)


def cell_span(where_ref, rank, side, half, cells):
    chips = where_ref.shape[0] - 1
    core = where_ref[chips]
    region = where_ref[rank] * 2 + (core if side == 0 else 1 - core)
    return pl.ds(pl.multiple_of(region * (HALVES * cells) + half * cells, LANES), cells)


def cut(half, where, prior):
    chips = where.shape[0] - 1
    members, tiers, total = prior.shape
    cells = total // (2 * chips * HALVES)
    shape = jax.ShapeDtypeStruct((2, members, tiers, cells), prior.dtype)

    def kernel(where_ref, prior_ref, *refs):
        copy_all(
            [
                (
                    prior_ref.at[:, :, cell_span(where_ref, rank, side, half, cells)],
                    refs[rank].at[side],
                )
                for rank in range(chips)
                for side in range(2)
            ],
            refs[chips],
        )

    return moved(kernel, where, [prior], [shape] * chips, 2 * chips)


def hand(where, pieces):
    chips = len(pieces)
    shape = jax.ShapeDtypeStruct((chips,) + pieces[0].shape[1:], pieces[0].dtype)

    def kernel(where_ref, *refs):
        out_ref = refs[chips]
        copy_all([(refs[p].at[1], out_ref.at[p]) for p in range(chips)], refs[chips + 1])

    return moved(kernel, where, pieces, shape, chips)


def pack(where, keep, got):
    chips = keep.shape[0]
    shape = jax.ShapeDtypeStruct((2,) + keep.shape[1:], keep.dtype)

    def kernel(where_ref, keep_ref, got_ref, *refs):
        copy_all(
            [
                (source.at[p], refs[p].at[side])
                for p in range(chips)
                for side, source in enumerate((keep_ref, got_ref))
            ],
            refs[chips],
        )

    return moved(kernel, where, [keep, got], [shape] * chips, 2 * chips)


def join(half, where, blocks, shape, base):
    chips = len(blocks)
    cells = blocks[0].shape[-1]
    operands = blocks + ([] if base is None else [base])

    def kernel(where_ref, *refs):
        out_ref = refs[len(operands)]
        copy_all(
            [
                (
                    refs[rank].at[side],
                    out_ref.at[:, :, cell_span(where_ref, rank, side, half, cells)],
                )
                for rank in range(chips)
                for side in range(2)
            ],
            refs[len(operands) + 1],
        )

    aliases = None if base is None else {len(operands): 0}
    out = jax.ShapeDtypeStruct(shape, blocks[0].dtype)
    return moved(kernel, where, operands, out, 2 * chips, aliases)


def transform_kernel(first, chips, where_ref, *refs):
    pieces = refs[:chips]
    other_ref, matrices_ref, keep_ref, give_ref, work = refs[chips:]
    _, members, tiers, cells = other_ref.shape
    total = chips * 2 * members
    rows = members * tiers
    core = where_ref[chips]
    for p in range(chips):
        for side, piece in ((core, pieces[p][0]), (1 - core, other_ref[p])):
            start = pl.multiple_of((where_ref[p] * 2 + side) * rows, 8)
            piece = piece.astype(jnp.float32).reshape(rows, cells)
            for b in range(cells // LANES):
                work[b, pl.ds(start, rows), :] = piece[:, b * LANES : (b + 1) * LANES]
    offset = lax.broadcasted_iota(jnp.int32, (1, LANES), 1).astype(jnp.float32)
    half = SPACING // 2
    blocks = cells // LANES
    for b in range(blocks):
        block = first * blocks + b
        skip = (block * LANES + half) % SPACING
        frac = (offset + skip) / SPACING
        frac = jnp.concatenate([frac] * tiers, axis=1)
        values = jnp.concatenate(
            [
                work[b, pl.ds(t, total, stride=tiers), :].astype(jnp.bfloat16)
                for t in range(tiers)
            ],
            axis=1,
        )
        base = (block + 1) // 2 - (first * blocks + 1) // 2
        under = jnp.dot(matrices_ref[base], values, preferred_element_type=jnp.float32)
        over = jnp.dot(matrices_ref[base + 1], values, preferred_element_type=jnp.float32)
        mixed = (1.0 - frac) * under + frac * over
        for t in range(tiers):
            work[b, pl.ds(t, total, stride=tiers), :] = mixed[:, t * LANES : (t + 1) * LANES]
    for p in range(chips):
        for side, out_ref in ((core, keep_ref), (1 - core, give_ref)):
            start = pl.multiple_of((where_ref[p] * 2 + side) * rows, 8)
            for b in range(blocks):
                block = work[b, pl.ds(start, rows), :].reshape(members, tiers, LANES)
                out_ref[p, :, :, b * LANES : (b + 1) * LANES] = block.astype(jnp.bfloat16)


def transform(first, where, pieces, other, matrices):
    chips, members, tiers, cells = other.shape
    out = jax.ShapeDtypeStruct(other.shape, jnp.bfloat16)
    whole = pl.BlockSpec(memory_space=pltpu.VMEM)
    own = pl.BlockSpec((1, members, tiers, cells), lambda i: (i, 0, 0, 0))
    return pl.pallas_call(
        functools.partial(transform_kernel, first, chips),
        grid=(1,),
        in_specs=[pl.BlockSpec(memory_space=pltpu.SMEM)] + [own] * chips + [whole] * 2,
        out_specs=[whole, whole],
        out_shape=[out, out],
        scratch_shapes=[pltpu.VMEM((cells // LANES, chips * 2 * members * tiers, LANES), jnp.float32)],
    )(where, *pieces, other, matrices)


def local_products(window, records, radius_cells, coarse):
    values = window.astype(jnp.float32)
    centre = jnp.mean(values, axis=0)
    departure = values - centre[None, :]
    innovation = records[3] * (records[0] - centre)
    distance = (records[2][None, :] - coarse[:, None]) / radius_cells
    root_weight = jnp.sqrt(jnp.exp(-0.5 * distance * distance) * records[1][None, :])
    scaled = (departure[None, :, :] * root_weight[:, None, :]).astype(jnp.bfloat16)
    weighted = (root_weight * innovation[None, :]).astype(jnp.bfloat16)
    gram_matrix = jnp.einsum("cjo,cmo->cjm", scaled, scaled, preferred_element_type=jnp.float32)
    right_side = jnp.einsum("cjo,co->cj", scaled, weighted, preferred_element_type=jnp.float32)
    return (gram_matrix, right_side)


def ensemble_weights(gram_matrix, right_side):
    sample_runs = gram_matrix.shape[-1]
    identity = jnp.eye(sample_runs, dtype=jnp.float32)
    shifted = gram_matrix + (sample_runs - 1) / inflation * identity[None]
    frobenius = jnp.sqrt(jnp.sum(shifted * shifted, axis=(1, 2)))
    iterate = shifted / frobenius[:, None, None]
    inverse = 1.5 * identity[None] - 0.5 * iterate
    high = lax.Precision.HIGHEST
    iterate = jnp.matmul(iterate, inverse, precision=high)
    for turn in range(1, NS_ITERS):
        factor = 1.5 * identity[None] - 0.5 * jnp.matmul(inverse, iterate, precision=high)
        if turn < NS_ITERS - 1:
            iterate = jnp.matmul(iterate, factor, precision=high)
        inverse = jnp.matmul(factor, inverse, precision=high)
    spread = inverse * jnp.sqrt((sample_runs - 1.0) / frobenius)[:, None, None]
    inner_step = jnp.einsum("cjm,cm->cj", inverse, right_side, precision=high)
    centre = jnp.einsum("cjm,cm->cj", inverse, inner_step, precision=high) / frobenius[:, None]
    weights = spread + centre[:, :, None]
    weights = weights - jnp.mean(weights, axis=1, keepdims=True) + 1.0 / sample_runs
    return jnp.swapaxes(weights, 1, 2).astype(jnp.bfloat16)


def moves(regions):
    across = regions // 8
    return [(dz, dx) for dz in (3, 2, 1, 0) for dx in reversed(range(across))]


def spread(block):
    return lax.all_to_all(block, "region", split_axis=0, concat_axis=0, tiled=True)


def analyse(
    prior_samples, measured_site, measured_datum, inverse_variance, active_slots, cutoff_distance
):
    members, tiers, _ = prior_samples.shape
    regions = lax.axis_size("region")
    levels = lax.axis_size("level")
    grid_sites = COARSE * SPACING
    slots = measured_site.shape[0]
    me = lax.axis_index("region")
    tier_rank = lax.axis_index("level")
    chips = regions // 2
    across = chips // 4
    core = me % 2
    chip = me // 2
    steps = moves(regions)

    def target(chip_index, dz, dx):
        return ((chip_index // across) ^ dz) * across + ((chip_index % across) ^ dx)

    def swap(block, rank):
        dz, dx = steps[rank]
        if (dz, dx) == (0, 0):
            return block
        pairs = [(i, target(i // 2, dz, dx) * 2 + i % 2) for i in range(regions)]
        return lax.ppermute(block, "region", pairs)

    def swap_core(block):
        return lax.ppermute(block, "region", [(i, i ^ 1) for i in range(regions)])

    partners = [target(chip, dz, dx) for dz, dx in steps]
    where = jnp.stack(partners + [core]).astype(jnp.int32)

    live = jnp.arange(slots, dtype=jnp.int32) < active_slots[0]
    live_f = live.astype(jnp.float32)
    records = jnp.stack(
        [
            jnp.where(live, measured_site, -1).astype(jnp.float32),
            measured_datum,
            inverse_variance * live_f,
        ]
    )
    table = spread(jnp.broadcast_to(records[None], (regions,) + records.shape))
    sites = table[:, 0:1].astype(jnp.int32)
    cell = jnp.where(sites < 0, -1, sites % grid_sites)
    tier = jnp.where(sites < 0, -1, sites // grid_sites - tier_rank * tiers)
    observed = gather_observed(prior_samples, cell, tier)
    flip = [(i, (i + 1) % levels) for i in range(levels)]
    observed = observed + lax.ppermute(observed, "level", flip)
    observed = spread(observed)
    observed = observed.reshape(regions * members, slots)
    up = [(i, (i + 1) % regions) for i in range(regions)]
    down = [(target_, source) for source, target_ in up]
    window = jnp.concatenate(
        [lax.ppermute(observed, "region", up), observed, lax.ppermute(observed, "region", down)],
        axis=1,
    )
    near = []
    for shift in (-1, 0, 1):
        row = lax.dynamic_index_in_dim(table, (me + shift) % regions, axis=0, keepdims=False)
        site = row[0].astype(jnp.int32)
        here = (site >= 0).astype(jnp.float32)
        point = jnp.where(site < 0, 0, site % grid_sites).astype(jnp.float32)
        near.append(jnp.stack([row[1], row[2], point + shift * grid_sites, here]))
    near = jnp.concatenate(near, axis=1)
    share = COARSE // levels
    coarse = (
        SPACING // 2 + SPACING * (tier_rank * share + jnp.arange(share, dtype=jnp.int32))
    ).astype(jnp.float32)
    gram_matrix, right_side = local_products(
        window, near, cutoff_distance[0].astype(jnp.float32), coarse
    )
    weights = ensemble_weights(gram_matrix, right_side)
    opposite = lax.ppermute(weights, "level", flip)
    weights = jnp.where(
        tier_rank == 0,
        jnp.concatenate([weights, opposite]),
        jnp.concatenate([opposite, weights]),
    )
    before = lax.ppermute(weights[-1:], "region", up)
    beyond = lax.ppermute(weights[:1], "region", down)

    analysis = None
    for half in range(HALVES):
        pieces = cut(half, where, prior_samples)
        pieces = [swap(block, rank) for rank, block in enumerate(pieces)]
        other = hand(where, pieces)
        other = swap_core(other)
        if half == 0:
            matrices = jnp.concatenate([before, weights[: COARSE // 2 + 1]])
        else:
            matrices = jnp.concatenate([weights[COARSE // 2 - 1 :], beyond])
        keep, give = transform(half, where, pieces, other, matrices)
        got = swap_core(give)
        blocks = pack(where, keep, got)
        blocks = [swap(block, rank) for rank, block in enumerate(blocks)]
        analysis = join(half, where, blocks, prior_samples.shape, analysis)
    return analysis


def solution(mesh):
    return jax.shard_map(
        analyse,
        mesh=mesh,
        in_specs=(
            P("region", "level", None),
            P("region"),
            P("region"),
            P("region"),
            P("region"),
            P("region"),
        ),
        out_specs=P("region", "level", None),
        check_vma=False,
    )
```

profile of v0, /device:TPU:1, one launch (start us, length us, event | category | flops | bytes accessed | tf_op | source)
XLA Modules:
  0.0 986.0 jit_solution(8579732768797713091)
XLA Ops:
  3.4 7.3 all-to-all-start
  11.4 97.2 %shard_map.64 = (bf16[2,16,8,768]{3,2,1,0:T(8,128)(2,1)}, bf16[2,16,8,768]{3,2,1,0:T(8,128)(2,1)}, bf16[2,16,8,768]{3,2,1,0:T(8,128)(2,1)}, bf16[2,16,8,768]{3,2...) custom-call(s32[9]{0:T(128)} %stack.66.where_ref, ...), custom_call_target="tpu_custom_call" | custom-call | tf_op jit(solution)/shard_map/pallas_call | solution.py:62
  108.6 4.1 collective-permute-start
  113.6 13.0 %gather_observed.1 = bf16[16,16,512]{2,1,0:T(8,128)(2,1)} custom-call(s32[16,1,512]{2,1,0:T(1,128)} %get-tuple-element.96.cell_ref, s32[16,1,512]{2,1,0:T(1,128)} %get-tuple-element.95.level_ref, bf16[16,8,24576]{2,1,0:T(8,128)(2,1)} %prior_ref.3), custom_call_target="tpu_custom_call" | custom-call | tf_op jit(solution)/shard_map/gather_observed/pallas_call | solution.py:37
  130.4 2.0 collective-permute-start.4
  134.0 97.3 %shard_map.68 = (bf16[2,16,8,768]{3,2,1,0:T(8,128)(2,1)}, bf16[2,16,8,768]{3,2,1,0:T(8,128)(2,1)}, bf16[2,16,8,768]{3,2,1,0:T(8,128)(2,1)}, bf16[2,16,8,768]{3,2...) custom-call(s32[9]{0:T(128)} %stack.66.where_ref, ...), custom_call_target="tpu_custom_call" | custom-call | tf_op jit(solution)/shard_map/pallas_call | solution.py:62
  232.2 27.8 %all-to-all-start.1 = ((bf16[16,16,512]{2,1,0:T(8,128)(2,1)}), bf16[16,16,512]{2,1,0:T(8,128)(2,1)S(1)}, u32[]{:S(2)}, u32[]{:S(2)}) async-start(bf16[16,16,512]{2,1,0:T(8,128)(2,1)} %add.192), calls=%async_computation.1 | async-start | bytes 524288 | tf_op jit(solution)/shard_map/all_to_all | solution.py:252
  261.5 3.0 collective-permute-start.21
  266.7 2.1 collective-permute-start.24
  269.5 12.6 %collective-permute-done.6.refs_6_ = bf16[2,16,8,768]{3,2,1,0:T(8,128)(2,1)} collective-permute-done((bf16[2,16,8,768]{3,2,1,0:T(8,128)(2,1)}, bf16[2,16,8,768]{3,2,1,0:T(8,128)(2,1)}, u32[]{:S(2)}, u32[]{:S(2)}) %collective-permute-start.6) | collective-permute-done | bytes 393248 | tf_op jit(solution)/shard_map/ppermute | solution.py:279
  282.0 36.3 %collective-permute-start.26 = (bf16[2,16,8,768]{3,2,1,0:T(8,128)(2,1)}, bf16[2,16,8,768]{3,2,1,0:T(8,128)(2,1)}, u32[]{:S(2)}, u32[]{:S(2)}) collective-permute-start(bf16[2,16,8,768]{3,2,1,0:T(8,128)(2,1)} %get-tuple-element.64), channel_id=1, source_target_pairs={{0,8},{2,10},{4,12},{6,14},{8,0},{10,2},{12,4},{14,6},{16,24},{18,... | collective-permute-start | bytes 1179656 | tf_op jit(solution)/shard_map/ppermute | solution.py:279
  318.7 16.4 %collective-permute-done.23.refs_2_ = bf16[2,16,8,768]{3,2,1,0:T(8,128)(2,1)} collective-permute-done((bf16[2,16,8,768]{3,2,1,0:T(8,128)(2,1)}, bf16[2,16,8,768]{3,2,1,0:T(8,128)(2,1)}, u32[]{:S(2)}, u32[]{:S(2)}) %collective-permute-start.23) | collective-permute-done | bytes 393248 | tf_op jit(solution)/shard_map/ppermute | solution.py:279
  336.7 5.9 collective-permute-done.24.refs_3_
  342.6 2.1 collective-permute-start.9
  345.4 49.5 %shard_map.65 = bf16[8,16,8,768]{3,2,1,0:T(8,128)(2,1)} custom-call(s32[9]{0:T(128)} %stack.66.where_ref, bf16[2,16,8,768]{3,2,1,0:T(8,128)(2,1)} %copy-done.2, bf16[2,16,8,768]{3,2,1,0:T(8,128)(2,1)} %copy-done.3, bf16[2,16,8,768]{3,2,1,0:T(8,128)(2,1)} %copy-done.4, bf16[2,16,8,768]{3,2,1,0:T(8,128)(2,1)} %copy-done.5, bf16[2,16,8,768]{3,2,1,0:T(8,128)(2,1)} %copy-done.6, ...), custom_call_target="tpu_custom_call" | custom-call | tf_op jit(solution)/shard_map/pallas_call | solution.py:62
  395.0 49.6 %shard_map.69 = bf16[8,16,8,768]{3,2,1,0:T(8,128)(2,1)} custom-call(s32[9]{0:T(128)} %stack.66.where_ref, bf16[2,16,8,768]{3,2,1,0:T(8,128)(2,1)} %copy-done.8, bf16[2,16,8,768]{3,2,1,0:T(8,128)(2,1)} %copy-done.9, bf16[2,16,8,768]{3,2,1,0:T(8,128)(2,1)} %collective-permute-done.23.refs_2_, bf16[2,16,8,768]{3,2,1,0:T(8,128)(2,1)} %collective-permute-done.24.refs_3_, ...), custom_call_target="tpu_custom_call" | custom-call | tf_op jit(solution)/shard_map/pallas_call | solution.py:62
  465.3 9.5 collective-permute-done.11
  474.9 2.1 collective-permute-start.29
  477.1 5.7 collective-permute-done.12
  483.7 7.4 shard_map.66
  493.3 7.4 shard_map.70
  501.3 97.2 %shard_map.67 = (bf16[2,16,8,768]{3,2,1,0:T(8,128)(2,1)}, bf16[2,16,8,768]{3,2,1,0:T(8,128)(2,1)}, bf16[2,16,8,768]{3,2,1,0:T(8,128)(2,1)}, bf16[2,16,8,768]{3,2...) custom-call(s32[9]{0:T(128)} %stack.66.where_ref, ...), custom_call_target="tpu_custom_call" | custom-call | tf_op jit(solution)/shard_map/pallas_call | solution.py:62
  598.5 4.0 collective-permute-start.14
  603.6 97.2 %shard_map.71 = (bf16[2,16,8,768]{3,2,1,0:T(8,128)(2,1)}, bf16[2,16,8,768]{3,2,1,0:T(8,128)(2,1)}, bf16[2,16,8,768]{3,2,1,0:T(8,128)(2,1)}, bf16[2,16,8,768]{3,2...) custom-call(s32[9]{0:T(128)} %stack.66.where_ref, ...), custom_call_target="tpu_custom_call" | custom-call | tf_op jit(solution)/shard_map/pallas_call | solution.py:62
  704.4 3.0 collective-permute-start.34
  708.7 5.6 collective-permute-done.31.refs_0_
  714.2 32.7 %collective-permute-start.36 = (bf16[2,16,8,768]{3,2,1,0:T(8,128)(2,1)}, bf16[2,16,8,768]{3,2,1,0:T(8,128)(2,1)S(1)}, u32[]{:S(2)}, u32[]{:S(2)}) collective-permute-start(bf16[2,16,8,768]{3,2,1,0:T(8,128)(2,1)} %get-tuple-element.74), channel_id=1, source_target_pairs={{0,8},{2,10},{4,12},{6,14},{8,0},{10,2},{12,4},{14,6},{16,24},{18,... | collective-permute-start | bytes 1179656 | tf_op jit(solution)/shard_map/ppermute | solution.py:279
  748.6 14.4 %collective-permute-done.33.refs_2_ = bf16[2,16,8,768]{3,2,1,0:T(8,128)(2,1)S(1)} collective-permute-done((bf16[2,16,8,768]{3,2,1,0:T(8,128)(2,1)}, bf16[2,16,8,768]{3,2,1,0:T(8,128)(2,1)S(1)}, u32[]{:S(2)}, u32[]{:S(2)}) %collective-permute-start.33) | collective-permute-done | bytes 393248 | tf_op jit(solution)/shard_map/ppermute | solution.py:279
  763.0 17.3 %collective-permute-done.34.refs_3_ = bf16[2,16,8,768]{3,2,1,0:T(8,128)(2,1)S(1)} collective-permute-done((bf16[2,16,8,768]{3,2,1,0:T(8,128)(2,1)}, bf16[2,16,8,768]{3,2,1,0:T(8,128)(2,1)S(1)}, u32[]{:S(2)}, u32[]{:S(2)}) %collective-permute-start.34) | collective-permute-done | bytes 393248 | tf_op jit(solution)/shard_map/ppermute | solution.py:279
  780.3 10.1 %collective-permute-start.18 = (bf16[2,16,8,768]{3,2,1,0:T(8,128)(2,1)}, bf16[2,16,8,768]{3,2,1,0:T(8,128)(2,1)}, u32[]{:S(2)}, u32[]{:S(2)}) collective-permute-start(bf16[2,16,8,768]{3,2,1,0:T(8,128)(2,1)} %get-tuple-element.55), channel_id=1, source_target_pairs={{0,12},{2,14},{4,8},{6,10},{8,4},{10,6},{12,0},{14,2},{16,28},{18,... | collective-permute-start | bytes 1179656 | tf_op jit(solution)/shard_map/ppermute | solution.py:279
  791.3 97.2 %shard_map.72.refs_8_ = bf16[16,8,24576]{2,1,0:T(8,128)(2,1)} custom-call(s32[9]{0:T(128)} %stack.66.where_ref, bf16[2,16,8,768]{3,2,1,0:T(8,128)(2,1)} %copy-done.11, bf16[2,16,8,768]{3,2,1,0:T(8,128)(2,1)} %copy-done.12, bf16[2,16,8,768]{3,2,1,0:T(8,128)(2,1)} %copy-done.13, bf16[2,16,8,768]{3,2,1,0:T(8,128)(2,1)} %copy-done.14, ...), custom_call_target="tpu_custom_call" | custom-call | tf_op jit(solution)/shard_map/pallas_call | solution.py:62
  888.6 97.2 %shard_map.73 = bf16[16,8,24576]{2,1,0:T(8,128)(2,1)} custom-call(s32[9]{0:T(128)} %stack.66.where_ref, bf16[2,16,8,768]{3,2,1,0:T(8,128)(2,1)} %copy-done.18, bf16[2,16,8,768]{3,2,1,0:T(8,128)(2,1)} %copy-done.19, bf16[2,16,8,768]{3,2,1,0:T(8,128)(2,1)} %collective-permute-done.16.refs_2_, ...), custom_call_target="tpu_custom_call", output_to_operand_aliasing={{}: (9, {})} | custom-call | tf_op jit(solution)/shard_map/pallas_call | solution.py:62
  (152 shorter events, 49.8 us)
Async XLA Ops:
  3.4 109.3 %all-to-all-start = ((f32[16,3,512]{2,1,0:T(4,128)}), f32[16,3,512]{2,1,0:T(4,128)S(1)}, u32[]{:S(2)}, u32[]{:S(2)}) async-start(f32[16,3,512]{2,1,0:T(4,128)} %broadcast_in_dim.16), calls=%async_computation | async-start | bytes 262144 | tf_op jit(solution)/shard_map/all_to_all | solution.py:252
  127.9 132.2 %collective-permute-start.1 = (bf16[2,16,8,768]{3,2,1,0:T(8,128)(2,1)}, bf16[2,16,8,768]{3,2,1,0:T(8,128)(2,1)S(1)}, u32[]{:S(2)}, u32[]{:S(2)}) collective-permute-start(bf16[2,16,8,768]{3,2,1,0:T(8,128)(2,1)} %get-tuple-element.42), channel_id=1, source_target_pairs={{0,24},{2,26},{4,28},{6,30},{8,16},{10,18},{12,20},{14,22},{16,8},... | collective-permute-start | bytes 1179656 | tf_op jit(solution)/shard_map/ppermute | solution.py:279
  128.2 133.3 %collective-permute-start.2 = (bf16[2,16,8,768]{3,2,1,0:T(8,128)(2,1)}, bf16[2,16,8,768]{3,2,1,0:T(8,128)(2,1)S(1)}, u32[]{:S(2)}, u32[]{:S(2)}) collective-permute-start(bf16[2,16,8,768]{3,2,1,0:T(8,128)(2,1)} %get-tuple-element.43), channel_id=1, source_target_pairs={{0,20},{2,22},{4,16},{6,18},{8,28},{10,30},{12,24},{14,26},{16,4},... | collective-permute-start | bytes 1179656 | tf_op jit(solution)/shard_map/ppermute | solution.py:279
  128.4 136.0 %collective-permute-start.3 = (bf16[2,16,8,768]{3,2,1,0:T(8,128)(2,1)}, bf16[2,16,8,768]{3,2,1,0:T(8,128)(2,1)S(1)}, u32[]{:S(2)}, u32[]{:S(2)}) collective-permute-start(bf16[2,16,8,768]{3,2,1,0:T(8,128)(2,1)} %get-tuple-element.44), channel_id=1, source_target_pairs={{0,16},{2,18},{4,20},{6,22},{8,24},{10,26},{12,28},{14,30},{16,0},... | collective-permute-start | bytes 1179656 | tf_op jit(solution)/shard_map/ppermute | solution.py:279
  130.4 135.0 %collective-permute-start.4 = (bf16[2,16,8,768]{3,2,1,0:T(8,128)(2,1)}, bf16[2,16,8,768]{3,2,1,0:T(8,128)(2,1)S(1)}, u32[]{:S(2)}, u32[]{:S(2)}) collective-permute-start(bf16[2,16,8,768]{3,2,1,0:T(8,128)(2,1)} %get-tuple-element.45), channel_id=1, source_target_pairs={{0,12},{2,14},{4,8},{6,10},{8,4},{10,6},{12,0},{14,2},{16,28},{18,... | collective-permute-start | bytes 1179656 | tf_op jit(solution)/shard_map/ppermute | solution.py:279
  134.0 132.6 %collective-permute-start.5 = (bf16[2,16,8,768]{3,2,1,0:T(8,128)(2,1)}, bf16[2,16,8,768]{3,2,1,0:T(8,128)(2,1)S(1)}, u32[]{:S(2)}, u32[]{:S(2)}) collective-permute-start(bf16[2,16,8,768]{3,2,1,0:T(8,128)(2,1)} %get-tuple-element.46), channel_id=1, source_target_pairs={{0,8},{2,10},{4,12},{6,14},{8,0},{10,2},{12,4},{14,6},{16,24},{18,... | collective-permute-start | bytes 1179656 | tf_op jit(solution)/shard_map/ppermute | solution.py:279
  232.2 102.9 %all-to-all-start.1 = ((bf16[16,16,512]{2,1,0:T(8,128)(2,1)}), bf16[16,16,512]{2,1,0:T(8,128)(2,1)S(1)}, u32[]{:S(2)}, u32[]{:S(2)}) async-start(bf16[16,16,512]{2,1,0:T(8,128)(2,1)} %add.192), calls=%async_computation.1 | async-start | bytes 524288 | tf_op jit(solution)/shard_map/all_to_all | solution.py:252
  260.1 22.0 %collective-permute-start.6 = (bf16[2,16,8,768]{3,2,1,0:T(8,128)(2,1)}, bf16[2,16,8,768]{3,2,1,0:T(8,128)(2,1)}, u32[]{:S(2)}, u32[]{:S(2)}) collective-permute-start(bf16[2,16,8,768]{3,2,1,0:T(8,128)(2,1)} %get-tuple-element.47), channel_id=1, source_target_pairs={{0,4},{2,6},{4,0},{6,2},{8,12},{10,14},{12,8},{14,10},{16,20},{18,... | collective-permute-start | bytes 1179656 | tf_op jit(solution)/shard_map/ppermute | solution.py:279
  264.5 53.9 %collective-permute-start.22 = (bf16[2,16,8,768]{3,2,1,0:T(8,128)(2,1)}, bf16[2,16,8,768]{3,2,1,0:T(8,128)(2,1)S(1)}, u32[]{:S(2)}, u32[]{:S(2)}) collective-permute-start(bf16[2,16,8,768]{3,2,1,0:T(8,128)(2,1)} %get-tuple-element.60), channel_id=1, source_target_pairs={{0,24},{2,26},{4,28},{6,30},{8,16},{10,18},{12,20},{14,22},{16,8},... | collective-permute-start | bytes 1179656 | tf_op jit(solution)/shard_map/ppermute | solution.py:279
  265.4 69.7 %collective-permute-start.23 = (bf16[2,16,8,768]{3,2,1,0:T(8,128)(2,1)}, bf16[2,16,8,768]{3,2,1,0:T(8,128)(2,1)}, u32[]{:S(2)}, u32[]{:S(2)}) collective-permute-start(bf16[2,16,8,768]{3,2,1,0:T(8,128)(2,1)} %get-tuple-element.61), channel_id=1, source_target_pairs={{0,20},{2,22},{4,16},{6,18},{8,28},{10,30},{12,24},{14,26},{16,4},... | collective-permute-start | bytes 1179656 | tf_op jit(solution)/shard_map/ppermute | solution.py:279
  266.7 75.9 %collective-permute-start.24 = (bf16[2,16,8,768]{3,2,1,0:T(8,128)(2,1)}, bf16[2,16,8,768]{3,2,1,0:T(8,128)(2,1)}, u32[]{:S(2)}, u32[]{:S(2)}) collective-permute-start(bf16[2,16,8,768]{3,2,1,0:T(8,128)(2,1)} %get-tuple-element.62), channel_id=1, source_target_pairs={{0,16},{2,18},{4,20},{6,22},{8,24},{10,26},{12,28},{14,30},{16,0},... | collective-permute-start | bytes 1179656 | tf_op jit(solution)/shard_map/ppermute | solution.py:279
  282.0 112.9 %collective-permute-start.25 = (bf16[2,16,8,768]{3,2,1,0:T(8,128)(2,1)}, bf16[2,16,8,768]{3,2,1,0:T(8,128)(2,1)}, u32[]{:S(2)}, u32[]{:S(2)}) collective-permute-start(bf16[2,16,8,768]{3,2,1,0:T(8,128)(2,1)} %get-tuple-element.63), channel_id=1, source_target_pairs={{0,12},{2,14},{4,8},{6,10},{8,4},{10,6},{12,0},{14,2},{16,28},{18,... | collective-permute-start | bytes 1179656 | tf_op jit(solution)/shard_map/ppermute | solution.py:279
  282.0 113.0 %collective-permute-start.26 = (bf16[2,16,8,768]{3,2,1,0:T(8,128)(2,1)}, bf16[2,16,8,768]{3,2,1,0:T(8,128)(2,1)}, u32[]{:S(2)}, u32[]{:S(2)}) collective-permute-start(bf16[2,16,8,768]{3,2,1,0:T(8,128)(2,1)} %get-tuple-element.64), channel_id=1, source_target_pairs={{0,8},{2,10},{4,12},{6,14},{8,0},{10,2},{12,4},{14,6},{16,24},{18,... | collective-permute-start | bytes 1179656 | tf_op jit(solution)/shard_map/ppermute | solution.py:279
  318.4 76.6 %collective-permute-start.27 = (bf16[2,16,8,768]{3,2,1,0:T(8,128)(2,1)}, bf16[2,16,8,768]{3,2,1,0:T(8,128)(2,1)}, u32[]{:S(2)}, u32[]{:S(2)}) collective-permute-start(bf16[2,16,8,768]{3,2,1,0:T(8,128)(2,1)} %get-tuple-element.65), channel_id=1, source_target_pairs={{0,4},{2,6},{4,0},{6,2},{8,12},{10,14},{12,8},{14,10},{16,20},{18,... | collective-permute-start | bytes 1179656 | tf_op jit(solution)/shard_map/ppermute | solution.py:279
  335.1 110.1 %collective-permute-start.10 = (bf16[256,512]{1,0:T(8,128)(2,1)S(1)}, bf16[256,512]{1,0:T(8,128)(2,1)}, u32[]{:S(2)}, u32[]{:S(2)}) collective-permute-start(bf16[256,512]{1,0:T(8,128)(2,1)S(1)} %bitcast.95), channel_id=1, source_target_pairs={{2,0},{4,2},{6,4},{8,6},{10,8},{12,10},{14,12},{16,14},{18,16},{20... | collective-permute-start | bytes 786440 | tf_op jit(solution)/shard_map/ppermute | solution.py:308
  342.6 102.6 %collective-permute-start.9 = (bf16[256,512]{1,0:T(8,128)(2,1)S(1)}, bf16[256,512]{1,0:T(8,128)(2,1)}, u32[]{:S(2)}, u32[]{:S(2)}) collective-permute-start(bf16[256,512]{1,0:T(8,128)(2,1)S(1)} %bitcast.96), channel_id=1, source_target_pairs={{0,2},{2,4},{4,6},{6,8},{8,10},{10,12},{12,14},{14,16},{16,18},{18... | collective-permute-start | bytes 786440 | tf_op jit(solution)/shard_map/ppermute | solution.py:308
  394.9 88.8 %collective-permute-start.7 = (bf16[8,16,8,768]{3,2,1,0:T(8,128)(2,1)}, bf16[8,16,8,768]{3,2,1,0:T(8,128)(2,1)}, u32[]{:S(2)}, u32[]{:S(2)}) collective-permute-start(bf16[8,16,8,768]{3,2,1,0:T(8,128)(2,1)} %shard_map.65), channel_id=1, source_target_pairs={{0,2},{2,0},{4,6},{6,4},{8,10},{10,8},{12,14},{14,12},{16,18},{18,... | collective-permute-start | bytes 4718600 | tf_op jit(solution)/shard_map/ppermute | solution.py:282
  444.7 47.4 %collective-permute-start.28 = (bf16[8,16,8,768]{3,2,1,0:T(8,128)(2,1)}, bf16[8,16,8,768]{3,2,1,0:T(8,128)(2,1)S(1)}, u32[]{:S(2)}, u32[]{:S(2)}) collective-permute-start(bf16[8,16,8,768]{3,2,1,0:T(8,128)(2,1)} %shard_map.69), channel_id=1, source_target_pairs={{0,2},{2,0},{4,6},{6,4},{8,10},{10,8},{12,14},{14,12},{16,18},{18,... | collective-permute-start | bytes 4718600 | tf_op jit(solution)/shard_map/ppermute | solution.py:282
  500.8 101.7 %collective-permute-start.30 = (bf16[8,16,8,768]{3,2,1,0:T(8,128)(2,1)}, bf16[8,16,8,768]{3,2,1,0:T(8,128)(2,1)S(1)}, u32[]{:S(2)}, u32[]{:S(2)}) collective-permute-start(bf16[8,16,8,768]{3,2,1,0:T(8,128)(2,1)} %get-tuple-element.68), channel_id=1, source_target_pairs={{0,2},{2,0},{4,6},{6,4},{8,10},{10,8},{12,14},{14,12},{16,18},{18,... | collective-permute-start | bytes 4718600 | tf_op jit(solution)/shard_map/ppermute | solution.py:282
  598.5 105.9 %collective-permute-start.14 = (bf16[2,16,8,768]{3,2,1,0:T(8,128)(2,1)}, bf16[2,16,8,768]{3,2,1,0:T(8,128)(2,1)S(1)}, u32[]{:S(2)}, u32[]{:S(2)}) collective-permute-start(bf16[2,16,8,768]{3,2,1,0:T(8,128)(2,1)} %get-tuple-element.51), channel_id=1, source_target_pairs={{0,28},{2,30},{4,24},{6,26},{8,20},{10,22},{12,16},{14,18},{16,12}... | collective-permute-start | bytes 1179656 | tf_op jit(solution)/shard_map/ppermute | solution.py:279
  602.4 105.0 %collective-permute-start.15 = (bf16[2,16,8,768]{3,2,1,0:T(8,128)(2,1)}, bf16[2,16,8,768]{3,2,1,0:T(8,128)(2,1)S(1)}, u32[]{:S(2)}, u32[]{:S(2)}) collective-permute-start(bf16[2,16,8,768]{3,2,1,0:T(8,128)(2,1)} %get-tuple-element.52), channel_id=1, source_target_pairs={{0,24},{2,26},{4,28},{6,30},{8,16},{10,18},{12,20},{14,22},{16,8},... | collective-permute-start | bytes 1179656 | tf_op jit(solution)/shard_map/ppermute | solution.py:279
  702.8 44.1 %collective-permute-start.32 = (bf16[2,16,8,768]{3,2,1,0:T(8,128)(2,1)}, bf16[2,16,8,768]{3,2,1,0:T(8,128)(2,1)S(1)}, u32[]{:S(2)}, u32[]{:S(2)}) collective-permute-start(bf16[2,16,8,768]{3,2,1,0:T(8,128)(2,1)} %get-tuple-element.70), channel_id=1, source_target_pairs={{0,24},{2,26},{4,28},{6,30},{8,16},{10,18},{12,20},{14,22},{16,8},... | collective-permute-start | bytes 1179656 | tf_op jit(solution)/shard_map/ppermute | solution.py:279
  704.4 58.6 %collective-permute-start.33 = (bf16[2,16,8,768]{3,2,1,0:T(8,128)(2,1)}, bf16[2,16,8,768]{3,2,1,0:T(8,128)(2,1)S(1)}, u32[]{:S(2)}, u32[]{:S(2)}) collective-permute-start(bf16[2,16,8,768]{3,2,1,0:T(8,128)(2,1)} %get-tuple-element.71), channel_id=1, source_target_pairs={{0,20},{2,22},{4,16},{6,18},{8,28},{10,30},{12,24},{14,26},{16,4},... | collective-permute-start | bytes 1179656 | tf_op jit(solution)/shard_map/ppermute | solution.py:279
  704.4 75.9 %collective-permute-start.34 = (bf16[2,16,8,768]{3,2,1,0:T(8,128)(2,1)}, bf16[2,16,8,768]{3,2,1,0:T(8,128)(2,1)S(1)}, u32[]{:S(2)}, u32[]{:S(2)}) collective-permute-start(bf16[2,16,8,768]{3,2,1,0:T(8,128)(2,1)} %get-tuple-element.72), channel_id=1, source_target_pairs={{0,16},{2,18},{4,20},{6,22},{8,24},{10,26},{12,28},{14,30},{16,0},... | collective-permute-start | bytes 1179656 | tf_op jit(solution)/shard_map/ppermute | solution.py:279
  707.4 72.9 %collective-permute-start.35 = (bf16[2,16,8,768]{3,2,1,0:T(8,128)(2,1)}, bf16[2,16,8,768]{3,2,1,0:T(8,128)(2,1)S(1)}, u32[]{:S(2)}, u32[]{:S(2)}) collective-permute-start(bf16[2,16,8,768]{3,2,1,0:T(8,128)(2,1)} %get-tuple-element.73), channel_id=1, source_target_pairs={{0,12},{2,14},{4,8},{6,10},{8,4},{10,6},{12,0},{14,2},{16,28},{18,... | collective-permute-start | bytes 1179656 | tf_op jit(solution)/shard_map/ppermute | solution.py:279
  714.2 76.2 %collective-permute-start.36 = (bf16[2,16,8,768]{3,2,1,0:T(8,128)(2,1)}, bf16[2,16,8,768]{3,2,1,0:T(8,128)(2,1)S(1)}, u32[]{:S(2)}, u32[]{:S(2)}) collective-permute-start(bf16[2,16,8,768]{3,2,1,0:T(8,128)(2,1)} %get-tuple-element.74), channel_id=1, source_target_pairs={{0,8},{2,10},{4,12},{6,14},{8,0},{10,2},{12,4},{14,6},{16,24},{18,... | collective-permute-start | bytes 1179656 | tf_op jit(solution)/shard_map/ppermute | solution.py:279
  746.9 43.5 %collective-permute-start.37 = (bf16[2,16,8,768]{3,2,1,0:T(8,128)(2,1)}, bf16[2,16,8,768]{3,2,1,0:T(8,128)(2,1)S(1)}, u32[]{:S(2)}, u32[]{:S(2)}) collective-permute-start(bf16[2,16,8,768]{3,2,1,0:T(8,128)(2,1)} %get-tuple-element.75), channel_id=1, source_target_pairs={{0,4},{2,6},{4,0},{6,2},{8,12},{10,14},{12,8},{14,10},{16,20},{18,... | collective-permute-start | bytes 1179656 | tf_op jit(solution)/shard_map/ppermute | solution.py:279
  763.0 125.6 %collective-permute-start.16 = (bf16[2,16,8,768]{3,2,1,0:T(8,128)(2,1)}, bf16[2,16,8,768]{3,2,1,0:T(8,128)(2,1)}, u32[]{:S(2)}, u32[]{:S(2)}) collective-permute-start(bf16[2,16,8,768]{3,2,1,0:T(8,128)(2,1)} %get-tuple-element.53), channel_id=1, source_target_pairs={{0,20},{2,22},{4,16},{6,18},{8,28},{10,30},{12,24},{14,26},{16,4},... | collective-permute-start | bytes 1179656 | tf_op jit(solution)/shard_map/ppermute | solution.py:279
  780.3 108.3 %collective-permute-start.17 = (bf16[2,16,8,768]{3,2,1,0:T(8,128)(2,1)}, bf16[2,16,8,768]{3,2,1,0:T(8,128)(2,1)}, u32[]{:S(2)}, u32[]{:S(2)}) collective-permute-start(bf16[2,16,8,768]{3,2,1,0:T(8,128)(2,1)} %get-tuple-element.54), channel_id=1, source_target_pairs={{0,16},{2,18},{4,20},{6,22},{8,24},{10,26},{12,28},{14,30},{16,0},... | collective-permute-start | bytes 1179656 | tf_op jit(solution)/shard_map/ppermute | solution.py:279
  780.3 108.3 %collective-permute-start.18 = (bf16[2,16,8,768]{3,2,1,0:T(8,128)(2,1)}, bf16[2,16,8,768]{3,2,1,0:T(8,128)(2,1)}, u32[]{:S(2)}, u32[]{:S(2)}) collective-permute-start(bf16[2,16,8,768]{3,2,1,0:T(8,128)(2,1)} %get-tuple-element.55), channel_id=1, source_target_pairs={{0,12},{2,14},{4,8},{6,10},{8,4},{10,6},{12,0},{14,2},{16,28},{18,... | collective-permute-start | bytes 1179656 | tf_op jit(solution)/shard_map/ppermute | solution.py:279
  790.4 98.2 %collective-permute-start.19 = (bf16[2,16,8,768]{3,2,1,0:T(8,128)(2,1)}, bf16[2,16,8,768]{3,2,1,0:T(8,128)(2,1)}, u32[]{:S(2)}, u32[]{:S(2)}) collective-permute-start(bf16[2,16,8,768]{3,2,1,0:T(8,128)(2,1)} %get-tuple-element.56), channel_id=1, source_target_pairs={{0,8},{2,10},{4,12},{6,14},{8,0},{10,2},{12,4},{14,6},{16,24},{18,... | collective-permute-start | bytes 1179656 | tf_op jit(solution)/shard_map/ppermute | solution.py:279
  790.4 98.2 %collective-permute-start.20 = (bf16[2,16,8,768]{3,2,1,0:T(8,128)(2,1)}, bf16[2,16,8,768]{3,2,1,0:T(8,128)(2,1)}, u32[]{:S(2)}, u32[]{:S(2)}) collective-permute-start(bf16[2,16,8,768]{3,2,1,0:T(8,128)(2,1)} %get-tuple-element.57), channel_id=1, source_target_pairs={{0,4},{2,6},{4,0},{6,2},{8,12},{10,14},{12,8},{14,10},{16,20},{18,... | collective-permute-start | bytes 1179656 | tf_op jit(solution)/shard_map/ppermute | solution.py:279
  (30 other events, 1496.4 us)
where the time goes:
time: 990 us; the launch traced here: 986 us
  Pallas kernels  710 us (72%)
  starting transfers between devices  155 us (16%)
  waiting for transfers between devices  89 us (9%)
  matrix products  14.7 us (1%)
  other arithmetic  10.3 us (1%)
    pallas_call x8, Pallas kernels, moved(): pl.pallas_call(kernel, in_specs=[pl.BlockSpec(memory_space=pltpu.SMEM)] +...  682 us
    ppermute x28, starting transfers between devices, swap(): return lax.ppermute(block, 'region', pairs)  110 us
    ppermute x28, waiting for transfers between devices, swap(): return lax.ppermute(block, 'region', pairs)  72.2 us
    all_to_all x2, starting transfers between devices, spread(): lax.all_to_all(block, 'region', split_axis=0, concat_axis=0, tiled=True)  35.2 us
  transfers between devices with their start and end apart: 40, of which 9 were waited for; matrix products, arithmetic and copies ran while one was open for 2% of the time, Pallas kernels for 62%

commit v1 on v0

--- a/solution.py
+++ b/solution.py
@@ -48,15 +48,28 @@
     )(cell, level, prior)
 
 
-def copy_all(pairs, semaphore):
-    copies = [pltpu.make_async_copy(a, b, semaphore.at[i]) for i, (a, b) in enumerate(pairs)]
-    for copy in copies:
+def copy_all(reads, writes, arrived, left):
+    share = len(reads) // len(writes)
+    into = [pltpu.make_async_copy(a, b, arrived.at[i]) for i, (a, b) in enumerate(reads)]
+    onward = [pltpu.make_async_copy(a, b, left.at[i]) for i, (a, b) in enumerate(writes)]
+    for copy in into:
         copy.start()
-    for copy in copies:
+    if share:
+        for i, copy in enumerate(onward):
+            for part in into[i * share : (i + 1) * share]:
+                part.wait()
+            copy.start()
+    else:
+        share = len(writes) // len(reads)
+        for i, copy in enumerate(into):
+            copy.wait()
+            for part in onward[i * share : (i + 1) * share]:
+                part.start()
+    for copy in onward:
         copy.wait()
 
 
-def moved(kernel, where, operands, out_shape, count, aliases=None):
+def moved(kernel, where, operands, out_shape, block, count, aliases=None):
     anywhere = pl.BlockSpec(memory_space=pl.ANY)
     several = isinstance(out_shape, list)
     return pl.pallas_call(
@@ -64,38 +77,49 @@
         in_specs=[pl.BlockSpec(memory_space=pltpu.SMEM)] + [anywhere] * len(operands),
         out_specs=[anywhere] * len(out_shape) if several else anywhere,
         out_shape=out_shape,
-        scratch_shapes=[pltpu.SemaphoreType.DMA((count,))],
+        scratch_shapes=[
+            pltpu.VMEM((count,) + block, jnp.bfloat16),
+            pltpu.SemaphoreType.DMA((2 * count,)),
+            pltpu.SemaphoreType.DMA((2 * count,)),
+        ],
         input_output_aliases=aliases or {},
     )(where, *operands)
 
 
-def cell_span(where_ref, rank, side, half, cells):
+def spans(half, cells):
+    shift = SPACING // 2
+    if half < HALVES - 1:
+        return [(0, half * cells + shift, cells)]
+    return [(0, half * cells + shift, cells - shift), (cells - shift, 0, shift)]
+
+
+def cell_spans(where_ref, rank, side, half, cells):
     chips = where_ref.shape[0] - 1
     core = where_ref[chips]
     region = where_ref[rank] * 2 + (core if side == 0 else 1 - core)
-    return pl.ds(pl.multiple_of(region * (HALVES * cells) + half * cells, LANES), cells)
-
-
-def cut(half, where, prior):
+    for lane, cell, count in spans(half, cells):
+        first = pl.multiple_of(region * (HALVES * cells) + cell, LANES)
+        yield pl.ds(lane, count), pl.ds(first, count)
+
+
+def cut(half, where, prior, ranks):
     chips = where.shape[0] - 1
     members, tiers, total = prior.shape
     cells = total // (2 * chips * HALVES)
     shape = jax.ShapeDtypeStruct((2, members, tiers, cells), prior.dtype)
 
     def kernel(where_ref, prior_ref, *refs):
-        copy_all(
-            [
-                (
-                    prior_ref.at[:, :, cell_span(where_ref, rank, side, half, cells)],
-                    refs[rank].at[side],
-                )
-                for rank in range(chips)
-                for side in range(2)
-            ],
-            refs[chips],
-        )
-
-    return moved(kernel, where, [prior], [shape] * chips, 2 * chips)
+        reads, writes = [], []
+        stage, arrived, left = refs[len(ranks) :]
+        for i, rank in enumerate(ranks):
+            for side in range(2):
+                slot = stage.at[2 * i + side]
+                for lanes, source in cell_spans(where_ref, rank, side, half, cells):
+                    reads.append((prior_ref.at[:, :, source], slot.at[:, :, lanes]))
+                writes.append((slot, refs[i].at[side]))
+        copy_all(reads, writes, arrived, left)
+
+    return moved(kernel, where, [prior], [shape] * len(ranks), shape.shape[1:], 2 * len(ranks))
 
 
 def hand(where, pieces):
@@ -103,10 +127,15 @@
     shape = jax.ShapeDtypeStruct((chips,) + pieces[0].shape[1:], pieces[0].dtype)
 
     def kernel(where_ref, *refs):
-        out_ref = refs[chips]
-        copy_all([(refs[p].at[1], out_ref.at[p]) for p in range(chips)], refs[chips + 1])
-
-    return moved(kernel, where, pieces, shape, chips)
+        out_ref, stage, arrived, left = refs[chips:]
+        copy_all(
+            [(refs[p].at[1], stage.at[p]) for p in range(chips)],
+            [(stage.at[p], out_ref.at[p]) for p in range(chips)],
+            arrived,
+            left,
+        )
+
+    return moved(kernel, where, pieces, shape, shape.shape[1:], chips)
 
 
 def pack(where, keep, got):
@@ -114,40 +143,36 @@
     shape = jax.ShapeDtypeStruct((2,) + keep.shape[1:], keep.dtype)
 
     def kernel(where_ref, keep_ref, got_ref, *refs):
-        copy_all(
-            [
-                (source.at[p], refs[p].at[side])
-                for p in range(chips)
-                for side, source in enumerate((keep_ref, got_ref))
-            ],
-            refs[chips],
-        )
-
-    return moved(kernel, where, [keep, got], [shape] * chips, 2 * chips)
-
-
-def join(half, where, blocks, shape, base):
-    chips = len(blocks)
+        stage, arrived, left = refs[chips:]
+        reads, writes = [], []
+        for p in range(chips):
+            for side, source in enumerate((keep_ref, got_ref)):
+                slot = stage.at[2 * p + side]
+                reads.append((source.at[p], slot))
+                writes.append((slot, refs[p].at[side]))
+        copy_all(reads, writes, arrived, left)
+
+    return moved(kernel, where, [keep, got], [shape] * chips, shape.shape[1:], 2 * chips)
+
+
+def join(half, where, blocks, shape, base, ranks):
     cells = blocks[0].shape[-1]
-    operands = blocks + ([] if base is None else [base])
+    operands = [blocks[rank] for rank in ranks] + ([] if base is None else [base])
 
     def kernel(where_ref, *refs):
-        out_ref = refs[len(operands)]
-        copy_all(
-            [
-                (
-                    refs[rank].at[side],
-                    out_ref.at[:, :, cell_span(where_ref, rank, side, half, cells)],
-                )
-                for rank in range(chips)
-                for side in range(2)
-            ],
-            refs[len(operands) + 1],
-        )
+        out_ref, stage, arrived, left = refs[len(operands) :]
+        reads, writes = [], []
+        for i, rank in enumerate(ranks):
+            for side in range(2):
+                slot = stage.at[2 * i + side]
+                reads.append((refs[i].at[side], slot))
+                for lanes, target in cell_spans(where_ref, rank, side, half, cells):
+                    writes.append((slot.at[:, :, lanes], out_ref.at[:, :, target]))
+        copy_all(reads, writes, arrived, left)
 
     aliases = None if base is None else {len(operands): 0}
     out = jax.ShapeDtypeStruct(shape, blocks[0].dtype)
-    return moved(kernel, where, operands, out, 2 * chips, aliases)
+    return moved(kernel, where, operands, out, blocks[0].shape[1:], 2 * len(ranks), aliases)
 
 
 def transform_kernel(first, chips, where_ref, *refs):
@@ -167,7 +192,7 @@
     half = SPACING // 2
     blocks = cells // LANES
     for b in range(blocks):
-        block = first * blocks + b
+        block = (first * blocks + b + half // LANES) % (HALVES * blocks)
         skip = (block * LANES + half) % SPACING
         frac = (offset + skip) / SPACING
         frac = jnp.concatenate([frac] * tiers, axis=1)
@@ -178,7 +203,7 @@
             ],
             axis=1,
         )
-        base = (block + 1) // 2 - (first * blocks + 1) // 2
+        base = (block * LANES + half) // SPACING - (first < HALVES - 1)
         under = jnp.dot(matrices_ref[base], values, preferred_element_type=jnp.float32)
         over = jnp.dot(matrices_ref[base + 1], values, preferred_element_type=jnp.float32)
         mixed = (1.0 - frac) * under + frac * over
@@ -335,19 +360,27 @@
 
     analysis = None
     for half in range(HALVES):
-        pieces = cut(half, where, prior_samples)
+        early = -(-2 * (chips - 1) // 7) if half == 0 else 0
+        pieces = []
+        if early:
+            pieces += cut(half, where, prior_samples, range(early))
+        pieces += cut(half, where, prior_samples, range(early, chips))
         pieces = [swap(block, rank) for rank, block in enumerate(pieces)]
         other = hand(where, pieces)
         other = swap_core(other)
-        if half == 0:
-            matrices = jnp.concatenate([before, weights[: COARSE // 2 + 1]])
-        else:
-            matrices = jnp.concatenate([weights[COARSE // 2 - 1 :], beyond])
+        matrices = weights
+        if half == HALVES - 1:
+            matrices = jnp.concatenate([before, weights, beyond])
         keep, give = transform(half, where, pieces, other, matrices)
         got = swap_core(give)
         blocks = pack(where, keep, got)
         blocks = [swap(block, rank) for rank, block in enumerate(blocks)]
-        analysis = join(half, where, blocks, prior_samples.shape, analysis)
+        late = [] if half == 0 else list(range(across, 2 * across))
+        rest = [rank for rank in range(chips) if rank not in late]
+        shape = prior_samples.shape
+        analysis = join(half, where, blocks, shape, analysis, rest)
+        if late:
+            analysis = join(half, where, blocks, shape, analysis, late)
     return analysis
 
 

time: 990 us -> 383 us (0.39)
  Pallas kernels: 710 us -> 63.5 us
  waiting for transfers between devices: 89 us -> 120 us
    pallas_call x8 -> x10, Pallas kernels: 682 us -> 35.4 us  [moved(): pl.pallas_call(kernel, in_specs=[pl.BlockSpec(memory_space=pltpu.SMEM)] +...]
    ppermute x28, waiting for transfers between devices: 72.2 us -> 106 us  [swap(): return lax.ppermute(block, 'region', pairs)]
    ppermute x28, starting transfers between devices: 110 us -> 137 us  [swap(): return lax.ppermute(block, 'region', pairs)]
    all_to_all x2, starting transfers between devices: 35.2 us -> 13.8 us  [spread(): lax.all_to_all(block, 'region', split_axis=0, concat_axis=0, tiled=True)]
  transfers between devices with their start and end apart: 40 -> 40, of which waited for: 9 -> 13; matrix products, arithmetic and copies ran while one was open for 2% -> 7% of each run, Pallas kernels for 62% -> 16%
where the time goes in v1:
time: 383 us; the launch traced here: 379 us
  starting transfers between devices  162 us (42%)
  waiting for transfers between devices  120 us (31%)
  Pallas kernels  63.5 us (17%)
  matrix products  14.7 us (4%)
  other arithmetic  12.9 us (3%)
    ppermute x28, starting transfers between devices, swap(): return lax.ppermute(block, 'region', pairs)  137 us
    ppermute x28, waiting for transfers between devices, swap(): return lax.ppermute(block, 'region', pairs)  106 us
    pallas_call x10, Pallas kernels, moved(): pl.pallas_call(kernel, in_specs=[pl.BlockSpec(memory_space=pltpu.SMEM)] +...  35.4 us
    pallas_call x2, Pallas kernels, transform(): pl.pallas_call(functools.partial(transform_kernel, first, chips), grid=(1...  15.1 us
    all_to_all x2, starting transfers between devices, spread(): lax.all_to_all(block, 'region', split_axis=0, concat_axis=0, tiled=True)  13.8 us
    pallas_call x1, Pallas kernels, gather_observed(): pl.pallas_call(gather_kernel, grid=(regions,), in_specs=[pl.BlockSpec((1,...  13 us
    ppermute x1, waiting for transfers between devices, analyse(): opposite = lax.ppermute(weights, 'level', flip)  9.64 us
  transfers between devices with their start and end apart: 40, of which 13 were waited for; matrix products, arithmetic and copies ran while one was open for 7% of the time, Pallas kernels for 16%

profile of v1, /device:TPU:1, one launch (start us, length us, event | category | flops | bytes accessed | tf_op | source)
XLA Modules:
  0.0 378.8 jit_solution(17872567696305222721)
XLA Ops:
  3.4 7.3 %all-to-all-start = ((f32[16,3,512]{2,1,0:T(4,128)}), f32[16,3,512]{2,1,0:T(4,128)S(1)}, u32[]{:S(2)}, u32[]{:S(2)}) async-start(f32[16,3,512]{2,1,0:T(4,128)} %broadcast_in_dim.16), calls=%async_computation | async-start | bytes 262144 | tf_op jit(solution)/shard_map/all_to_all | solution.py:277
  14.0 4.1 %collective-permute-start.22 = (bf16[2,16,8,768]{3,2,1,0:T(8,128)(2,1)}, bf16[2,16,8,768]{3,2,1,0:T(8,128)(2,1)S(1)}, u32[]{:S(2)}, u32[]{:S(2)}) collective-permute-start(bf16[2,16,8,768]{3,2,1,0:T(8,128)(2,1)} %get-tuple-element.59), channel_id=1, source_target_pairs={{0,28},{2,30},{4,24},{6,26},{8,20},{10,22},{12,16},{14,18},{16,12}... | collective-permute-start | bytes 1179656 | tf_op jit(solution)/shard_map/ppermute | solution.py:304
  19.1 13.0 %gather_observed.1 = bf16[16,16,512]{2,1,0:T(8,128)(2,1)} custom-call(s32[16,1,512]{2,1,0:T(1,128)} %get-tuple-element.94.cell_ref, s32[16,1,512]{2,1,0:T(1,128)} %get-tuple-element.93.level_ref, bf16[16,8,24576]{2,1,0:T(8,128)(2,1)} %prior_ref.5), custom_call_target="tpu_custom_call" | custom-call | tf_op jit(solution)/shard_map/gather_observed/pallas_call | solution.py:37
  34.0 3.6 shard_map.69
  42.5 4.2 %shard_map.64 = (bf16[2,16,8,768]{3,2,1,0:T(8,128)(2,1)}, bf16[2,16,8,768]{3,2,1,0:T(8,128)(2,1)}, bf16[2,16,8,768]{3,2,1,0:T(8,128)(2,1)}, bf16[2,16,8,768]{3,2...) custom-call(s32[9]{0:T(128)} %stack.66.where_ref, ...), custom_call_target="tpu_custom_call" | custom-call | tf_op jit(solution)/shard_map/pallas_call | solution.py:75
  47.5 6.5 %all-to-all-start.1 = ((bf16[16,16,512]{2,1,0:T(8,128)(2,1)}), bf16[16,16,512]{2,1,0:T(8,128)(2,1)S(1)}, u32[]{:S(2)}, u32[]{:S(2)}) async-start(bf16[16,16,512]{2,1,0:T(8,128)(2,1)} %add.192), calls=%async_computation.1 | async-start | bytes 524288 | tf_op jit(solution)/shard_map/all_to_all | solution.py:277
  55.5 21.8 %collective-permute-done.24.refs_2_ = bf16[2,16,8,768]{3,2,1,0:T(8,128)(2,1)S(1)} collective-permute-done((bf16[2,16,8,768]{3,2,1,0:T(8,128)(2,1)}, bf16[2,16,8,768]{3,2,1,0:T(8,128)(2,1)S(1)}, u32[]{:S(2)}, u32[]{:S(2)}) %collective-permute-start.24) | collective-permute-done | bytes 393248 | tf_op jit(solution)/shard_map/ppermute | solution.py:304
  80.3 16.4 %collective-permute-done.25.refs_3_ = bf16[2,16,8,768]{3,2,1,0:T(8,128)(2,1)S(1)} collective-permute-done((bf16[2,16,8,768]{3,2,1,0:T(8,128)(2,1)}, bf16[2,16,8,768]{3,2,1,0:T(8,128)(2,1)S(1)}, u32[]{:S(2)}, u32[]{:S(2)}) %collective-permute-start.25) | collective-permute-done | bytes 393248 | tf_op jit(solution)/shard_map/ppermute | solution.py:304
  104.2 33.4 %collective-permute-start.5 = (bf16[2,16,8,768]{3,2,1,0:T(8,128)(2,1)}, bf16[2,16,8,768]{3,2,1,0:T(8,128)(2,1)}, u32[]{:S(2)}, u32[]{:S(2)}) collective-permute-start(bf16[2,16,8,768]{3,2,1,0:T(8,128)(2,1)} %get-tuple-element.46), channel_id=1, source_target_pairs={{0,8},{2,10},{4,12},{6,14},{8,0},{10,2},{12,4},{14,6},{16,24},{18,... | collective-permute-start | bytes 1179656 | tf_op jit(solution)/shard_map/ppermute | solution.py:304
  138.9 14.7 %collective-permute-done.2.refs_2_ = bf16[2,16,8,768]{3,2,1,0:T(8,128)(2,1)} collective-permute-done((bf16[2,16,8,768]{3,2,1,0:T(8,128)(2,1)}, bf16[2,16,8,768]{3,2,1,0:T(8,128)(2,1)}, u32[]{:S(2)}, u32[]{:S(2)}) %collective-permute-start.2) | collective-permute-done | bytes 393248 | tf_op jit(solution)/shard_map/ppermute | solution.py:304
  155.7 5.9 %collective-permute-done.3.refs_3_ = bf16[2,16,8,768]{3,2,1,0:T(8,128)(2,1)} collective-permute-done((bf16[2,16,8,768]{3,2,1,0:T(8,128)(2,1)}, bf16[2,16,8,768]{3,2,1,0:T(8,128)(2,1)}, u32[]{:S(2)}, u32[]{:S(2)}) %collective-permute-start.3) | collective-permute-done | bytes 393248 | tf_op jit(solution)/shard_map/ppermute | solution.py:304
  165.6 3.1 shard_map.70
  168.8 3.1 shard_map.65
  191.7 9.6 %collective-permute-done.11 = bf16[3,256,256]{2,1,0:T(8,128)(2,1)S(1)} collective-permute-done((bf16[3,256,256]{2,1,0:T(8,128)(2,1)S(1)}, bf16[3,256,256]{2,1,0:T(8,128)(2,1)S(1)}, u32[]{:S(2)}, u32[]{:S(2)}) %collective-permute-start.11) | collective-permute-done | bytes 393248 | tf_op jit(solution)/shard_map/ppermute | solution.py:352
  202.4 7.5 %shard_map.71 = (bf16[8,16,8,768]{3,2,1,0:T(8,128)(2,1)}, bf16[8,16,8,768]{3,2,1,0:T(8,128)(2,1)}) custom-call(s32[9]{0:T(128)} %stack.66.where_ref, bf16[2,16,8,768]{3,2,1,0:T(8,128)(2,1)} %copy-done.1, bf16[2,16,8,768]{3,2,1,0:T(8,128)(2,1)} %copy-done.2, bf16[2,16,8,768]{3,2,1,0:T(8,128)(2,1)} %copy-done.3, bf16[2,16,8,768]{3,2,1,0:T(8,128)(2,1)} %copy-done.4, ...), custom_call_target="tpu_custom_call" | custom-call | tf_op jit(solution)/shard_map/pallas_call | solution.py:225
  210.8 3.2 collective-permute-start.12
  221.0 7.6 %shard_map.66 = (bf16[8,16,8,768]{3,2,1,0:T(8,128)(2,1)}, bf16[8,16,8,768]{3,2,1,0:T(8,128)(2,1)}) custom-call(s32[9]{0:T(128)} %stack.66.where_ref, bf16[2,16,8,768]{3,2,1,0:T(8,128)(2,1)} %copy-done.6, bf16[2,16,8,768]{3,2,1,0:T(8,128)(2,1)} %copy-done.8, bf16[2,16,8,768]{3,2,1,0:T(8,128)(2,1)} %collective-permute-done.2.refs_2_, ...), custom_call_target="tpu_custom_call" | custom-call | tf_op jit(solution)/shard_map/pallas_call | solution.py:225
  228.6 4.1 %shard_map.72 = (bf16[2,16,8,768]{3,2,1,0:T(8,128)(2,1)}, bf16[2,16,8,768]{3,2,1,0:T(8,128)(2,1)}, bf16[2,16,8,768]{3,2,1,0:T(8,128)(2,1)}, bf16[2,16,8,768]{3,2...) custom-call(s32[9]{0:T(128)} %stack.66.where_ref, ...), custom_call_target="tpu_custom_call" | custom-call | tf_op jit(solution)/shard_map/pallas_call | solution.py:75
  232.7 3.4 collective-permute-start.31
  240.7 4.1 %shard_map.67 = (bf16[2,16,8,768]{3,2,1,0:T(8,128)(2,1)}, bf16[2,16,8,768]{3,2,1,0:T(8,128)(2,1)}, bf16[2,16,8,768]{3,2,1,0:T(8,128)(2,1)}, bf16[2,16,8,768]{3,2...) custom-call(s32[9]{0:T(128)} %stack.66.where_ref, ...), custom_call_target="tpu_custom_call" | custom-call | tf_op jit(solution)/shard_map/pallas_call | solution.py:75
  246.0 40.6 %collective-permute-start.36 = (bf16[2,16,8,768]{3,2,1,0:T(8,128)(2,1)}, bf16[2,16,8,768]{3,2,1,0:T(8,128)(2,1)S(1)}, u32[]{:S(2)}, u32[]{:S(2)}) collective-permute-start(bf16[2,16,8,768]{3,2,1,0:T(8,128)(2,1)} %get-tuple-element.74), channel_id=1, source_target_pairs={{0,8},{2,10},{4,12},{6,14},{8,0},{10,2},{12,4},{14,6},{16,24},{18,... | collective-permute-start | bytes 1179656 | tf_op jit(solution)/shard_map/ppermute | solution.py:304
  286.6 16.0 %collective-permute-done.33.refs_2_ = bf16[2,16,8,768]{3,2,1,0:T(8,128)(2,1)S(1)} collective-permute-done((bf16[2,16,8,768]{3,2,1,0:T(8,128)(2,1)}, bf16[2,16,8,768]{3,2,1,0:T(8,128)(2,1)S(1)}, u32[]{:S(2)}, u32[]{:S(2)}) %collective-permute-start.33) | collective-permute-done | bytes 393248 | tf_op jit(solution)/shard_map/ppermute | solution.py:304
  302.6 3.8 %collective-permute-start.17 = (bf16[2,16,8,768]{3,2,1,0:T(8,128)(2,1)}, bf16[2,16,8,768]{3,2,1,0:T(8,128)(2,1)S(1)}, u32[]{:S(2)}, u32[]{:S(2)}) collective-permute-start(bf16[2,16,8,768]{3,2,1,0:T(8,128)(2,1)} %get-tuple-element.53), channel_id=1, source_target_pairs={{0,28},{2,30},{4,24},{6,26},{8,20},{10,22},{12,16},{14,18},{16,12}... | collective-permute-start | bytes 1179656 | tf_op jit(solution)/shard_map/ppermute | solution.py:304
  306.5 10.3 %collective-permute-done.34.refs_3_ = bf16[2,16,8,768]{3,2,1,0:T(8,128)(2,1)S(1)} collective-permute-done((bf16[2,16,8,768]{3,2,1,0:T(8,128)(2,1)}, bf16[2,16,8,768]{3,2,1,0:T(8,128)(2,1)S(1)}, u32[]{:S(2)}, u32[]{:S(2)}) %collective-permute-start.34) | collective-permute-done | bytes 393248 | tf_op jit(solution)/shard_map/ppermute | solution.py:304
  316.8 5.7 %collective-permute-start.18 = (bf16[2,16,8,768]{3,2,1,0:T(8,128)(2,1)}, bf16[2,16,8,768]{3,2,1,0:T(8,128)(2,1)S(1)}, u32[]{:S(2)}, u32[]{:S(2)}) collective-permute-start(bf16[2,16,8,768]{3,2,1,0:T(8,128)(2,1)} %get-tuple-element.54), channel_id=1, source_target_pairs={{0,24},{2,26},{4,28},{6,30},{8,16},{10,18},{12,20},{14,22},{16,8},... | collective-permute-start | bytes 1179656 | tf_op jit(solution)/shard_map/ppermute | solution.py:304
  325.1 16.7 %collective-permute-start.15 = (bf16[2,16,8,768]{3,2,1,0:T(8,128)(2,1)}, bf16[2,16,8,768]{3,2,1,0:T(8,128)(2,1)}, u32[]{:S(2)}, u32[]{:S(2)}) collective-permute-start(bf16[2,16,8,768]{3,2,1,0:T(8,128)(2,1)} %get-tuple-element.51), channel_id=1, source_target_pairs={{0,20},{2,22},{4,16},{6,18},{8,28},{10,30},{12,24},{14,26},{16,4},... | collective-permute-start | bytes 1179656 | tf_op jit(solution)/shard_map/ppermute | solution.py:304
  341.8 6.9 %collective-permute-start.16 = (bf16[2,16,8,768]{3,2,1,0:T(8,128)(2,1)}, bf16[2,16,8,768]{3,2,1,0:T(8,128)(2,1)}, u32[]{:S(2)}, u32[]{:S(2)}) collective-permute-start(bf16[2,16,8,768]{3,2,1,0:T(8,128)(2,1)} %get-tuple-element.52), channel_id=1, source_target_pairs={{0,16},{2,18},{4,20},{6,22},{8,24},{10,26},{12,28},{14,30},{16,0},... | collective-permute-start | bytes 1179656 | tf_op jit(solution)/shard_map/ppermute | solution.py:304
  348.8 4.1 %shard_map.73.refs_6_ = bf16[16,8,24576]{2,1,0:T(8,128)(2,1)} custom-call(s32[9]{0:T(128)} %stack.66.where_ref, bf16[2,16,8,768]{3,2,1,0:T(8,128)(2,1)} %copy-done.12, bf16[2,16,8,768]{3,2,1,0:T(8,128)(2,1)} %copy-done.13, bf16[2,16,8,768]{3,2,1,0:T(8,128)(2,1)} %copy-done.14, bf16[2,16,8,768]{3,2,1,0:T(8,128)(2,1)} %copy-done.15, ...), custom_call_target="tpu_custom_call" | custom-call | tf_op jit(solution)/shard_map/pallas_call | solution.py:75
  353.0 5.6 %collective-permute-done.20.refs_3_ = bf16[2,16,8,768]{3,2,1,0:T(8,128)(2,1)} collective-permute-done((bf16[2,16,8,768]{3,2,1,0:T(8,128)(2,1)}, bf16[2,16,8,768]{3,2,1,0:T(8,128)(2,1)}, u32[]{:S(2)}, u32[]{:S(2)}) %collective-permute-start.20) | collective-permute-done | bytes 393248 | tf_op jit(solution)/shard_map/ppermute | solution.py:304
  358.6 3.5 shard_map.74.refs_2_
  362.1 9.3 %collective-permute-done.15.refs_0_ = bf16[2,16,8,768]{3,2,1,0:T(8,128)(2,1)} collective-permute-done((bf16[2,16,8,768]{3,2,1,0:T(8,128)(2,1)}, bf16[2,16,8,768]{3,2,1,0:T(8,128)(2,1)}, u32[]{:S(2)}, u32[]{:S(2)}) %collective-permute-start.15) | collective-permute-done | bytes 393248 | tf_op jit(solution)/shard_map/ppermute | solution.py:304
  371.4 4.5 %collective-permute-done.16.refs_1_ = bf16[2,16,8,768]{3,2,1,0:T(8,128)(2,1)} collective-permute-done((bf16[2,16,8,768]{3,2,1,0:T(8,128)(2,1)}, bf16[2,16,8,768]{3,2,1,0:T(8,128)(2,1)}, u32[]{:S(2)}, u32[]{:S(2)}) %collective-permute-start.16) | collective-permute-done | bytes 393248 | tf_op jit(solution)/shard_map/ppermute | solution.py:304
  (158 shorter events, 72.8 us)
Async XLA Ops:
  14.0 26.3 %collective-permute-start.22 = (bf16[2,16,8,768]{3,2,1,0:T(8,128)(2,1)}, bf16[2,16,8,768]{3,2,1,0:T(8,128)(2,1)S(1)}, u32[]{:S(2)}, u32[]{:S(2)}) collective-permute-start(bf16[2,16,8,768]{3,2,1,0:T(8,128)(2,1)} %get-tuple-element.59), channel_id=1, source_target_pairs={{0,28},{2,30},{4,24},{6,26},{8,20},{10,22},{12,16},{14,18},{16,12}... | collective-permute-start | bytes 1179656 | tf_op jit(solution)/shard_map/ppermute | solution.py:304
  33.3 20.7 %collective-permute-start.23 = (bf16[2,16,8,768]{3,2,1,0:T(8,128)(2,1)}, bf16[2,16,8,768]{3,2,1,0:T(8,128)(2,1)S(1)}, u32[]{:S(2)}, u32[]{:S(2)}) collective-permute-start(bf16[2,16,8,768]{3,2,1,0:T(8,128)(2,1)} %get-tuple-element.60), channel_id=1, source_target_pairs={{0,24},{2,26},{4,28},{6,30},{8,16},{10,18},{12,20},{14,22},{16,8},... | collective-permute-start | bytes 1179656 | tf_op jit(solution)/shard_map/ppermute | solution.py:304
  37.6 39.6 %collective-permute-start.24 = (bf16[2,16,8,768]{3,2,1,0:T(8,128)(2,1)}, bf16[2,16,8,768]{3,2,1,0:T(8,128)(2,1)S(1)}, u32[]{:S(2)}, u32[]{:S(2)}) collective-permute-start(bf16[2,16,8,768]{3,2,1,0:T(8,128)(2,1)} %get-tuple-element.61), channel_id=1, source_target_pairs={{0,20},{2,22},{4,16},{6,18},{8,28},{10,30},{12,24},{14,26},{16,4},... | collective-permute-start | bytes 1179656 | tf_op jit(solution)/shard_map/ppermute | solution.py:304
  38.2 58.5 %collective-permute-start.25 = (bf16[2,16,8,768]{3,2,1,0:T(8,128)(2,1)}, bf16[2,16,8,768]{3,2,1,0:T(8,128)(2,1)S(1)}, u32[]{:S(2)}, u32[]{:S(2)}) collective-permute-start(bf16[2,16,8,768]{3,2,1,0:T(8,128)(2,1)} %get-tuple-element.62), channel_id=1, source_target_pairs={{0,16},{2,18},{4,20},{6,22},{8,24},{10,26},{12,28},{14,30},{16,0},... | collective-permute-start | bytes 1179656 | tf_op jit(solution)/shard_map/ppermute | solution.py:304
  40.4 59.4 %collective-permute-start.26 = (bf16[2,16,8,768]{3,2,1,0:T(8,128)(2,1)}, bf16[2,16,8,768]{3,2,1,0:T(8,128)(2,1)S(1)}, u32[]{:S(2)}, u32[]{:S(2)}) collective-permute-start(bf16[2,16,8,768]{3,2,1,0:T(8,128)(2,1)} %get-tuple-element.63), channel_id=1, source_target_pairs={{0,12},{2,14},{4,8},{6,10},{8,4},{10,6},{12,0},{14,2},{16,28},{18,... | collective-permute-start | bytes 1179656 | tf_op jit(solution)/shard_map/ppermute | solution.py:304
  41.6 58.2 %collective-permute-start.27 = (bf16[2,16,8,768]{3,2,1,0:T(8,128)(2,1)}, bf16[2,16,8,768]{3,2,1,0:T(8,128)(2,1)S(1)}, u32[]{:S(2)}, u32[]{:S(2)}) collective-permute-start(bf16[2,16,8,768]{3,2,1,0:T(8,128)(2,1)} %get-tuple-element.64), channel_id=1, source_target_pairs={{0,8},{2,10},{4,12},{6,14},{8,0},{10,2},{12,4},{14,6},{16,24},{18,... | collective-permute-start | bytes 1179656 | tf_op jit(solution)/shard_map/ppermute | solution.py:304
  47.5 106.1 %all-to-all-start.1 = ((bf16[16,16,512]{2,1,0:T(8,128)(2,1)}), bf16[16,16,512]{2,1,0:T(8,128)(2,1)S(1)}, u32[]{:S(2)}, u32[]{:S(2)}) async-start(bf16[16,16,512]{2,1,0:T(8,128)(2,1)} %add.192), calls=%async_computation.1 | async-start | bytes 524288 | tf_op jit(solution)/shard_map/all_to_all | solution.py:277
  54.1 50.0 %collective-permute-start.28 = (bf16[2,16,8,768]{3,2,1,0:T(8,128)(2,1)}, bf16[2,16,8,768]{3,2,1,0:T(8,128)(2,1)}, u32[]{:S(2)}, u32[]{:S(2)}) collective-permute-start(bf16[2,16,8,768]{3,2,1,0:T(8,128)(2,1)} %get-tuple-element.65), channel_id=1, source_target_pairs={{0,4},{2,6},{4,0},{6,2},{8,12},{10,14},{12,8},{14,10},{16,20},{18,... | collective-permute-start | bytes 1179656 | tf_op jit(solution)/shard_map/ppermute | solution.py:304
  77.2 26.9 %collective-permute-start = (bf16[2,16,8,768]{3,2,1,0:T(8,128)(2,1)}, bf16[2,16,8,768]{3,2,1,0:T(8,128)(2,1)S(1)}, u32[]{:S(2)}, u32[]{:S(2)}) collective-permute-start(bf16[2,16,8,768]{3,2,1,0:T(8,128)(2,1)} %get-tuple-element.41), channel_id=1, source_target_pairs={{0,28},{2,30},{4,24},{6,26},{8,20},{10,22},{12,16},{14,18},{16,12}... | collective-permute-start | bytes 1179656 | tf_op jit(solution)/shard_map/ppermute | solution.py:304
  96.7 40.9 %collective-permute-start.1 = (bf16[2,16,8,768]{3,2,1,0:T(8,128)(2,1)}, bf16[2,16,8,768]{3,2,1,0:T(8,128)(2,1)S(1)}, u32[]{:S(2)}, u32[]{:S(2)}) collective-permute-start(bf16[2,16,8,768]{3,2,1,0:T(8,128)(2,1)} %get-tuple-element.42), channel_id=1, source_target_pairs={{0,24},{2,26},{4,28},{6,30},{8,16},{10,18},{12,20},{14,22},{16,8},... | collective-permute-start | bytes 1179656 | tf_op jit(solution)/shard_map/ppermute | solution.py:304
  99.8 53.8 %collective-permute-start.2 = (bf16[2,16,8,768]{3,2,1,0:T(8,128)(2,1)}, bf16[2,16,8,768]{3,2,1,0:T(8,128)(2,1)}, u32[]{:S(2)}, u32[]{:S(2)}) collective-permute-start(bf16[2,16,8,768]{3,2,1,0:T(8,128)(2,1)} %get-tuple-element.43), channel_id=1, source_target_pairs={{0,20},{2,22},{4,16},{6,18},{8,28},{10,30},{12,24},{14,26},{16,4},... | collective-permute-start | bytes 1179656 | tf_op jit(solution)/shard_map/ppermute | solution.py:304
  99.8 61.8 %collective-permute-start.3 = (bf16[2,16,8,768]{3,2,1,0:T(8,128)(2,1)}, bf16[2,16,8,768]{3,2,1,0:T(8,128)(2,1)}, u32[]{:S(2)}, u32[]{:S(2)}) collective-permute-start(bf16[2,16,8,768]{3,2,1,0:T(8,128)(2,1)} %get-tuple-element.44), channel_id=1, source_target_pairs={{0,16},{2,18},{4,20},{6,22},{8,24},{10,26},{12,28},{14,30},{16,0},... | collective-permute-start | bytes 1179656 | tf_op jit(solution)/shard_map/ppermute | solution.py:304
  104.1 64.6 %collective-permute-start.4 = (bf16[2,16,8,768]{3,2,1,0:T(8,128)(2,1)}, bf16[2,16,8,768]{3,2,1,0:T(8,128)(2,1)}, u32[]{:S(2)}, u32[]{:S(2)}) collective-permute-start(bf16[2,16,8,768]{3,2,1,0:T(8,128)(2,1)} %get-tuple-element.45), channel_id=1, source_target_pairs={{0,12},{2,14},{4,8},{6,10},{8,4},{10,6},{12,0},{14,2},{16,28},{18,... | collective-permute-start | bytes 1179656 | tf_op jit(solution)/shard_map/ppermute | solution.py:304
  104.2 64.6 %collective-permute-start.5 = (bf16[2,16,8,768]{3,2,1,0:T(8,128)(2,1)}, bf16[2,16,8,768]{3,2,1,0:T(8,128)(2,1)}, u32[]{:S(2)}, u32[]{:S(2)}) collective-permute-start(bf16[2,16,8,768]{3,2,1,0:T(8,128)(2,1)} %get-tuple-element.46), channel_id=1, source_target_pairs={{0,8},{2,10},{4,12},{6,14},{8,0},{10,2},{12,4},{14,6},{16,24},{18,... | collective-permute-start | bytes 1179656 | tf_op jit(solution)/shard_map/ppermute | solution.py:304
  137.6 31.2 %collective-permute-start.6 = (bf16[2,16,8,768]{3,2,1,0:T(8,128)(2,1)}, bf16[2,16,8,768]{3,2,1,0:T(8,128)(2,1)}, u32[]{:S(2)}, u32[]{:S(2)}) collective-permute-start(bf16[2,16,8,768]{3,2,1,0:T(8,128)(2,1)} %get-tuple-element.47), channel_id=1, source_target_pairs={{0,4},{2,6},{4,0},{6,2},{8,12},{10,14},{12,8},{14,10},{16,20},{18,... | collective-permute-start | bytes 1179656 | tf_op jit(solution)/shard_map/ppermute | solution.py:304
  153.6 19.0 %collective-permute-start.10 = (bf16[256,512]{1,0:T(8,128)(2,1)S(1)}, bf16[256,512]{1,0:T(8,128)(2,1)S(1)}, u32[]{:S(2)}, u32[]{:S(2)}) collective-permute-start(bf16[256,512]{1,0:T(8,128)(2,1)S(1)} %bitcast.95), channel_id=1, source_target_pairs={{2,0},{4,2},{6,4},{8,6},{10,8},{12,10},{14,12},{16,14},{18,16},{20... | collective-permute-start | bytes 786440 | tf_op jit(solution)/shard_map/ppermute | solution.py:333
  168.7 33.7 %collective-permute-start.29 = (bf16[8,16,8,768]{3,2,1,0:T(8,128)(2,1)}, bf16[8,16,8,768]{3,2,1,0:T(8,128)(2,1)}, u32[]{:S(2)}, u32[]{:S(2)}) collective-permute-start(bf16[8,16,8,768]{3,2,1,0:T(8,128)(2,1)} %shard_map.70), channel_id=1, source_target_pairs={{0,2},{2,0},{4,6},{6,4},{8,10},{10,8},{12,14},{14,12},{16,18},{18,... | collective-permute-start | bytes 4718600 | tf_op jit(solution)/shard_map/ppermute | solution.py:307
  171.9 47.9 %collective-permute-start.7 = (bf16[8,16,8,768]{3,2,1,0:T(8,128)(2,1)}, bf16[8,16,8,768]{3,2,1,0:T(8,128)(2,1)S(1)}, u32[]{:S(2)}, u32[]{:S(2)}) collective-permute-start(bf16[8,16,8,768]{3,2,1,0:T(8,128)(2,1)} %shard_map.65), channel_id=1, source_target_pairs={{0,2},{2,0},{4,6},{6,4},{8,10},{10,8},{12,14},{14,12},{16,18},{18,... | collective-permute-start | bytes 4718600 | tf_op jit(solution)/shard_map/ppermute | solution.py:307
  209.9 18.7 %collective-permute-start.30 = (bf16[8,16,8,768]{3,2,1,0:T(8,128)(2,1)}, bf16[8,16,8,768]{3,2,1,0:T(8,128)(2,1)}, u32[]{:S(2)}, u32[]{:S(2)}) collective-permute-start(bf16[8,16,8,768]{3,2,1,0:T(8,128)(2,1)} %get-tuple-element.68), channel_id=1, source_target_pairs={{0,2},{2,0},{4,6},{6,4},{8,10},{10,8},{12,14},{14,12},{16,18},{18,... | collective-permute-start | bytes 4718600 | tf_op jit(solution)/shard_map/ppermute | solution.py:307
  236.1 50.5 %collective-permute-start.32 = (bf16[2,16,8,768]{3,2,1,0:T(8,128)(2,1)}, bf16[2,16,8,768]{3,2,1,0:T(8,128)(2,1)S(1)}, u32[]{:S(2)}, u32[]{:S(2)}) collective-permute-start(bf16[2,16,8,768]{3,2,1,0:T(8,128)(2,1)} %get-tuple-element.70), channel_id=1, source_target_pairs={{0,24},{2,26},{4,28},{6,30},{8,16},{10,18},{12,20},{14,22},{16,8},... | collective-permute-start | bytes 1179656 | tf_op jit(solution)/shard_map/ppermute | solution.py:304
  236.9 65.7 %collective-permute-start.33 = (bf16[2,16,8,768]{3,2,1,0:T(8,128)(2,1)}, bf16[2,16,8,768]{3,2,1,0:T(8,128)(2,1)S(1)}, u32[]{:S(2)}, u32[]{:S(2)}) collective-permute-start(bf16[2,16,8,768]{3,2,1,0:T(8,128)(2,1)} %get-tuple-element.71), channel_id=1, source_target_pairs={{0,20},{2,22},{4,16},{6,18},{8,28},{10,30},{12,24},{14,26},{16,4},... | collective-permute-start | bytes 1179656 | tf_op jit(solution)/shard_map/ppermute | solution.py:304
  238.1 78.7 %collective-permute-start.34 = (bf16[2,16,8,768]{3,2,1,0:T(8,128)(2,1)}, bf16[2,16,8,768]{3,2,1,0:T(8,128)(2,1)S(1)}, u32[]{:S(2)}, u32[]{:S(2)}) collective-permute-start(bf16[2,16,8,768]{3,2,1,0:T(8,128)(2,1)} %get-tuple-element.72), channel_id=1, source_target_pairs={{0,16},{2,18},{4,20},{6,22},{8,24},{10,26},{12,28},{14,30},{16,0},... | collective-permute-start | bytes 1179656 | tf_op jit(solution)/shard_map/ppermute | solution.py:304
  239.3 83.1 %collective-permute-start.35 = (bf16[2,16,8,768]{3,2,1,0:T(8,128)(2,1)}, bf16[2,16,8,768]{3,2,1,0:T(8,128)(2,1)S(1)}, u32[]{:S(2)}, u32[]{:S(2)}) collective-permute-start(bf16[2,16,8,768]{3,2,1,0:T(8,128)(2,1)} %get-tuple-element.73), channel_id=1, source_target_pairs={{0,12},{2,14},{4,8},{6,10},{8,4},{10,6},{12,0},{14,2},{16,28},{18,... | collective-permute-start | bytes 1179656 | tf_op jit(solution)/shard_map/ppermute | solution.py:304
  246.0 76.5 %collective-permute-start.36 = (bf16[2,16,8,768]{3,2,1,0:T(8,128)(2,1)}, bf16[2,16,8,768]{3,2,1,0:T(8,128)(2,1)S(1)}, u32[]{:S(2)}, u32[]{:S(2)}) collective-permute-start(bf16[2,16,8,768]{3,2,1,0:T(8,128)(2,1)} %get-tuple-element.74), channel_id=1, source_target_pairs={{0,8},{2,10},{4,12},{6,14},{8,0},{10,2},{12,4},{14,6},{16,24},{18,... | collective-permute-start | bytes 1179656 | tf_op jit(solution)/shard_map/ppermute | solution.py:304
  286.6 36.0 %collective-permute-start.37 = (bf16[2,16,8,768]{3,2,1,0:T(8,128)(2,1)}, bf16[2,16,8,768]{3,2,1,0:T(8,128)(2,1)S(1)}, u32[]{:S(2)}, u32[]{:S(2)}) collective-permute-start(bf16[2,16,8,768]{3,2,1,0:T(8,128)(2,1)} %get-tuple-element.75), channel_id=1, source_target_pairs={{0,4},{2,6},{4,0},{6,2},{8,12},{10,14},{12,8},{14,10},{16,20},{18,... | collective-permute-start | bytes 1179656 | tf_op jit(solution)/shard_map/ppermute | solution.py:304
  302.6 22.5 %collective-permute-start.17 = (bf16[2,16,8,768]{3,2,1,0:T(8,128)(2,1)}, bf16[2,16,8,768]{3,2,1,0:T(8,128)(2,1)S(1)}, u32[]{:S(2)}, u32[]{:S(2)}) collective-permute-start(bf16[2,16,8,768]{3,2,1,0:T(8,128)(2,1)} %get-tuple-element.53), channel_id=1, source_target_pairs={{0,28},{2,30},{4,24},{6,26},{8,20},{10,22},{12,16},{14,18},{16,12}... | collective-permute-start | bytes 1179656 | tf_op jit(solution)/shard_map/ppermute | solution.py:304
  316.8 25.0 %collective-permute-start.18 = (bf16[2,16,8,768]{3,2,1,0:T(8,128)(2,1)}, bf16[2,16,8,768]{3,2,1,0:T(8,128)(2,1)S(1)}, u32[]{:S(2)}, u32[]{:S(2)}) collective-permute-start(bf16[2,16,8,768]{3,2,1,0:T(8,128)(2,1)} %get-tuple-element.54), channel_id=1, source_target_pairs={{0,24},{2,26},{4,28},{6,30},{8,16},{10,18},{12,20},{14,22},{16,8},... | collective-permute-start | bytes 1179656 | tf_op jit(solution)/shard_map/ppermute | solution.py:304
  322.4 30.5 %collective-permute-start.19 = (bf16[2,16,8,768]{3,2,1,0:T(8,128)(2,1)}, bf16[2,16,8,768]{3,2,1,0:T(8,128)(2,1)}, u32[]{:S(2)}, u32[]{:S(2)}) collective-permute-start(bf16[2,16,8,768]{3,2,1,0:T(8,128)(2,1)} %get-tuple-element.55), channel_id=1, source_target_pairs={{0,12},{2,14},{4,8},{6,10},{8,4},{10,6},{12,0},{14,2},{16,28},{18,... | collective-permute-start | bytes 1179656 | tf_op jit(solution)/shard_map/ppermute | solution.py:304
  322.5 36.1 %collective-permute-start.20 = (bf16[2,16,8,768]{3,2,1,0:T(8,128)(2,1)}, bf16[2,16,8,768]{3,2,1,0:T(8,128)(2,1)}, u32[]{:S(2)}, u32[]{:S(2)}) collective-permute-start(bf16[2,16,8,768]{3,2,1,0:T(8,128)(2,1)} %get-tuple-element.56), channel_id=1, source_target_pairs={{0,8},{2,10},{4,12},{6,14},{8,0},{10,2},{12,4},{14,6},{16,24},{18,... | collective-permute-start | bytes 1179656 | tf_op jit(solution)/shard_map/ppermute | solution.py:304
  322.6 36.0 %collective-permute-start.21 = (bf16[2,16,8,768]{3,2,1,0:T(8,128)(2,1)}, bf16[2,16,8,768]{3,2,1,0:T(8,128)(2,1)}, u32[]{:S(2)}, u32[]{:S(2)}) collective-permute-start(bf16[2,16,8,768]{3,2,1,0:T(8,128)(2,1)} %get-tuple-element.57), channel_id=1, source_target_pairs={{0,4},{2,6},{4,0},{6,2},{8,12},{10,14},{12,8},{14,10},{16,20},{18,... | collective-permute-start | bytes 1179656 | tf_op jit(solution)/shard_map/ppermute | solution.py:304
  325.1 46.3 %collective-permute-start.15 = (bf16[2,16,8,768]{3,2,1,0:T(8,128)(2,1)}, bf16[2,16,8,768]{3,2,1,0:T(8,128)(2,1)}, u32[]{:S(2)}, u32[]{:S(2)}) collective-permute-start(bf16[2,16,8,768]{3,2,1,0:T(8,128)(2,1)} %get-tuple-element.51), channel_id=1, source_target_pairs={{0,20},{2,22},{4,16},{6,18},{8,28},{10,30},{12,24},{14,26},{16,4},... | collective-permute-start | bytes 1179656 | tf_op jit(solution)/shard_map/ppermute | solution.py:304
  341.8 34.1 %collective-permute-start.16 = (bf16[2,16,8,768]{3,2,1,0:T(8,128)(2,1)}, bf16[2,16,8,768]{3,2,1,0:T(8,128)(2,1)}, u32[]{:S(2)}, u32[]{:S(2)}) collective-permute-start(bf16[2,16,8,768]{3,2,1,0:T(8,128)(2,1)} %get-tuple-element.52), channel_id=1, source_target_pairs={{0,16},{2,18},{4,20},{6,22},{8,24},{10,26},{12,28},{14,30},{16,0},... | collective-permute-start | bytes 1179656 | tf_op jit(solution)/shard_map/ppermute | solution.py:304
  (33 other events, 1091.8 us)

commit v2 on v1

--- a/solution.py
+++ b/solution.py
@@ -15,6 +15,26 @@
 LANES = 128
 
 inflation = 1.1
+
+
+def moves(regions):
+    across = regions // 8
+    steps = [(dz, dx) for dz in (3, 2, 1, 0) for dx in reversed(range(across))]
+    turns = zip(steps[: 2 * across], steps[2 * across :])
+    return [step for turn in turns for step in turn]
+
+
+def target(chip, step, across):
+    dz, dx = step
+    return ((chip // across) ^ dz) * across + ((chip % across) ^ dx)
+
+
+def standing(regions):
+    across = regions // 8
+    me = lax.axis_index("region")
+    core = lax.rem(me, 2)
+    row, column = lax.div(me, 2 * across), lax.rem(lax.div(me, 2), across)
+    return core, [(row ^ dz) * across + (column ^ dx) for dz, dx in moves(regions)]
 
 
 def gather_kernel(cell_ref, level_ref, fields_ref, out_ref):
@@ -69,12 +89,12 @@
         copy.wait()
 
 
-def moved(kernel, where, operands, out_shape, block, count, aliases=None):
+def moved(kernel, operands, out_shape, block, count, aliases=None):
     anywhere = pl.BlockSpec(memory_space=pl.ANY)
     several = isinstance(out_shape, list)
     return pl.pallas_call(
         kernel,
-        in_specs=[pl.BlockSpec(memory_space=pltpu.SMEM)] + [anywhere] * len(operands),
+        in_specs=[anywhere] * len(operands),
         out_specs=[anywhere] * len(out_shape) if several else anywhere,
         out_shape=out_shape,
         scratch_shapes=[
@@ -83,7 +103,7 @@
             pltpu.SemaphoreType.DMA((2 * count,)),
         ],
         input_output_aliases=aliases or {},
-    )(where, *operands)
+    )(*operands)
 
 
 def spans(half, cells):
@@ -93,40 +113,38 @@
     return [(0, half * cells + shift, cells - shift), (cells - shift, 0, shift)]
 
 
-def cell_spans(where_ref, rank, side, half, cells):
-    chips = where_ref.shape[0] - 1
-    core = where_ref[chips]
-    region = where_ref[rank] * 2 + (core if side == 0 else 1 - core)
+def cell_spans(chip, core, half, cells):
+    region = chip * 2 + core
     for lane, cell, count in spans(half, cells):
         first = pl.multiple_of(region * (HALVES * cells) + cell, LANES)
         yield pl.ds(lane, count), pl.ds(first, count)
 
 
-def cut(half, where, prior, ranks):
-    chips = where.shape[0] - 1
+def cut(half, prior, ranks, regions):
     members, tiers, total = prior.shape
-    cells = total // (2 * chips * HALVES)
+    cells = total // (regions * HALVES)
     shape = jax.ShapeDtypeStruct((2, members, tiers, cells), prior.dtype)
 
-    def kernel(where_ref, prior_ref, *refs):
+    def kernel(prior_ref, *refs):
+        core, partners = standing(regions)
         reads, writes = [], []
         stage, arrived, left = refs[len(ranks) :]
         for i, rank in enumerate(ranks):
             for side in range(2):
                 slot = stage.at[2 * i + side]
-                for lanes, source in cell_spans(where_ref, rank, side, half, cells):
+                for lanes, source in cell_spans(partners[rank], core ^ side, half, cells):
                     reads.append((prior_ref.at[:, :, source], slot.at[:, :, lanes]))
                 writes.append((slot, refs[i].at[side]))
         copy_all(reads, writes, arrived, left)
 
-    return moved(kernel, where, [prior], [shape] * len(ranks), shape.shape[1:], 2 * len(ranks))
-
-
-def hand(where, pieces):
+    return moved(kernel, [prior], [shape] * len(ranks), shape.shape[1:], 2 * len(ranks))
+
+
+def hand(pieces):
     chips = len(pieces)
     shape = jax.ShapeDtypeStruct((chips,) + pieces[0].shape[1:], pieces[0].dtype)
 
-    def kernel(where_ref, *refs):
+    def kernel(*refs):
         out_ref, stage, arrived, left = refs[chips:]
         copy_all(
             [(refs[p].at[1], stage.at[p]) for p in range(chips)],
@@ -135,14 +153,14 @@
             left,
         )
 
-    return moved(kernel, where, pieces, shape, shape.shape[1:], chips)
-
-
-def pack(where, keep, got):
+    return moved(kernel, pieces, shape, shape.shape[1:], chips)
+
+
+def pack(keep, got):
     chips = keep.shape[0]
     shape = jax.ShapeDtypeStruct((2,) + keep.shape[1:], keep.dtype)
 
-    def kernel(where_ref, keep_ref, got_ref, *refs):
+    def kernel(keep_ref, got_ref, *refs):
         stage, arrived, left = refs[chips:]
         reads, writes = [], []
         for p in range(chips):
@@ -152,39 +170,48 @@
                 writes.append((slot, refs[p].at[side]))
         copy_all(reads, writes, arrived, left)
 
-    return moved(kernel, where, [keep, got], [shape] * chips, shape.shape[1:], 2 * chips)
-
-
-def join(half, where, blocks, shape, base, ranks):
+    return moved(kernel, [keep, got], [shape] * chips, shape.shape[1:], 2 * chips)
+
+
+def join(half, blocks, shape, base, ranks, regions):
     cells = blocks[0].shape[-1]
     operands = [blocks[rank] for rank in ranks] + ([] if base is None else [base])
 
-    def kernel(where_ref, *refs):
+    def kernel(*refs):
+        core, partners = standing(regions)
         out_ref, stage, arrived, left = refs[len(operands) :]
         reads, writes = [], []
         for i, rank in enumerate(ranks):
             for side in range(2):
                 slot = stage.at[2 * i + side]
                 reads.append((refs[i].at[side], slot))
-                for lanes, target in cell_spans(where_ref, rank, side, half, cells):
+                for lanes, target in cell_spans(partners[rank], core ^ side, half, cells):
                     writes.append((slot.at[:, :, lanes], out_ref.at[:, :, target]))
         copy_all(reads, writes, arrived, left)
 
-    aliases = None if base is None else {len(operands): 0}
+    aliases = None if base is None else {len(operands) - 1: 0}
     out = jax.ShapeDtypeStruct(shape, blocks[0].dtype)
-    return moved(kernel, where, operands, out, blocks[0].shape[1:], 2 * len(ranks), aliases)
-
-
-def transform_kernel(first, chips, where_ref, *refs):
+    return moved(kernel, operands, out, blocks[0].shape[1:], 2 * len(ranks), aliases)
+
+
+def transform_kernel(first, chips, *refs):
     pieces = refs[:chips]
-    other_ref, matrices_ref, keep_ref, give_ref, work = refs[chips:]
+    other_ref, own_ref, opposite_ref, *edges = refs[chips:-4]
+    keep_ref, give_ref, work, matrices = refs[-4:]
+    core, partners = standing(2 * chips)
+    share = own_ref.shape[0]
+    rank = lax.axis_index("level")
+    for k in range(share):
+        matrices[1 + rank * share + k] = own_ref[k]
+        matrices[1 + (1 - rank) * share + k] = opposite_ref[k]
+    for k, edge in zip((0, 2 * share + 1), edges):
+        matrices[k] = edge[0]
     _, members, tiers, cells = other_ref.shape
     total = chips * 2 * members
     rows = members * tiers
-    core = where_ref[chips]
     for p in range(chips):
         for side, piece in ((core, pieces[p][0]), (1 - core, other_ref[p])):
-            start = pl.multiple_of((where_ref[p] * 2 + side) * rows, 8)
+            start = pl.multiple_of((partners[p] * 2 + side) * rows, 8)
             piece = piece.astype(jnp.float32).reshape(rows, cells)
             for b in range(cells // LANES):
                 work[b, pl.ds(start, rows), :] = piece[:, b * LANES : (b + 1) * LANES]
@@ -203,33 +230,36 @@
             ],
             axis=1,
         )
-        base = (block * LANES + half) // SPACING - (first < HALVES - 1)
-        under = jnp.dot(matrices_ref[base], values, preferred_element_type=jnp.float32)
-        over = jnp.dot(matrices_ref[base + 1], values, preferred_element_type=jnp.float32)
+        base = (block * LANES + half) // SPACING
+        under = jnp.dot(matrices[base], values, preferred_element_type=jnp.float32)
+        over = jnp.dot(matrices[base + 1], values, preferred_element_type=jnp.float32)
         mixed = (1.0 - frac) * under + frac * over
         for t in range(tiers):
             work[b, pl.ds(t, total, stride=tiers), :] = mixed[:, t * LANES : (t + 1) * LANES]
     for p in range(chips):
         for side, out_ref in ((core, keep_ref), (1 - core, give_ref)):
-            start = pl.multiple_of((where_ref[p] * 2 + side) * rows, 8)
+            start = pl.multiple_of((partners[p] * 2 + side) * rows, 8)
             for b in range(blocks):
                 block = work[b, pl.ds(start, rows), :].reshape(members, tiers, LANES)
                 out_ref[p, :, :, b * LANES : (b + 1) * LANES] = block.astype(jnp.bfloat16)
 
 
-def transform(first, where, pieces, other, matrices):
+def transform(first, pieces, other, own, opposite, edges):
     chips, members, tiers, cells = other.shape
     out = jax.ShapeDtypeStruct(other.shape, jnp.bfloat16)
     whole = pl.BlockSpec(memory_space=pltpu.VMEM)
-    own = pl.BlockSpec((1, members, tiers, cells), lambda i: (i, 0, 0, 0))
+    mine = pl.BlockSpec((1, members, tiers, cells), lambda i: (i, 0, 0, 0))
     return pl.pallas_call(
         functools.partial(transform_kernel, first, chips),
         grid=(1,),
-        in_specs=[pl.BlockSpec(memory_space=pltpu.SMEM)] + [own] * chips + [whole] * 2,
+        in_specs=[mine] * chips + [whole] * (3 + len(edges)),
         out_specs=[whole, whole],
         out_shape=[out, out],
-        scratch_shapes=[pltpu.VMEM((cells // LANES, chips * 2 * members * tiers, LANES), jnp.float32)],
-    )(where, *pieces, other, matrices)
+        scratch_shapes=[
+            pltpu.VMEM((cells // LANES, chips * 2 * members * tiers, LANES), jnp.float32),
+            pltpu.VMEM((2 * own.shape[0] + 2,) + own.shape[1:], own.dtype),
+        ],
+    )(*pieces, other, own, opposite, *edges)
 
 
 def local_products(window, records, radius_cells, coarse):
@@ -253,7 +283,7 @@
     frobenius = jnp.sqrt(jnp.sum(shifted * shifted, axis=(1, 2)))
     iterate = shifted / frobenius[:, None, None]
     inverse = 1.5 * identity[None] - 0.5 * iterate
-    high = lax.Precision.HIGHEST
+    high = lax.Precision.HIGH
     iterate = jnp.matmul(iterate, inverse, precision=high)
     for turn in range(1, NS_ITERS):
         factor = 1.5 * identity[None] - 0.5 * jnp.matmul(inverse, iterate, precision=high)
@@ -268,11 +298,6 @@
     return jnp.swapaxes(weights, 1, 2).astype(jnp.bfloat16)
 
 
-def moves(regions):
-    across = regions // 8
-    return [(dz, dx) for dz in (3, 2, 1, 0) for dx in reversed(range(across))]
-
-
 def spread(block):
     return lax.all_to_all(block, "region", split_axis=0, concat_axis=0, tiled=True)
 
@@ -289,25 +314,16 @@
     tier_rank = lax.axis_index("level")
     chips = regions // 2
     across = chips // 4
-    core = me % 2
-    chip = me // 2
     steps = moves(regions)
 
-    def target(chip_index, dz, dx):
-        return ((chip_index // across) ^ dz) * across + ((chip_index % across) ^ dx)
-
     def swap(block, rank):
-        dz, dx = steps[rank]
-        if (dz, dx) == (0, 0):
+        if steps[rank] == (0, 0):
             return block
-        pairs = [(i, target(i // 2, dz, dx) * 2 + i % 2) for i in range(regions)]
+        pairs = [(i, target(i // 2, steps[rank], across) * 2 + i % 2) for i in range(regions)]
         return lax.ppermute(block, "region", pairs)
 
     def swap_core(block):
         return lax.ppermute(block, "region", [(i, i ^ 1) for i in range(regions)])
-
-    partners = [target(chip, dz, dx) for dz, dx in steps]
-    where = jnp.stack(partners + [core]).astype(jnp.int32)
 
     live = jnp.arange(slots, dtype=jnp.int32) < active_slots[0]
     live_f = live.astype(jnp.float32)
@@ -350,37 +366,31 @@
     )
     weights = ensemble_weights(gram_matrix, right_side)
     opposite = lax.ppermute(weights, "level", flip)
-    weights = jnp.where(
-        tier_rank == 0,
-        jnp.concatenate([weights, opposite]),
-        jnp.concatenate([opposite, weights]),
-    )
-    before = lax.ppermute(weights[-1:], "region", up)
-    beyond = lax.ppermute(weights[:1], "region", down)
+    before = lax.ppermute(jnp.where(tier_rank == 0, opposite, weights)[-1:], "region", up)
+    beyond = lax.ppermute(jnp.where(tier_rank == 0, weights, opposite)[:1], "region", down)
 
     analysis = None
+    early_count = -(-2 * (chips - 1) // 7)
     for half in range(HALVES):
-        early = -(-2 * (chips - 1) // 7) if half == 0 else 0
+        early = -(-(chips - 1) // 7) if half == 0 else 0
         pieces = []
         if early:
-            pieces += cut(half, where, prior_samples, range(early))
-        pieces += cut(half, where, prior_samples, range(early, chips))
+            pieces += cut(half, prior_samples, range(early), regions)
+        pieces += cut(half, prior_samples, range(early, chips), regions)
         pieces = [swap(block, rank) for rank, block in enumerate(pieces)]
-        other = hand(where, pieces)
+        other = hand(pieces)
         other = swap_core(other)
-        matrices = weights
-        if half == HALVES - 1:
-            matrices = jnp.concatenate([before, weights, beyond])
-        keep, give = transform(half, where, pieces, other, matrices)
+        edges = [] if half == 0 else [before, beyond]
+        keep, give = transform(half, pieces, other, weights, opposite, edges)
         got = swap_core(give)
-        blocks = pack(where, keep, got)
+        blocks = pack(keep, got)
         blocks = [swap(block, rank) for rank, block in enumerate(blocks)]
-        late = [] if half == 0 else list(range(across, 2 * across))
+        late = [] if half == 0 else list(range(chips - 1 - early_count, chips - 1))
         rest = [rank for rank in range(chips) if rank not in late]
         shape = prior_samples.shape
-        analysis = join(half, where, blocks, shape, analysis, rest)
+        analysis = join(half, blocks, shape, analysis, rest, regions)
         if late:
-            analysis = join(half, where, blocks, shape, analysis, late)
+            analysis = join(half, blocks, shape, analysis, late, regions)
     return analysis
 
 

time: 383 us -> 371 us (0.969)
  starting transfers between devices: 162 us -> 114 us
  waiting for transfers between devices: 120 us -> 158 us
  local copies, waits for them, and re-layouts: 3.43 us -> 13.5 us
  Pallas kernels: 63.5 us -> 56.7 us
  matrix products: 14.7 us -> 9.11 us
    ppermute x28, starting transfers between devices: 137 us -> 76.2 us  [swap(): return lax.ppermute(block, 'region', pairs)]
    ppermute x28, waiting for transfers between devices: 106 us -> 144 us  [swap(): return lax.ppermute(block, 'region', pairs)]
    ppermute x4, starting transfers between devices: 1.63 us -> 12.3 us  [swap_core(): return lax.ppermute(block, 'region', [(i, i ^ 1) for i in range(regions)])]
    unnamed x50 -> x72, local copies, waits for them, and re-layouts: 1.24 us -> 11.1 us
    pallas_call x10, Pallas kernels: 35.4 us -> 28.5 us  [moved(): pl.pallas_call(kernel, in_specs=[anywhere] * len(operands), out_specs=[an...]
  transfers between devices with their start and end apart: 40 -> 40, of which waited for: 13 -> 16; matrix products, arithmetic and copies ran while one was open for 7% -> 6% of each run, Pallas kernels for 16% -> 15%
where the time goes in v2:
time: 371 us; the launch traced here: 368 us
  waiting for transfers between devices  158 us (43%)
  starting transfers between devices  114 us (31%)
  Pallas kernels  56.7 us (15%)
  other arithmetic  14.1 us (4%)
  local copies, waits for them, and re-layouts  13.5 us (4%)
  matrix products  9.11 us (2%)
    ppermute x28, waiting for transfers between devices, swap(): return lax.ppermute(block, 'region', pairs)  144 us
    ppermute x28, starting transfers between devices, swap(): return lax.ppermute(block, 'region', pairs)  76.2 us
    pallas_call x10, Pallas kernels, moved(): pl.pallas_call(kernel, in_specs=[anywhere] * len(operands), out_specs=[an...  28.5 us
    pallas_call x2, Pallas kernels, transform(): pl.pallas_call(functools.partial(transform_kernel, first, chips), grid=(1...  15.2 us
    all_to_all x2, starting transfers between devices, spread(): lax.all_to_all(block, 'region', split_axis=0, concat_axis=0, tiled=True)  13.3 us
    pallas_call x1, Pallas kernels, gather_observed(): pl.pallas_call(gather_kernel, grid=(regions,), in_specs=[pl.BlockSpec((1,...  13 us
    ppermute x4, starting transfers between devices, swap_core(): return lax.ppermute(block, 'region', [(i, i ^ 1) for i in range(regions)])  12.3 us
    unnamed x72, local copies, waits for them, and re-layouts  11.1 us
  transfers between devices with their start and end apart: 40, of which 16 were waited for; matrix products, arithmetic and copies ran while one was open for 6% of the time, Pallas kernels for 15%

profile of v2, /device:TPU:1, one launch (start us, length us, event | category | flops | bytes accessed | tf_op | source)
XLA Modules:
  0.0 367.7 jit_solution(15543844830393709230)
XLA Ops:
  3.4 7.3 %all-to-all-start = ((f32[16,3,512]{2,1,0:T(4,128)}), f32[16,3,512]{2,1,0:T(4,128)S(1)}, u32[]{:S(2)}, u32[]{:S(2)}) async-start(f32[16,3,512]{2,1,0:T(4,128)} %broadcast_in_dim.16), calls=%async_computation | async-start | bytes 262144 | tf_op jit(solution)/shard_map/all_to_all | solution.py:302
  12.5 4.1 %collective-permute-start.22 = (bf16[2,16,8,768]{3,2,1,0:T(8,128)(2,1)}, bf16[2,16,8,768]{3,2,1,0:T(8,128)(2,1)S(1)}, u32[]{:S(2)}, u32[]{:S(2)}) collective-permute-start(bf16[2,16,8,768]{3,2,1,0:T(8,128)(2,1)} %shard_map.68), channel_id=1, source_target_pairs={{0,28},{2,30},{4,24},{6,26},{8,20},{10,22},{12,16},{14,18},{16,12}... | collective-permute-start | bytes 1179656 | tf_op jit(solution)/shard_map/ppermute | solution.py:323
  18.4 13.0 %gather_observed.1 = bf16[16,16,512]{2,1,0:T(8,128)(2,1)} custom-call(s32[16,1,512]{2,1,0:T(1,128)} %get-tuple-element.92.cell_ref, s32[16,1,512]{2,1,0:T(1,128)} %get-tuple-element.91.level_ref, bf16[16,8,24576]{2,1,0:T(8,128)(2,1)} %prior_ref.5), custom_call_target="tpu_custom_call" | custom-call | tf_op jit(solution)/shard_map/gather_observed/pallas_call | solution.py:57
  32.6 3.1 shard_map.69
  41.2 3.5 shard_map.64
  45.6 6.0 %all-to-all-start.1 = ((bf16[16,16,512]{2,1,0:T(8,128)(2,1)}), bf16[16,16,512]{2,1,0:T(8,128)(2,1)S(1)}, u32[]{:S(2)}, u32[]{:S(2)}) async-start(bf16[16,16,512]{2,1,0:T(8,128)(2,1)} %add.143), calls=%async_computation.1 | async-start | bytes 524288 | tf_op jit(solution)/shard_map/all_to_all | solution.py:302
  55.3 3.0 collective-permute-start
  58.3 13.2 %collective-permute-done.25.refs_3_ = bf16[2,16,8,768]{3,2,1,0:T(8,128)(2,1)S(1)} collective-permute-done((bf16[2,16,8,768]{3,2,1,0:T(8,128)(2,1)}, bf16[2,16,8,768]{3,2,1,0:T(8,128)(2,1)S(1)}, u32[]{:S(2)}, u32[]{:S(2)}) %collective-permute-start.25) | collective-permute-done | bytes 393248 | tf_op jit(solution)/shard_map/ppermute | solution.py:323
  80.1 32.2 %collective-permute-done.28.refs_6_ = bf16[2,16,8,768]{3,2,1,0:T(8,128)(2,1)S(1)} collective-permute-done((bf16[2,16,8,768]{3,2,1,0:T(8,128)(2,1)}, bf16[2,16,8,768]{3,2,1,0:T(8,128)(2,1)S(1)}, u32[]{:S(2)}, u32[]{:S(2)}) %collective-permute-start.28) | collective-permute-done | bytes 393248 | tf_op jit(solution)/shard_map/ppermute | solution.py:323
  113.2 15.4 %collective-permute-start.6 = (bf16[2,16,8,768]{3,2,1,0:T(8,128)(2,1)}, bf16[2,16,8,768]{3,2,1,0:T(8,128)(2,1)S(1)}, u32[]{:S(2)}, u32[]{:S(2)}) collective-permute-start(bf16[2,16,8,768]{3,2,1,0:T(8,128)(2,1)} %get-tuple-element.46), channel_id=1, source_target_pairs={{0,16},{2,18},{4,20},{6,22},{8,24},{10,26},{12,28},{14,30},{16,0},... | collective-permute-start | bytes 1179656 | tf_op jit(solution)/shard_map/ppermute | solution.py:323
  129.9 5.7 %collective-permute-start.10 = (bf16[256,512]{1,0:T(8,128)(2,1)S(1)}, bf16[256,512]{1,0:T(8,128)(2,1)S(1)}, u32[]{:S(2)}, u32[]{:S(2)}) collective-permute-start(bf16[256,512]{1,0:T(8,128)(2,1)S(1)} %bitcast.86), channel_id=1, source_target_pairs={{2,0},{4,2},{6,4},{8,6},{10,8},{12,10},{14,12},{16,14},{18,16},{20... | collective-permute-start | bytes 786440 | tf_op jit(solution)/shard_map/ppermute | solution.py:349
  141.4 15.0 %collective-permute-done.4.refs_4_ = bf16[2,16,8,768]{3,2,1,0:T(8,128)(2,1)S(1)} collective-permute-done((bf16[2,16,8,768]{3,2,1,0:T(8,128)(2,1)}, bf16[2,16,8,768]{3,2,1,0:T(8,128)(2,1)S(1)}, u32[]{:S(2)}, u32[]{:S(2)}) %collective-permute-start.4) | collective-permute-done | bytes 393248 | tf_op jit(solution)/shard_map/ppermute | solution.py:323
  156.5 5.2 %collective-permute-start.29 = (bf16[8,16,8,768]{3,2,1,0:T(8,128)(2,1)}, bf16[8,16,8,768]{3,2,1,0:T(8,128)(2,1)}, u32[]{:S(2)}, u32[]{:S(2)}) collective-permute-start(bf16[8,16,8,768]{3,2,1,0:T(8,128)(2,1)} %shard_map.70), channel_id=1, source_target_pairs={{0,2},{2,0},{4,6},{6,4},{8,10},{10,8},{12,14},{14,12},{16,18},{18,... | collective-permute-start | bytes 4718600 | tf_op jit(solution)/shard_map/ppermute | solution.py:326
  181.2 10.4 %collective-permute-done.11.refs_10_ = bf16[3,256,256]{2,1,0:T(8,128)(2,1)S(1)} collective-permute-done((bf16[3,256,256]{2,1,0:T(8,128)(2,1)S(1)}, bf16[3,256,256]{2,1,0:T(8,128)(2,1)S(1)}, u32[]{:S(2)}, u32[]{:S(2)}) %collective-permute-start.11) | collective-permute-done | bytes 393248 | tf_op jit(solution)/shard_map/ppermute | solution.py:368
  192.4 7.6 %shard_map.71 = (bf16[8,16,8,768]{3,2,1,0:T(8,128)(2,1)}, bf16[8,16,8,768]{3,2,1,0:T(8,128)(2,1)}) custom-call(bf16[2,16,8,768]{3,2,1,0:T(8,128)(2,1)} %copy-done.12, bf16[2,16,8,768]{3,2,1,0:T(8,128)(2,1)} %copy-done.13, bf16[2,16,8,768]{3,2,1,0:T(8,128)(2,1)} %copy-done.14, bf16[2,16,8,768]{3,2,1,0:T(8,128)(2,1)} %copy-done.15, ...), custom_call_target="tpu_custom_call" | custom-call | tf_op jit(solution)/shard_map/pallas_call | solution.py:252
  202.1 3.7 collective-permute-start.12
  210.2 7.5 %shard_map.66 = (bf16[8,16,8,768]{3,2,1,0:T(8,128)(2,1)}, bf16[8,16,8,768]{3,2,1,0:T(8,128)(2,1)}) custom-call(bf16[2,16,8,768]{3,2,1,0:T(8,128)(2,1)} %copy-done.2, bf16[2,16,8,768]{3,2,1,0:T(8,128)(2,1)} %copy-done.3, bf16[2,16,8,768]{3,2,1,0:T(8,128)(2,1)} %copy-done.4, bf16[2,16,8,768]{3,2,1,0:T(8,128)(2,1)} %copy-done.5, ...), custom_call_target="tpu_custom_call" | custom-call | tf_op jit(solution)/shard_map/pallas_call | solution.py:252
  217.7 4.8 %collective-permute-start.14 = (bf16[8,16,8,768]{3,2,1,0:T(8,128)(2,1)}, bf16[8,16,8,768]{3,2,1,0:T(8,128)(2,1)S(1)}, u32[]{:S(2)}, u32[]{:S(2)}) collective-permute-start(bf16[8,16,8,768]{3,2,1,0:T(8,128)(2,1)} %get-tuple-element.49), channel_id=1, source_target_pairs={{0,2},{2,0},{4,6},{6,4},{8,10},{10,8},{12,14},{14,12},{16,18},{18,... | collective-permute-start | bytes 4718600 | tf_op jit(solution)/shard_map/ppermute | solution.py:326
  223.7 3.4 shard_map.72
  233.1 3.5 shard_map.67
  236.6 4.3 %collective-permute-done.31.refs_0_ = bf16[2,16,8,768]{3,2,1,0:T(8,128)(2,1)S(1)} collective-permute-done((bf16[2,16,8,768]{3,2,1,0:T(8,128)(2,1)}, bf16[2,16,8,768]{3,2,1,0:T(8,128)(2,1)S(1)}, u32[]{:S(2)}, u32[]{:S(2)}) %collective-permute-start.31) | collective-permute-done | bytes 393248 | tf_op jit(solution)/shard_map/ppermute | solution.py:323
  240.8 8.2 %collective-permute-done.32.refs_1_ = bf16[2,16,8,768]{3,2,1,0:T(8,128)(2,1)S(1)} collective-permute-done((bf16[2,16,8,768]{3,2,1,0:T(8,128)(2,1)}, bf16[2,16,8,768]{3,2,1,0:T(8,128)(2,1)S(1)}, u32[]{:S(2)}, u32[]{:S(2)}) %collective-permute-start.32) | collective-permute-done | bytes 393248 | tf_op jit(solution)/shard_map/ppermute | solution.py:323
  249.1 3.9 %collective-permute-start.37 = (bf16[2,16,8,768]{3,2,1,0:T(8,128)(2,1)}, bf16[2,16,8,768]{3,2,1,0:T(8,128)(2,1)S(1)}, u32[]{:S(2)}, u32[]{:S(2)}) collective-permute-start(bf16[2,16,8,768]{3,2,1,0:T(8,128)(2,1)} %get-tuple-element.73), channel_id=1, source_target_pairs={{0,16},{2,18},{4,20},{6,22},{8,24},{10,26},{12,28},{14,30},{16,0},... | collective-permute-start | bytes 1179656 | tf_op jit(solution)/shard_map/ppermute | solution.py:323
  252.9 6.3 %collective-permute-done.33.refs_2_ = bf16[2,16,8,768]{3,2,1,0:T(8,128)(2,1)S(1)} collective-permute-done((bf16[2,16,8,768]{3,2,1,0:T(8,128)(2,1)}, bf16[2,16,8,768]{3,2,1,0:T(8,128)(2,1)S(1)}, u32[]{:S(2)}, u32[]{:S(2)}) %collective-permute-start.33) | collective-permute-done | bytes 393248 | tf_op jit(solution)/shard_map/ppermute | solution.py:323
  260.0 5.9 %collective-permute-done.34.refs_3_ = bf16[2,16,8,768]{3,2,1,0:T(8,128)(2,1)S(1)} collective-permute-done((bf16[2,16,8,768]{3,2,1,0:T(8,128)(2,1)}, bf16[2,16,8,768]{3,2,1,0:T(8,128)(2,1)S(1)}, u32[]{:S(2)}, u32[]{:S(2)}) %collective-permute-start.34) | collective-permute-done | bytes 393248 | tf_op jit(solution)/shard_map/ppermute | solution.py:323
  266.0 3.2 collective-permute-start.18
  269.1 32.2 %collective-permute-done.35.refs_4_ = bf16[2,16,8,768]{3,2,1,0:T(8,128)(2,1)S(1)} collective-permute-done((bf16[2,16,8,768]{3,2,1,0:T(8,128)(2,1)}, bf16[2,16,8,768]{3,2,1,0:T(8,128)(2,1)S(1)}, u32[]{:S(2)}, u32[]{:S(2)}) %collective-permute-start.35) | collective-permute-done | bytes 393248 | tf_op jit(solution)/shard_map/ppermute | solution.py:323
  301.4 4.3 %collective-permute-done.37.refs_6_ = bf16[2,16,8,768]{3,2,1,0:T(8,128)(2,1)S(1)} collective-permute-done((bf16[2,16,8,768]{3,2,1,0:T(8,128)(2,1)}, bf16[2,16,8,768]{3,2,1,0:T(8,128)(2,1)S(1)}, u32[]{:S(2)}, u32[]{:S(2)}) %collective-permute-start.37) | collective-permute-done | bytes 393248 | tf_op jit(solution)/shard_map/ppermute | solution.py:323
  305.8 11.8 %collective-permute-start.21 = (bf16[2,16,8,768]{3,2,1,0:T(8,128)(2,1)}, bf16[2,16,8,768]{3,2,1,0:T(8,128)(2,1)}, u32[]{:S(2)}, u32[]{:S(2)}) collective-permute-start(bf16[2,16,8,768]{3,2,1,0:T(8,128)(2,1)} %get-tuple-element.56), channel_id=1, source_target_pairs={{0,20},{2,22},{4,16},{6,18},{8,28},{10,30},{12,24},{14,26},{16,4},... | collective-permute-start | bytes 1179656 | tf_op jit(solution)/shard_map/ppermute | solution.py:323
  320.1 18.0 %collective-permute-start.16 = (bf16[2,16,8,768]{3,2,1,0:T(8,128)(2,1)}, bf16[2,16,8,768]{3,2,1,0:T(8,128)(2,1)S(1)}, u32[]{:S(2)}, u32[]{:S(2)}) collective-permute-start(bf16[2,16,8,768]{3,2,1,0:T(8,128)(2,1)} %get-tuple-element.51), channel_id=1, source_target_pairs={{0,16},{2,18},{4,20},{6,22},{8,24},{10,26},{12,28},{14,30},{16,0},... | collective-permute-start | bytes 1179656 | tf_op jit(solution)/shard_map/ppermute | solution.py:323
  338.2 3.5 shard_map.73.refs_6_
  341.6 18.8 %collective-permute-done.21.refs_4_ = bf16[2,16,8,768]{3,2,1,0:T(8,128)(2,1)} collective-permute-done((bf16[2,16,8,768]{3,2,1,0:T(8,128)(2,1)}, bf16[2,16,8,768]{3,2,1,0:T(8,128)(2,1)}, u32[]{:S(2)}, u32[]{:S(2)}) %collective-permute-start.21) | collective-permute-done | bytes 393248 | tf_op jit(solution)/shard_map/ppermute | solution.py:323
  (177 shorter events, 77.7 us)
Async XLA Ops:
  12.5 25.5 %collective-permute-start.22 = (bf16[2,16,8,768]{3,2,1,0:T(8,128)(2,1)}, bf16[2,16,8,768]{3,2,1,0:T(8,128)(2,1)S(1)}, u32[]{:S(2)}, u32[]{:S(2)}) collective-permute-start(bf16[2,16,8,768]{3,2,1,0:T(8,128)(2,1)} %shard_map.68), channel_id=1, source_target_pairs={{0,28},{2,30},{4,24},{6,26},{8,20},{10,22},{12,16},{14,18},{16,12}... | collective-permute-start | bytes 1179656 | tf_op jit(solution)/shard_map/ppermute | solution.py:323
  36.5 18.8 %collective-permute-start.24 = (bf16[2,16,8,768]{3,2,1,0:T(8,128)(2,1)}, bf16[2,16,8,768]{3,2,1,0:T(8,128)(2,1)S(1)}, u32[]{:S(2)}, u32[]{:S(2)}) collective-permute-start(bf16[2,16,8,768]{3,2,1,0:T(8,128)(2,1)} %get-tuple-element.59), channel_id=1, source_target_pairs={{0,24},{2,26},{4,28},{6,30},{8,16},{10,18},{12,20},{14,22},{16,8},... | collective-permute-start | bytes 1179656 | tf_op jit(solution)/shard_map/ppermute | solution.py:323
  37.8 33.6 %collective-permute-start.25 = (bf16[2,16,8,768]{3,2,1,0:T(8,128)(2,1)}, bf16[2,16,8,768]{3,2,1,0:T(8,128)(2,1)S(1)}, u32[]{:S(2)}, u32[]{:S(2)}) collective-permute-start(bf16[2,16,8,768]{3,2,1,0:T(8,128)(2,1)} %get-tuple-element.60), channel_id=1, source_target_pairs={{0,8},{2,10},{4,12},{6,14},{8,0},{10,2},{12,4},{14,6},{16,24},{18,... | collective-permute-start | bytes 1179656 | tf_op jit(solution)/shard_map/ppermute | solution.py:323
  38.0 34.9 %collective-permute-start.26 = (bf16[2,16,8,768]{3,2,1,0:T(8,128)(2,1)}, bf16[2,16,8,768]{3,2,1,0:T(8,128)(2,1)S(1)}, u32[]{:S(2)}, u32[]{:S(2)}) collective-permute-start(bf16[2,16,8,768]{3,2,1,0:T(8,128)(2,1)} %get-tuple-element.61), channel_id=1, source_target_pairs={{0,20},{2,22},{4,16},{6,18},{8,28},{10,30},{12,24},{14,26},{16,4},... | collective-permute-start | bytes 1179656 | tf_op jit(solution)/shard_map/ppermute | solution.py:323
  40.7 34.1 %collective-permute-start.27 = (bf16[2,16,8,768]{3,2,1,0:T(8,128)(2,1)}, bf16[2,16,8,768]{3,2,1,0:T(8,128)(2,1)S(1)}, u32[]{:S(2)}, u32[]{:S(2)}) collective-permute-start(bf16[2,16,8,768]{3,2,1,0:T(8,128)(2,1)} %get-tuple-element.62), channel_id=1, source_target_pairs={{0,4},{2,6},{4,0},{6,2},{8,12},{10,14},{12,8},{14,10},{16,20},{18,... | collective-permute-start | bytes 1179656 | tf_op jit(solution)/shard_map/ppermute | solution.py:323
  45.6 84.3 %all-to-all-start.1 = ((bf16[16,16,512]{2,1,0:T(8,128)(2,1)}), bf16[16,16,512]{2,1,0:T(8,128)(2,1)S(1)}, u32[]{:S(2)}, u32[]{:S(2)}) async-start(bf16[16,16,512]{2,1,0:T(8,128)(2,1)} %add.143), calls=%async_computation.1 | async-start | bytes 524288 | tf_op jit(solution)/shard_map/all_to_all | solution.py:302
  51.6 60.6 %collective-permute-start.28 = (bf16[2,16,8,768]{3,2,1,0:T(8,128)(2,1)}, bf16[2,16,8,768]{3,2,1,0:T(8,128)(2,1)S(1)}, u32[]{:S(2)}, u32[]{:S(2)}) collective-permute-start(bf16[2,16,8,768]{3,2,1,0:T(8,128)(2,1)} %get-tuple-element.63), channel_id=1, source_target_pairs={{0,16},{2,18},{4,20},{6,22},{8,24},{10,26},{12,28},{14,30},{16,0},... | collective-permute-start | bytes 1179656 | tf_op jit(solution)/shard_map/ppermute | solution.py:323
  55.3 57.8 %collective-permute-start = (bf16[2,16,8,768]{3,2,1,0:T(8,128)(2,1)}, bf16[2,16,8,768]{3,2,1,0:T(8,128)(2,1)S(1)}, u32[]{:S(2)}, u32[]{:S(2)}) collective-permute-start(bf16[2,16,8,768]{3,2,1,0:T(8,128)(2,1)} %get-tuple-element.40), channel_id=1, source_target_pairs={{0,28},{2,30},{4,24},{6,26},{8,20},{10,22},{12,16},{14,18},{16,12}... | collective-permute-start | bytes 1179656 | tf_op jit(solution)/shard_map/ppermute | solution.py:323
  72.2 41.0 %collective-permute-start.1 = (bf16[2,16,8,768]{3,2,1,0:T(8,128)(2,1)}, bf16[2,16,8,768]{3,2,1,0:T(8,128)(2,1)S(1)}, u32[]{:S(2)}, u32[]{:S(2)}) collective-permute-start(bf16[2,16,8,768]{3,2,1,0:T(8,128)(2,1)} %get-tuple-element.41), channel_id=1, source_target_pairs={{0,12},{2,14},{4,8},{6,10},{8,4},{10,6},{12,0},{14,2},{16,28},{18,... | collective-permute-start | bytes 1179656 | tf_op jit(solution)/shard_map/ppermute | solution.py:323
  73.7 56.3 %collective-permute-start.2 = (bf16[2,16,8,768]{3,2,1,0:T(8,128)(2,1)}, bf16[2,16,8,768]{3,2,1,0:T(8,128)(2,1)S(1)}, u32[]{:S(2)}, u32[]{:S(2)}) collective-permute-start(bf16[2,16,8,768]{3,2,1,0:T(8,128)(2,1)} %get-tuple-element.42), channel_id=1, source_target_pairs={{0,24},{2,26},{4,28},{6,30},{8,16},{10,18},{12,20},{14,22},{16,8},... | collective-permute-start | bytes 1179656 | tf_op jit(solution)/shard_map/ppermute | solution.py:323
  75.6 60.0 %collective-permute-start.3 = (bf16[2,16,8,768]{3,2,1,0:T(8,128)(2,1)}, bf16[2,16,8,768]{3,2,1,0:T(8,128)(2,1)S(1)}, u32[]{:S(2)}, u32[]{:S(2)}) collective-permute-start(bf16[2,16,8,768]{3,2,1,0:T(8,128)(2,1)} %get-tuple-element.43), channel_id=1, source_target_pairs={{0,8},{2,10},{4,12},{6,14},{8,0},{10,2},{12,4},{14,6},{16,24},{18,... | collective-permute-start | bytes 1179656 | tf_op jit(solution)/shard_map/ppermute | solution.py:323
  113.0 43.4 %collective-permute-start.4 = (bf16[2,16,8,768]{3,2,1,0:T(8,128)(2,1)}, bf16[2,16,8,768]{3,2,1,0:T(8,128)(2,1)S(1)}, u32[]{:S(2)}, u32[]{:S(2)}) collective-permute-start(bf16[2,16,8,768]{3,2,1,0:T(8,128)(2,1)} %get-tuple-element.44), channel_id=1, source_target_pairs={{0,20},{2,22},{4,16},{6,18},{8,28},{10,30},{12,24},{14,26},{16,4},... | collective-permute-start | bytes 1179656 | tf_op jit(solution)/shard_map/ppermute | solution.py:323
  113.1 48.6 %collective-permute-start.5 = (bf16[2,16,8,768]{3,2,1,0:T(8,128)(2,1)}, bf16[2,16,8,768]{3,2,1,0:T(8,128)(2,1)S(1)}, u32[]{:S(2)}, u32[]{:S(2)}) collective-permute-start(bf16[2,16,8,768]{3,2,1,0:T(8,128)(2,1)} %get-tuple-element.45), channel_id=1, source_target_pairs={{0,4},{2,6},{4,0},{6,2},{8,12},{10,14},{12,8},{14,10},{16,20},{18,... | collective-permute-start | bytes 1179656 | tf_op jit(solution)/shard_map/ppermute | solution.py:323
  113.2 49.7 %collective-permute-start.6 = (bf16[2,16,8,768]{3,2,1,0:T(8,128)(2,1)}, bf16[2,16,8,768]{3,2,1,0:T(8,128)(2,1)S(1)}, u32[]{:S(2)}, u32[]{:S(2)}) collective-permute-start(bf16[2,16,8,768]{3,2,1,0:T(8,128)(2,1)} %get-tuple-element.46), channel_id=1, source_target_pairs={{0,16},{2,18},{4,20},{6,22},{8,24},{10,26},{12,28},{14,30},{16,0},... | collective-permute-start | bytes 1179656 | tf_op jit(solution)/shard_map/ppermute | solution.py:323
  129.9 37.6 %collective-permute-start.10 = (bf16[256,512]{1,0:T(8,128)(2,1)S(1)}, bf16[256,512]{1,0:T(8,128)(2,1)S(1)}, u32[]{:S(2)}, u32[]{:S(2)}) collective-permute-start(bf16[256,512]{1,0:T(8,128)(2,1)S(1)} %bitcast.86), channel_id=1, source_target_pairs={{2,0},{4,2},{6,4},{8,6},{10,8},{12,10},{14,12},{16,14},{18,16},{20... | collective-permute-start | bytes 786440 | tf_op jit(solution)/shard_map/ppermute | solution.py:349
  135.6 31.9 %collective-permute-start.9 = (bf16[256,512]{1,0:T(8,128)(2,1)S(1)}, bf16[256,512]{1,0:T(8,128)(2,1)}, u32[]{:S(2)}, u32[]{:S(2)}) collective-permute-start(bf16[256,512]{1,0:T(8,128)(2,1)S(1)} %bitcast.87), channel_id=1, source_target_pairs={{0,2},{2,4},{4,6},{6,8},{8,10},{10,12},{12,14},{14,16},{16,18},{18... | collective-permute-start | bytes 786440 | tf_op jit(solution)/shard_map/ppermute | solution.py:349
  156.5 35.1 %collective-permute-start.29 = (bf16[8,16,8,768]{3,2,1,0:T(8,128)(2,1)}, bf16[8,16,8,768]{3,2,1,0:T(8,128)(2,1)}, u32[]{:S(2)}, u32[]{:S(2)}) collective-permute-start(bf16[8,16,8,768]{3,2,1,0:T(8,128)(2,1)} %shard_map.70), channel_id=1, source_target_pairs={{0,2},{2,0},{4,6},{6,4},{8,10},{10,8},{12,14},{14,12},{16,18},{18,... | collective-permute-start | bytes 4718600 | tf_op jit(solution)/shard_map/ppermute | solution.py:326
  166.1 42.3 %collective-permute-start.7 = (bf16[8,16,8,768]{3,2,1,0:T(8,128)(2,1)}, bf16[8,16,8,768]{3,2,1,0:T(8,128)(2,1)S(1)}, u32[]{:S(2)}, u32[]{:S(2)}) collective-permute-start(bf16[8,16,8,768]{3,2,1,0:T(8,128)(2,1)} %shard_map.65), channel_id=1, source_target_pairs={{0,2},{2,0},{4,6},{6,4},{8,10},{10,8},{12,14},{14,12},{16,18},{18,... | collective-permute-start | bytes 4718600 | tf_op jit(solution)/shard_map/ppermute | solution.py:326
  200.0 22.6 %collective-permute-start.30 = (bf16[8,16,8,768]{3,2,1,0:T(8,128)(2,1)}, bf16[8,16,8,768]{3,2,1,0:T(8,128)(2,1)S(1)}, u32[]{:S(2)}, u32[]{:S(2)}) collective-permute-start(bf16[8,16,8,768]{3,2,1,0:T(8,128)(2,1)} %get-tuple-element.66), channel_id=1, source_target_pairs={{0,2},{2,0},{4,6},{6,4},{8,10},{10,8},{12,14},{14,12},{16,18},{18,... | collective-permute-start | bytes 4718600 | tf_op jit(solution)/shard_map/ppermute | solution.py:326
  227.2 21.8 %collective-permute-start.32 = (bf16[2,16,8,768]{3,2,1,0:T(8,128)(2,1)}, bf16[2,16,8,768]{3,2,1,0:T(8,128)(2,1)S(1)}, u32[]{:S(2)}, u32[]{:S(2)}) collective-permute-start(bf16[2,16,8,768]{3,2,1,0:T(8,128)(2,1)} %get-tuple-element.68), channel_id=1, source_target_pairs={{0,12},{2,14},{4,8},{6,10},{8,4},{10,6},{12,0},{14,2},{16,28},{18,... | collective-permute-start | bytes 1179656 | tf_op jit(solution)/shard_map/ppermute | solution.py:323
  227.3 31.9 %collective-permute-start.33 = (bf16[2,16,8,768]{3,2,1,0:T(8,128)(2,1)}, bf16[2,16,8,768]{3,2,1,0:T(8,128)(2,1)S(1)}, u32[]{:S(2)}, u32[]{:S(2)}) collective-permute-start(bf16[2,16,8,768]{3,2,1,0:T(8,128)(2,1)} %get-tuple-element.69), channel_id=1, source_target_pairs={{0,24},{2,26},{4,28},{6,30},{8,16},{10,18},{12,20},{14,22},{16,8},... | collective-permute-start | bytes 1179656 | tf_op jit(solution)/shard_map/ppermute | solution.py:323
  229.9 36.0 %collective-permute-start.34 = (bf16[2,16,8,768]{3,2,1,0:T(8,128)(2,1)}, bf16[2,16,8,768]{3,2,1,0:T(8,128)(2,1)S(1)}, u32[]{:S(2)}, u32[]{:S(2)}) collective-permute-start(bf16[2,16,8,768]{3,2,1,0:T(8,128)(2,1)} %get-tuple-element.70), channel_id=1, source_target_pairs={{0,8},{2,10},{4,12},{6,14},{8,0},{10,2},{12,4},{14,6},{16,24},{18,... | collective-permute-start | bytes 1179656 | tf_op jit(solution)/shard_map/ppermute | solution.py:323
  232.0 69.4 %collective-permute-start.35 = (bf16[2,16,8,768]{3,2,1,0:T(8,128)(2,1)}, bf16[2,16,8,768]{3,2,1,0:T(8,128)(2,1)S(1)}, u32[]{:S(2)}, u32[]{:S(2)}) collective-permute-start(bf16[2,16,8,768]{3,2,1,0:T(8,128)(2,1)} %get-tuple-element.71), channel_id=1, source_target_pairs={{0,20},{2,22},{4,16},{6,18},{8,28},{10,30},{12,24},{14,26},{16,4},... | collective-permute-start | bytes 1179656 | tf_op jit(solution)/shard_map/ppermute | solution.py:323
  240.8 60.5 %collective-permute-start.36 = (bf16[2,16,8,768]{3,2,1,0:T(8,128)(2,1)}, bf16[2,16,8,768]{3,2,1,0:T(8,128)(2,1)S(1)}, u32[]{:S(2)}, u32[]{:S(2)}) collective-permute-start(bf16[2,16,8,768]{3,2,1,0:T(8,128)(2,1)} %get-tuple-element.72), channel_id=1, source_target_pairs={{0,4},{2,6},{4,0},{6,2},{8,12},{10,14},{12,8},{14,10},{16,20},{18,... | collective-permute-start | bytes 1179656 | tf_op jit(solution)/shard_map/ppermute | solution.py:323
  249.1 56.7 %collective-permute-start.37 = (bf16[2,16,8,768]{3,2,1,0:T(8,128)(2,1)}, bf16[2,16,8,768]{3,2,1,0:T(8,128)(2,1)S(1)}, u32[]{:S(2)}, u32[]{:S(2)}) collective-permute-start(bf16[2,16,8,768]{3,2,1,0:T(8,128)(2,1)} %get-tuple-element.73), channel_id=1, source_target_pairs={{0,16},{2,18},{4,20},{6,22},{8,24},{10,26},{12,28},{14,30},{16,0},... | collective-permute-start | bytes 1179656 | tf_op jit(solution)/shard_map/ppermute | solution.py:323
  259.3 58.3 %collective-permute-start.17 = (bf16[2,16,8,768]{3,2,1,0:T(8,128)(2,1)}, bf16[2,16,8,768]{3,2,1,0:T(8,128)(2,1)S(1)}, u32[]{:S(2)}, u32[]{:S(2)}) collective-permute-start(bf16[2,16,8,768]{3,2,1,0:T(8,128)(2,1)} %get-tuple-element.52), channel_id=1, source_target_pairs={{0,28},{2,30},{4,24},{6,26},{8,20},{10,22},{12,16},{14,18},{16,12}... | collective-permute-start | bytes 1179656 | tf_op jit(solution)/shard_map/ppermute | solution.py:323
  266.0 53.4 %collective-permute-start.18 = (bf16[2,16,8,768]{3,2,1,0:T(8,128)(2,1)}, bf16[2,16,8,768]{3,2,1,0:T(8,128)(2,1)S(1)}, u32[]{:S(2)}, u32[]{:S(2)}) collective-permute-start(bf16[2,16,8,768]{3,2,1,0:T(8,128)(2,1)} %get-tuple-element.53), channel_id=1, source_target_pairs={{0,12},{2,14},{4,8},{6,10},{8,4},{10,6},{12,0},{14,2},{16,28},{18,... | collective-permute-start | bytes 1179656 | tf_op jit(solution)/shard_map/ppermute | solution.py:323
  301.3 40.3 %collective-permute-start.19 = (bf16[2,16,8,768]{3,2,1,0:T(8,128)(2,1)}, bf16[2,16,8,768]{3,2,1,0:T(8,128)(2,1)}, u32[]{:S(2)}, u32[]{:S(2)}) collective-permute-start(bf16[2,16,8,768]{3,2,1,0:T(8,128)(2,1)} %get-tuple-element.54), channel_id=1, source_target_pairs={{0,24},{2,26},{4,28},{6,30},{8,16},{10,18},{12,20},{14,22},{16,8},... | collective-permute-start | bytes 1179656 | tf_op jit(solution)/shard_map/ppermute | solution.py:323
  301.3 40.3 %collective-permute-start.20 = (bf16[2,16,8,768]{3,2,1,0:T(8,128)(2,1)}, bf16[2,16,8,768]{3,2,1,0:T(8,128)(2,1)}, u32[]{:S(2)}, u32[]{:S(2)}) collective-permute-start(bf16[2,16,8,768]{3,2,1,0:T(8,128)(2,1)} %get-tuple-element.55), channel_id=1, source_target_pairs={{0,8},{2,10},{4,12},{6,14},{8,0},{10,2},{12,4},{14,6},{16,24},{18,... | collective-permute-start | bytes 1179656 | tf_op jit(solution)/shard_map/ppermute | solution.py:323
  305.8 54.7 %collective-permute-start.21 = (bf16[2,16,8,768]{3,2,1,0:T(8,128)(2,1)}, bf16[2,16,8,768]{3,2,1,0:T(8,128)(2,1)}, u32[]{:S(2)}, u32[]{:S(2)}) collective-permute-start(bf16[2,16,8,768]{3,2,1,0:T(8,128)(2,1)} %get-tuple-element.56), channel_id=1, source_target_pairs={{0,20},{2,22},{4,16},{6,18},{8,28},{10,30},{12,24},{14,26},{16,4},... | collective-permute-start | bytes 1179656 | tf_op jit(solution)/shard_map/ppermute | solution.py:323
  318.4 44.9 %collective-permute-start.15 = (bf16[2,16,8,768]{3,2,1,0:T(8,128)(2,1)}, bf16[2,16,8,768]{3,2,1,0:T(8,128)(2,1)S(1)}, u32[]{:S(2)}, u32[]{:S(2)}) collective-permute-start(bf16[2,16,8,768]{3,2,1,0:T(8,128)(2,1)} %get-tuple-element.50), channel_id=1, source_target_pairs={{0,4},{2,6},{4,0},{6,2},{8,12},{10,14},{12,8},{14,10},{16,20},{18,... | collective-permute-start | bytes 1179656 | tf_op jit(solution)/shard_map/ppermute | solution.py:323
  320.1 44.7 %collective-permute-start.16 = (bf16[2,16,8,768]{3,2,1,0:T(8,128)(2,1)}, bf16[2,16,8,768]{3,2,1,0:T(8,128)(2,1)S(1)}, u32[]{:S(2)}, u32[]{:S(2)}) collective-permute-start(bf16[2,16,8,768]{3,2,1,0:T(8,128)(2,1)} %get-tuple-element.51), channel_id=1, source_target_pairs={{0,16},{2,18},{4,20},{6,22},{8,24},{10,26},{12,28},{14,30},{16,0},... | collective-permute-start | bytes 1179656 | tf_op jit(solution)/shard_map/ppermute | solution.py:323
  (44 other events, 790.5 us)

commit v3 on v2

--- a/solution.py
+++ b/solution.py
@@ -47,10 +47,14 @@
     found = found.reshape(members, tiers, slots)
     tier = lax.broadcasted_iota(jnp.int32, (members, tiers, slots), 1)
     found = jnp.where(tier == level_ref[...], found, 0.0)
-    out_ref[0] = jnp.sum(found, axis=1).astype(jnp.bfloat16)
-
-
-def gather_observed(prior, cell, level):
+    found = jnp.sum(found, axis=1).astype(jnp.bfloat16)
+    levels, _, _, share = out_ref.shape
+    rank = lax.axis_index("level")
+    for h in range(levels):
+        out_ref[lax.rem(h + rank, levels), 0] = found[:, h * share : (h + 1) * share]
+
+
+def gather_observed(prior, cell, level, levels):
     members, tiers, total = prior.shape
     regions, _, slots = cell.shape
     cells = total // regions
@@ -62,8 +66,10 @@
             pl.BlockSpec((1, 1, slots), lambda r: (r, 0, 0)),
             pl.BlockSpec((members, tiers, cells), lambda r: (0, 0, r)),
         ],
-        out_specs=pl.BlockSpec((1, members, slots), lambda r: (r, 0, 0)),
-        out_shape=jax.ShapeDtypeStruct((regions, members, slots), jnp.bfloat16),
+        out_specs=pl.BlockSpec((levels, 1, members, slots // levels), lambda r: (0, r, 0, 0)),
+        out_shape=jax.ShapeDtypeStruct(
+            (levels, regions, members, slots // levels), jnp.bfloat16
+        ),
         name="gather_observed",
     )(cell, level, prior)
 
@@ -283,7 +289,7 @@
     frobenius = jnp.sqrt(jnp.sum(shifted * shifted, axis=(1, 2)))
     iterate = shifted / frobenius[:, None, None]
     inverse = 1.5 * identity[None] - 0.5 * iterate
-    high = lax.Precision.HIGH
+    high = lax.Precision.HIGHEST
     iterate = jnp.matmul(iterate, inverse, precision=high)
     for turn in range(1, NS_ITERS):
         factor = 1.5 * identity[None] - 0.5 * jnp.matmul(inverse, iterate, precision=high)
@@ -327,35 +333,40 @@
 
     live = jnp.arange(slots, dtype=jnp.int32) < active_slots[0]
     live_f = live.astype(jnp.float32)
-    records = jnp.stack(
-        [
-            jnp.where(live, measured_site, -1).astype(jnp.float32),
-            measured_datum,
-            inverse_variance * live_f,
-        ]
-    )
-    table = spread(jnp.broadcast_to(records[None], (regions,) + records.shape))
-    sites = table[:, 0:1].astype(jnp.int32)
+    slot_site = jnp.where(live, measured_site, -1).astype(jnp.float32)
+    table = spread(jnp.broadcast_to(slot_site[None, None], (regions, 1, slots)))
+    facts = jnp.stack([measured_datum, inverse_variance * live_f])
+    up = [(i, (i + 1) % regions) for i in range(regions)]
+    down = [(target_, source) for source, target_ in up]
+    facts = {
+        -1: lax.ppermute(facts, "region", up), 0: facts, 1: lax.ppermute(facts, "region", down)
+    }
+    sites = table.astype(jnp.int32)
     cell = jnp.where(sites < 0, -1, sites % grid_sites)
     tier = jnp.where(sites < 0, -1, sites // grid_sites - tier_rank * tiers)
-    observed = gather_observed(prior_samples, cell, tier)
+    observed = gather_observed(prior_samples, cell, tier, levels)
     flip = [(i, (i + 1) % levels) for i in range(levels)]
-    observed = observed + lax.ppermute(observed, "level", flip)
+    observed = observed[0] + lax.ppermute(observed[1], "level", flip)
     observed = spread(observed)
-    observed = observed.reshape(regions * members, slots)
-    up = [(i, (i + 1) % regions) for i in range(regions)]
-    down = [(target_, source) for source, target_ in up]
-    window = jnp.concatenate(
-        [lax.ppermute(observed, "region", up), observed, lax.ppermute(observed, "region", down)],
+    part = slots // levels
+    observed = observed.reshape(regions * members, part)
+    opposite = lax.ppermute(observed, "level", flip)
+    sides = jnp.concatenate(
+        [lax.ppermute(observed, "region", up), lax.ppermute(observed, "region", down)],
         axis=1,
     )
+    window = jnp.concatenate(
+        [observed, sides, opposite, lax.ppermute(sides, "level", flip)], axis=1
+    )
     near = []
-    for shift in (-1, 0, 1):
-        row = lax.dynamic_index_in_dim(table, (me + shift) % regions, axis=0, keepdims=False)
-        site = row[0].astype(jnp.int32)
-        here = (site >= 0).astype(jnp.float32)
-        point = jnp.where(site < 0, 0, site % grid_sites).astype(jnp.float32)
-        near.append(jnp.stack([row[1], row[2], point + shift * grid_sites, here]))
+    for rank in (tier_rank, 1 - tier_rank):
+        for shift in (0, -1, 1):
+            start = rank * part
+            site = lax.dynamic_slice(sites, ((me + shift) % regions, 0, start), (1, 1, part))[0, 0]
+            value, weight = lax.dynamic_slice_in_dim(facts[shift], start, part, axis=1)
+            here = (site >= 0).astype(jnp.float32)
+            point = jnp.where(site < 0, 0, site % grid_sites).astype(jnp.float32)
+            near.append(jnp.stack([value, weight, point + shift * grid_sites, here]))
     near = jnp.concatenate(near, axis=1)
     share = COARSE // levels
     coarse = (

time: 371 us -> 381 us (1.027)
  waiting for transfers between devices: 158 us -> 174 us
  starting transfers between devices: 114 us -> 102 us
  matrix products: 9.11 us -> 14.7 us
    all_to_all x2, waiting for transfers between devices: 0.9 us -> 13.4 us  [spread(): lax.all_to_all(block, 'region', split_axis=0, concat_axis=0, tiled=True)]
    ppermute x28, starting transfers between devices: 76.2 us -> 65.6 us  [swap(): return lax.ppermute(block, 'region', pairs)]
    ppermute x1 -> x5, waiting for transfers between devices: 0.01 us -> 8.18 us  [the longest x1 5.59 us: analyse(): lax.ppermute(sides, 'level', flip)]
    ppermute x1, starting transfers between devices: 5.66 us -> 0.01 us  [analyse(): lax.ppermute(observed, 'region', down)]
    ppermute x1 -> x5, starting transfers between devices: 1.24 us -> 5.66 us  [the longest x1 2.59 us: analyse(): lax.ppermute(facts, 'region', up)]
    unnamed x72 -> x80, local copies, waits for them, and re-layouts: 11.1 us -> 11.6 us
  transfers between devices with their start and end apart: 40 -> 44, of which waited for: 16 -> 19; matrix products, arithmetic and copies ran while one was open for 6% -> 9% of each run, Pallas kernels for 15% -> 14%
where the time goes in v3:
time: 381 us; the launch traced here: 379 us
  waiting for transfers between devices  174 us (46%)
  starting transfers between devices  102 us (27%)
  Pallas kernels  56.6 us (15%)
  other arithmetic  16 us (4%)
  matrix products  14.7 us (4%)
  local copies, waits for them, and re-layouts  13.4 us (4%)
    ppermute x28, waiting for transfers between devices, swap(): return lax.ppermute(block, 'region', pairs)  141 us
    ppermute x28, starting transfers between devices, swap(): return lax.ppermute(block, 'region', pairs)  65.6 us
    pallas_call x10, Pallas kernels, moved(): pl.pallas_call(kernel, in_specs=[anywhere] * len(operands), out_specs=[an...  28.5 us
    pallas_call x2, Pallas kernels, transform(): pl.pallas_call(functools.partial(transform_kernel, first, chips), grid=(1...  15 us
    all_to_all x2, waiting for transfers between devices, spread(): lax.all_to_all(block, 'region', split_axis=0, concat_axis=0, tiled=True)  13.4 us
    pallas_call x1, Pallas kernels, gather_observed(): pl.pallas_call(gather_kernel, grid=(regions,), in_specs=[pl.BlockSpec((1,...  13.1 us
    all_to_all x2, starting transfers between devices, spread(): lax.all_to_all(block, 'region', split_axis=0, concat_axis=0, tiled=True)  13 us
    ppermute x4, starting transfers between devices, swap_core(): return lax.ppermute(block, 'region', [(i, i ^ 1) for i in range(regions)])  12.3 us
  transfers between devices with their start and end apart: 44, of which 19 were waited for; matrix products, arithmetic and copies ran while one was open for 9% of the time, Pallas kernels for 14%

profile of v3, /device:TPU:1, one launch (start us, length us, event | category | flops | bytes accessed | tf_op | source)
XLA Modules:
  0.0 378.6 jit_solution(6844057897399202029)
XLA Ops:
  5.9 6.5 %all-to-all-start = ((f32[16,1,512]{2,1,0:T(1,128)}), f32[16,1,512]{2,1,0:T(1,128)S(1)}, u32[]{:S(2)}, u32[]{:S(2)}) async-start(f32[16,1,512]{2,1,0:T(1,128)} %broadcast_in_dim.19), calls=%async_computation | async-start | bytes 65536 | tf_op jit(solution)/shard_map/all_to_all | solution.py:308
  14.2 4.1 %collective-permute-start.26 = (bf16[2,16,8,768]{3,2,1,0:T(8,128)(2,1)}, bf16[2,16,8,768]{3,2,1,0:T(8,128)(2,1)S(1)}, u32[]{:S(2)}, u32[]{:S(2)}) collective-permute-start(bf16[2,16,8,768]{3,2,1,0:T(8,128)(2,1)} %shard_map.68), channel_id=1, source_target_pairs={{0,28},{2,30},{4,24},{6,26},{8,20},{10,22},{12,16},{14,18},{16,12}... | collective-permute-start | bytes 1179656 | tf_op jit(solution)/shard_map/ppermute | solution.py:329
  18.3 3.1 shard_map.69
  23.4 3.5 shard_map.64
  29.5 13.1 %gather_observed.1 = bf16[2,16,16,256]{3,2,1,0:T(8,128)(2,1)} custom-call(s32[16,1,512]{2,1,0:T(1,128)} %get-tuple-element.93.cell_ref, s32[16,1,512]{2,1,0:T(1,128)} %get-tuple-element.92.level_ref, bf16[16,8,24576]{2,1,0:T(8,128)(2,1)} %prior_ref.5), custom_call_target="tpu_custom_call" | custom-call | tf_op jit(solution)/shard_map/gather_observed/pallas_call | solution.py:61
  60.4 30.2 %collective-permute-done.30.refs_4_ = bf16[2,16,8,768]{3,2,1,0:T(8,128)(2,1)S(1)} collective-permute-done((bf16[2,16,8,768]{3,2,1,0:T(8,128)(2,1)}, bf16[2,16,8,768]{3,2,1,0:T(8,128)(2,1)S(1)}, u32[]{:S(2)}, u32[]{:S(2)}) %collective-permute-start.30) | collective-permute-done | bytes 393248 | tf_op jit(solution)/shard_map/ppermute | solution.py:329
  94.0 6.6 %all-to-all-start.1 = ((bf16[16,16,256]{2,1,0:T(8,128)(2,1)}), bf16[16,16,256]{2,1,0:T(8,128)(2,1)S(1)}, u32[]{:S(2)}, u32[]{:S(2)}) async-start(bf16[16,16,256]{2,1,0:T(8,128)(2,1)} %fusion.23), calls=%async_computation.1 | async-start | bytes 262144 | tf_op jit(solution)/shard_map/all_to_all | solution.py:308
  100.5 6.6 %collective-permute-done.32.refs_6_ = bf16[2,16,8,768]{3,2,1,0:T(8,128)(2,1)S(1)} collective-permute-done((bf16[2,16,8,768]{3,2,1,0:T(8,128)(2,1)}, bf16[2,16,8,768]{3,2,1,0:T(8,128)(2,1)S(1)}, u32[]{:S(2)}, u32[]{:S(2)}) %collective-permute-start.32) | collective-permute-done | bytes 393248 | tf_op jit(solution)/shard_map/ppermute | solution.py:329
  108.5 19.1 %collective-permute-start.6 = (bf16[2,16,8,768]{3,2,1,0:T(8,128)(2,1)}, bf16[2,16,8,768]{3,2,1,0:T(8,128)(2,1)S(1)}, u32[]{:S(2)}, u32[]{:S(2)}) collective-permute-start(bf16[2,16,8,768]{3,2,1,0:T(8,128)(2,1)} %get-tuple-element.46), channel_id=1, source_target_pairs={{0,16},{2,18},{4,20},{6,22},{8,24},{10,26},{12,28},{14,30},{16,0},... | collective-permute-start | bytes 1179656 | tf_op jit(solution)/shard_map/ppermute | solution.py:329
  131.4 13.4 %all-to-all-done.1 = bf16[16,16,256]{2,1,0:T(8,128)(2,1)S(1)} async-done(((bf16[16,16,256]{2,1,0:T(8,128)(2,1)}), bf16[16,16,256]{2,1,0:T(8,128)(2,1)S(1)}, u32[]{:S(2)}, u32[]{:S(2)}) %all-to-all-start.1) | async-done | bytes 131104 | tf_op jit(solution)/shard_map/all_to_all | solution.py:308
  152.4 3.5 collective-permute-start.33
  155.9 4.6 %collective-permute-done.6.refs_6_ = bf16[2,16,8,768]{3,2,1,0:T(8,128)(2,1)S(1)} collective-permute-done((bf16[2,16,8,768]{3,2,1,0:T(8,128)(2,1)}, bf16[2,16,8,768]{3,2,1,0:T(8,128)(2,1)S(1)}, u32[]{:S(2)}, u32[]{:S(2)}) %collective-permute-start.6) | collective-permute-done | bytes 393248 | tf_op jit(solution)/shard_map/ppermute | solution.py:329
  170.1 5.6 %collective-permute-done.12 = bf16[256,512]{1,0:T(8,128)(2,1)S(1)} collective-permute-done((bf16[256,512]{1,0:T(8,128)(2,1)S(1)}, bf16[256,512]{1,0:T(8,128)(2,1)S(1)}, u32[]{:S(2)}, u32[]{:S(2)}) %collective-permute-start.12) | collective-permute-done | bytes 262176 | tf_op jit(solution)/shard_map/ppermute | solution.py:359
  193.9 8.3 %collective-permute-done.15.refs_10_ = bf16[3,256,256]{2,1,0:T(8,128)(2,1)S(1)} collective-permute-done((bf16[3,256,256]{2,1,0:T(8,128)(2,1)S(1)}, bf16[3,256,256]{2,1,0:T(8,128)(2,1)S(1)}, u32[]{:S(2)}, u32[]{:S(2)}) %collective-permute-start.15) | collective-permute-done | bytes 393248 | tf_op jit(solution)/shard_map/ppermute | solution.py:379
  202.9 7.5 %shard_map.71 = (bf16[8,16,8,768]{3,2,1,0:T(8,128)(2,1)}, bf16[8,16,8,768]{3,2,1,0:T(8,128)(2,1)}) custom-call(bf16[2,16,8,768]{3,2,1,0:T(8,128)(2,1)} %copy-done.12, bf16[2,16,8,768]{3,2,1,0:T(8,128)(2,1)} %copy-done.13, bf16[2,16,8,768]{3,2,1,0:T(8,128)(2,1)} %copy-done.14, bf16[2,16,8,768]{3,2,1,0:T(8,128)(2,1)} %copy-done.15, ...), custom_call_target="tpu_custom_call" | custom-call | tf_op jit(solution)/shard_map/pallas_call | solution.py:258
  219.8 7.6 %shard_map.66 = (bf16[8,16,8,768]{3,2,1,0:T(8,128)(2,1)}, bf16[8,16,8,768]{3,2,1,0:T(8,128)(2,1)}) custom-call(bf16[2,16,8,768]{3,2,1,0:T(8,128)(2,1)} %copy-done.2, bf16[2,16,8,768]{3,2,1,0:T(8,128)(2,1)} %copy-done.3, bf16[2,16,8,768]{3,2,1,0:T(8,128)(2,1)} %copy-done.4, bf16[2,16,8,768]{3,2,1,0:T(8,128)(2,1)} %copy-done.5, ...), custom_call_target="tpu_custom_call" | custom-call | tf_op jit(solution)/shard_map/pallas_call | solution.py:258
  227.3 5.7 %collective-permute-start.18 = (bf16[8,16,8,768]{3,2,1,0:T(8,128)(2,1)}, bf16[8,16,8,768]{3,2,1,0:T(8,128)(2,1)S(1)}, u32[]{:S(2)}, u32[]{:S(2)}) collective-permute-start(bf16[8,16,8,768]{3,2,1,0:T(8,128)(2,1)} %get-tuple-element.49), channel_id=1, source_target_pairs={{0,2},{2,0},{4,6},{6,4},{8,10},{10,8},{12,14},{14,12},{16,18},{18,... | collective-permute-start | bytes 4718600 | tf_op jit(solution)/shard_map/ppermute | solution.py:332
  234.1 3.5 shard_map.72
  239.5 2.9 collective-permute-start.38
  243.6 3.5 shard_map.67
  247.0 4.3 %collective-permute-done.35.refs_0_ = bf16[2,16,8,768]{3,2,1,0:T(8,128)(2,1)S(1)} collective-permute-done((bf16[2,16,8,768]{3,2,1,0:T(8,128)(2,1)}, bf16[2,16,8,768]{3,2,1,0:T(8,128)(2,1)S(1)}, u32[]{:S(2)}, u32[]{:S(2)}) %collective-permute-start.35) | collective-permute-done | bytes 393248 | tf_op jit(solution)/shard_map/ppermute | solution.py:329
  251.3 8.4 %collective-permute-done.36.refs_1_ = bf16[2,16,8,768]{3,2,1,0:T(8,128)(2,1)S(1)} collective-permute-done((bf16[2,16,8,768]{3,2,1,0:T(8,128)(2,1)}, bf16[2,16,8,768]{3,2,1,0:T(8,128)(2,1)S(1)}, u32[]{:S(2)}, u32[]{:S(2)}) %collective-permute-start.36) | collective-permute-done | bytes 393248 | tf_op jit(solution)/shard_map/ppermute | solution.py:329
  259.8 3.2 collective-permute-start.41
  262.9 7.6 %collective-permute-done.37.refs_2_ = bf16[2,16,8,768]{3,2,1,0:T(8,128)(2,1)S(1)} collective-permute-done((bf16[2,16,8,768]{3,2,1,0:T(8,128)(2,1)}, bf16[2,16,8,768]{3,2,1,0:T(8,128)(2,1)S(1)}, u32[]{:S(2)}, u32[]{:S(2)}) %collective-permute-start.37) | collective-permute-done | bytes 393248 | tf_op jit(solution)/shard_map/ppermute | solution.py:329
  270.5 6.1 %collective-permute-done.38.refs_3_ = bf16[2,16,8,768]{3,2,1,0:T(8,128)(2,1)S(1)} collective-permute-done((bf16[2,16,8,768]{3,2,1,0:T(8,128)(2,1)}, bf16[2,16,8,768]{3,2,1,0:T(8,128)(2,1)S(1)}, u32[]{:S(2)}, u32[]{:S(2)}) %collective-permute-start.38) | collective-permute-done | bytes 393248 | tf_op jit(solution)/shard_map/ppermute | solution.py:329
  278.0 32.1 %collective-permute-done.39.refs_4_ = bf16[2,16,8,768]{3,2,1,0:T(8,128)(2,1)S(1)} collective-permute-done((bf16[2,16,8,768]{3,2,1,0:T(8,128)(2,1)}, bf16[2,16,8,768]{3,2,1,0:T(8,128)(2,1)S(1)}, u32[]{:S(2)}, u32[]{:S(2)}) %collective-permute-start.39) | collective-permute-done | bytes 393248 | tf_op jit(solution)/shard_map/ppermute | solution.py:329
  310.2 14.9 %collective-permute-done.41.refs_6_ = bf16[2,16,8,768]{3,2,1,0:T(8,128)(2,1)S(1)} collective-permute-done((bf16[2,16,8,768]{3,2,1,0:T(8,128)(2,1)}, bf16[2,16,8,768]{3,2,1,0:T(8,128)(2,1)S(1)}, u32[]{:S(2)}, u32[]{:S(2)}) %collective-permute-start.41) | collective-permute-done | bytes 393248 | tf_op jit(solution)/shard_map/ppermute | solution.py:329
  328.8 18.1 %collective-permute-start.20 = (bf16[2,16,8,768]{3,2,1,0:T(8,128)(2,1)}, bf16[2,16,8,768]{3,2,1,0:T(8,128)(2,1)S(1)}, u32[]{:S(2)}, u32[]{:S(2)}) collective-permute-start(bf16[2,16,8,768]{3,2,1,0:T(8,128)(2,1)} %get-tuple-element.51), channel_id=1, source_target_pairs={{0,16},{2,18},{4,20},{6,22},{8,24},{10,26},{12,28},{14,30},{16,0},... | collective-permute-start | bytes 1179656 | tf_op jit(solution)/shard_map/ppermute | solution.py:329
  347.0 3.5 shard_map.73.refs_6_
  350.5 18.8 %collective-permute-done.25.refs_4_ = bf16[2,16,8,768]{3,2,1,0:T(8,128)(2,1)} collective-permute-done((bf16[2,16,8,768]{3,2,1,0:T(8,128)(2,1)}, bf16[2,16,8,768]{3,2,1,0:T(8,128)(2,1)}, u32[]{:S(2)}, u32[]{:S(2)}) %collective-permute-start.25) | collective-permute-done | bytes 393248 | tf_op jit(solution)/shard_map/ppermute | solution.py:329
  369.2 2.8 shard_map.74.refs_2_
  372.1 3.6 collective-permute-done.20.refs_1_
  (204 shorter events, 94.6 us)
Async XLA Ops:
  2.0 25.6 %collective-permute-start.13 = (f32[2,512]{1,0:T(2,128)S(1)}, f32[2,512]{1,0:T(2,128)S(1)}, u32[]{:S(2)}, u32[]{:S(2)}) collective-permute-start(f32[2,512]{1,0:T(2,128)S(1)} %pad_maximum_fusion.1), channel_id=1, source_target_pairs={{0,2},{2,4},{4,6},{6,8},{8,10},{10,12},{12,14},{14,16},{16,18},{18... | collective-permute-start | bytes 12296 | tf_op jit(solution)/shard_map/ppermute | solution.py:342
  4.6 38.9 %collective-permute-start.14 = (f32[2,512]{1,0:T(2,128)S(1)}, f32[2,512]{1,0:T(2,128)S(1)}, u32[]{:S(2)}, u32[]{:S(2)}) collective-permute-start(f32[2,512]{1,0:T(2,128)S(1)} %pad_maximum_fusion.1), channel_id=1, source_target_pairs={{2,0},{4,2},{6,4},{8,6},{10,8},{12,10},{14,12},{16,14},{18,16},{20... | collective-permute-start | bytes 12296 | tf_op jit(solution)/shard_map/ppermute | solution.py:342
  5.9 22.7 %all-to-all-start = ((f32[16,1,512]{2,1,0:T(1,128)}), f32[16,1,512]{2,1,0:T(1,128)S(1)}, u32[]{:S(2)}, u32[]{:S(2)}) async-start(f32[16,1,512]{2,1,0:T(1,128)} %broadcast_in_dim.19), calls=%async_computation | async-start | bytes 65536 | tf_op jit(solution)/shard_map/all_to_all | solution.py:308
  14.2 35.9 %collective-permute-start.26 = (bf16[2,16,8,768]{3,2,1,0:T(8,128)(2,1)}, bf16[2,16,8,768]{3,2,1,0:T(8,128)(2,1)S(1)}, u32[]{:S(2)}, u32[]{:S(2)}) collective-permute-start(bf16[2,16,8,768]{3,2,1,0:T(8,128)(2,1)} %shard_map.68), channel_id=1, source_target_pairs={{0,28},{2,30},{4,24},{6,26},{8,20},{10,22},{12,16},{14,18},{16,12}... | collective-permute-start | bytes 1179656 | tf_op jit(solution)/shard_map/ppermute | solution.py:329
  21.4 30.9 %collective-permute-start.27 = (bf16[2,16,8,768]{3,2,1,0:T(8,128)(2,1)}, bf16[2,16,8,768]{3,2,1,0:T(8,128)(2,1)S(1)}, u32[]{:S(2)}, u32[]{:S(2)}) collective-permute-start(bf16[2,16,8,768]{3,2,1,0:T(8,128)(2,1)} %get-tuple-element.58), channel_id=1, source_target_pairs={{0,12},{2,14},{4,8},{6,10},{8,4},{10,6},{12,0},{14,2},{16,28},{18,... | collective-permute-start | bytes 1179656 | tf_op jit(solution)/shard_map/ppermute | solution.py:329
  21.5 31.1 %collective-permute-start.28 = (bf16[2,16,8,768]{3,2,1,0:T(8,128)(2,1)}, bf16[2,16,8,768]{3,2,1,0:T(8,128)(2,1)S(1)}, u32[]{:S(2)}, u32[]{:S(2)}) collective-permute-start(bf16[2,16,8,768]{3,2,1,0:T(8,128)(2,1)} %get-tuple-element.59), channel_id=1, source_target_pairs={{0,24},{2,26},{4,28},{6,30},{8,16},{10,18},{12,20},{14,22},{16,8},... | collective-permute-start | bytes 1179656 | tf_op jit(solution)/shard_map/ppermute | solution.py:329
  27.6 30.5 %collective-permute-start.29 = (bf16[2,16,8,768]{3,2,1,0:T(8,128)(2,1)}, bf16[2,16,8,768]{3,2,1,0:T(8,128)(2,1)S(1)}, u32[]{:S(2)}, u32[]{:S(2)}) collective-permute-start(bf16[2,16,8,768]{3,2,1,0:T(8,128)(2,1)} %get-tuple-element.60), channel_id=1, source_target_pairs={{0,8},{2,10},{4,12},{6,14},{8,0},{10,2},{12,4},{14,6},{16,24},{18,... | collective-permute-start | bytes 1179656 | tf_op jit(solution)/shard_map/ppermute | solution.py:329
  47.7 42.8 %collective-permute-start.30 = (bf16[2,16,8,768]{3,2,1,0:T(8,128)(2,1)}, bf16[2,16,8,768]{3,2,1,0:T(8,128)(2,1)S(1)}, u32[]{:S(2)}, u32[]{:S(2)}) collective-permute-start(bf16[2,16,8,768]{3,2,1,0:T(8,128)(2,1)} %get-tuple-element.61), channel_id=1, source_target_pairs={{0,20},{2,22},{4,16},{6,18},{8,28},{10,30},{12,24},{14,26},{16,4},... | collective-permute-start | bytes 1179656 | tf_op jit(solution)/shard_map/ppermute | solution.py:329
  50.1 42.1 %collective-permute-start.31 = (bf16[2,16,8,768]{3,2,1,0:T(8,128)(2,1)S(1)}, bf16[2,16,8,768]{3,2,1,0:T(8,128)(2,1)S(1)}, u32[]{:S(2)}, u32[]{:S(2)}) collective-permute-start(bf16[2,16,8,768]{3,2,1,0:T(8,128)(2,1)S(1)} %copy-done.37), channel_id=1, source_target_pairs={{0,4},{2,6},{4,0},{6,2},{8,12},{10,14},{12,8},{14,10},{16,20},{18,... | collective-permute-start | bytes 1179656 | tf_op jit(solution)/shard_map/ppermute | solution.py:329
  52.3 54.7 %collective-permute-start.32 = (bf16[2,16,8,768]{3,2,1,0:T(8,128)(2,1)}, bf16[2,16,8,768]{3,2,1,0:T(8,128)(2,1)S(1)}, u32[]{:S(2)}, u32[]{:S(2)}) collective-permute-start(bf16[2,16,8,768]{3,2,1,0:T(8,128)(2,1)} %get-tuple-element.63), channel_id=1, source_target_pairs={{0,16},{2,18},{4,20},{6,22},{8,24},{10,26},{12,28},{14,30},{16,0},... | collective-permute-start | bytes 1179656 | tf_op jit(solution)/shard_map/ppermute | solution.py:329
  53.1 54.0 %collective-permute-start = (bf16[2,16,8,768]{3,2,1,0:T(8,128)(2,1)}, bf16[2,16,8,768]{3,2,1,0:T(8,128)(2,1)S(1)}, u32[]{:S(2)}, u32[]{:S(2)}) collective-permute-start(bf16[2,16,8,768]{3,2,1,0:T(8,128)(2,1)} %get-tuple-element.40), channel_id=1, source_target_pairs={{0,28},{2,30},{4,24},{6,26},{8,20},{10,22},{12,16},{14,18},{16,12}... | collective-permute-start | bytes 1179656 | tf_op jit(solution)/shard_map/ppermute | solution.py:329
  58.2 50.3 %collective-permute-start.1 = (bf16[2,16,8,768]{3,2,1,0:T(8,128)(2,1)}, bf16[2,16,8,768]{3,2,1,0:T(8,128)(2,1)S(1)}, u32[]{:S(2)}, u32[]{:S(2)}) collective-permute-start(bf16[2,16,8,768]{3,2,1,0:T(8,128)(2,1)} %get-tuple-element.41), channel_id=1, source_target_pairs={{0,12},{2,14},{4,8},{6,10},{8,4},{10,6},{12,0},{14,2},{16,28},{18,... | collective-permute-start | bytes 1179656 | tf_op jit(solution)/shard_map/ppermute | solution.py:329
  90.6 40.8 %collective-permute-start.2 = (bf16[2,16,8,768]{3,2,1,0:T(8,128)(2,1)}, bf16[2,16,8,768]{3,2,1,0:T(8,128)(2,1)S(1)}, u32[]{:S(2)}, u32[]{:S(2)}) collective-permute-start(bf16[2,16,8,768]{3,2,1,0:T(8,128)(2,1)} %get-tuple-element.42), channel_id=1, source_target_pairs={{0,24},{2,26},{4,28},{6,30},{8,16},{10,18},{12,20},{14,22},{16,8},... | collective-permute-start | bytes 1179656 | tf_op jit(solution)/shard_map/ppermute | solution.py:329
  92.2 52.6 %collective-permute-start.3 = (bf16[2,16,8,768]{3,2,1,0:T(8,128)(2,1)}, bf16[2,16,8,768]{3,2,1,0:T(8,128)(2,1)S(1)}, u32[]{:S(2)}, u32[]{:S(2)}) collective-permute-start(bf16[2,16,8,768]{3,2,1,0:T(8,128)(2,1)} %get-tuple-element.43), channel_id=1, source_target_pairs={{0,8},{2,10},{4,12},{6,14},{8,0},{10,2},{12,4},{14,6},{16,24},{18,... | collective-permute-start | bytes 1179656 | tf_op jit(solution)/shard_map/ppermute | solution.py:329
  94.0 50.9 %all-to-all-start.1 = ((bf16[16,16,256]{2,1,0:T(8,128)(2,1)}), bf16[16,16,256]{2,1,0:T(8,128)(2,1)S(1)}, u32[]{:S(2)}, u32[]{:S(2)}) async-start(bf16[16,16,256]{2,1,0:T(8,128)(2,1)} %fusion.23), calls=%async_computation.1 | async-start | bytes 262144 | tf_op jit(solution)/shard_map/all_to_all | solution.py:308
  107.1 45.3 %collective-permute-start.4 = (bf16[2,16,8,768]{3,2,1,0:T(8,128)(2,1)}, bf16[2,16,8,768]{3,2,1,0:T(8,128)(2,1)S(1)}, u32[]{:S(2)}, u32[]{:S(2)}) collective-permute-start(bf16[2,16,8,768]{3,2,1,0:T(8,128)(2,1)} %get-tuple-element.44), channel_id=1, source_target_pairs={{0,20},{2,22},{4,16},{6,18},{8,28},{10,30},{12,24},{14,26},{16,4},... | collective-permute-start | bytes 1179656 | tf_op jit(solution)/shard_map/ppermute | solution.py:329
  107.8 48.1 %collective-permute-start.5 = (bf16[2,16,8,768]{3,2,1,0:T(8,128)(2,1)}, bf16[2,16,8,768]{3,2,1,0:T(8,128)(2,1)S(1)}, u32[]{:S(2)}, u32[]{:S(2)}) collective-permute-start(bf16[2,16,8,768]{3,2,1,0:T(8,128)(2,1)} %get-tuple-element.45), channel_id=1, source_target_pairs={{0,4},{2,6},{4,0},{6,2},{8,12},{10,14},{12,8},{14,10},{16,20},{18,... | collective-permute-start | bytes 1179656 | tf_op jit(solution)/shard_map/ppermute | solution.py:329
  108.5 52.0 %collective-permute-start.6 = (bf16[2,16,8,768]{3,2,1,0:T(8,128)(2,1)}, bf16[2,16,8,768]{3,2,1,0:T(8,128)(2,1)S(1)}, u32[]{:S(2)}, u32[]{:S(2)}) collective-permute-start(bf16[2,16,8,768]{3,2,1,0:T(8,128)(2,1)} %get-tuple-element.46), channel_id=1, source_target_pairs={{0,16},{2,18},{4,20},{6,22},{8,24},{10,26},{12,28},{14,30},{16,0},... | collective-permute-start | bytes 1179656 | tf_op jit(solution)/shard_map/ppermute | solution.py:329
  152.4 49.7 %collective-permute-start.33 = (bf16[8,16,8,768]{3,2,1,0:T(8,128)(2,1)}, bf16[8,16,8,768]{3,2,1,0:T(8,128)(2,1)}, u32[]{:S(2)}, u32[]{:S(2)}) collective-permute-start(bf16[8,16,8,768]{3,2,1,0:T(8,128)(2,1)} %shard_map.70), channel_id=1, source_target_pairs={{0,2},{2,0},{4,6},{6,4},{8,10},{10,8},{12,14},{14,12},{16,18},{18,... | collective-permute-start | bytes 4718600 | tf_op jit(solution)/shard_map/ppermute | solution.py:332
  163.7 54.2 %collective-permute-start.7 = (bf16[8,16,8,768]{3,2,1,0:T(8,128)(2,1)}, bf16[8,16,8,768]{3,2,1,0:T(8,128)(2,1)S(1)}, u32[]{:S(2)}, u32[]{:S(2)}) collective-permute-start(bf16[8,16,8,768]{3,2,1,0:T(8,128)(2,1)} %shard_map.65), channel_id=1, source_target_pairs={{0,2},{2,0},{4,6},{6,4},{8,10},{10,8},{12,14},{14,12},{16,18},{18,... | collective-permute-start | bytes 4718600 | tf_op jit(solution)/shard_map/ppermute | solution.py:332
  237.8 32.7 %collective-permute-start.37 = (bf16[2,16,8,768]{3,2,1,0:T(8,128)(2,1)}, bf16[2,16,8,768]{3,2,1,0:T(8,128)(2,1)S(1)}, u32[]{:S(2)}, u32[]{:S(2)}) collective-permute-start(bf16[2,16,8,768]{3,2,1,0:T(8,128)(2,1)} %get-tuple-element.69), channel_id=1, source_target_pairs={{0,24},{2,26},{4,28},{6,30},{8,16},{10,18},{12,20},{14,22},{16,8},... | collective-permute-start | bytes 1179656 | tf_op jit(solution)/shard_map/ppermute | solution.py:329
  239.5 37.1 %collective-permute-start.38 = (bf16[2,16,8,768]{3,2,1,0:T(8,128)(2,1)}, bf16[2,16,8,768]{3,2,1,0:T(8,128)(2,1)S(1)}, u32[]{:S(2)}, u32[]{:S(2)}) collective-permute-start(bf16[2,16,8,768]{3,2,1,0:T(8,128)(2,1)} %get-tuple-element.70), channel_id=1, source_target_pairs={{0,8},{2,10},{4,12},{6,14},{8,0},{10,2},{12,4},{14,6},{16,24},{18,... | collective-permute-start | bytes 1179656 | tf_op jit(solution)/shard_map/ppermute | solution.py:329
  242.4 67.7 %collective-permute-start.39 = (bf16[2,16,8,768]{3,2,1,0:T(8,128)(2,1)}, bf16[2,16,8,768]{3,2,1,0:T(8,128)(2,1)S(1)}, u32[]{:S(2)}, u32[]{:S(2)}) collective-permute-start(bf16[2,16,8,768]{3,2,1,0:T(8,128)(2,1)} %get-tuple-element.71), channel_id=1, source_target_pairs={{0,20},{2,22},{4,16},{6,18},{8,28},{10,30},{12,24},{14,26},{16,4},... | collective-permute-start | bytes 1179656 | tf_op jit(solution)/shard_map/ppermute | solution.py:329
  251.3 58.8 %collective-permute-start.40 = (bf16[2,16,8,768]{3,2,1,0:T(8,128)(2,1)}, bf16[2,16,8,768]{3,2,1,0:T(8,128)(2,1)S(1)}, u32[]{:S(2)}, u32[]{:S(2)}) collective-permute-start(bf16[2,16,8,768]{3,2,1,0:T(8,128)(2,1)} %get-tuple-element.72), channel_id=1, source_target_pairs={{0,4},{2,6},{4,0},{6,2},{8,12},{10,14},{12,8},{14,10},{16,20},{18,... | collective-permute-start | bytes 1179656 | tf_op jit(solution)/shard_map/ppermute | solution.py:329
  259.8 65.4 %collective-permute-start.41 = (bf16[2,16,8,768]{3,2,1,0:T(8,128)(2,1)}, bf16[2,16,8,768]{3,2,1,0:T(8,128)(2,1)S(1)}, u32[]{:S(2)}, u32[]{:S(2)}) collective-permute-start(bf16[2,16,8,768]{3,2,1,0:T(8,128)(2,1)} %get-tuple-element.73), channel_id=1, source_target_pairs={{0,16},{2,18},{4,20},{6,22},{8,24},{10,26},{12,28},{14,30},{16,0},... | collective-permute-start | bytes 1179656 | tf_op jit(solution)/shard_map/ppermute | solution.py:329
  270.5 55.8 %collective-permute-start.21 = (bf16[2,16,8,768]{3,2,1,0:T(8,128)(2,1)}, bf16[2,16,8,768]{3,2,1,0:T(8,128)(2,1)S(1)}, u32[]{:S(2)}, u32[]{:S(2)}) collective-permute-start(bf16[2,16,8,768]{3,2,1,0:T(8,128)(2,1)} %get-tuple-element.52), channel_id=1, source_target_pairs={{0,28},{2,30},{4,24},{6,26},{8,20},{10,22},{12,16},{14,18},{16,12}... | collective-permute-start | bytes 1179656 | tf_op jit(solution)/shard_map/ppermute | solution.py:329
  276.6 51.4 %collective-permute-start.22 = (bf16[2,16,8,768]{3,2,1,0:T(8,128)(2,1)}, bf16[2,16,8,768]{3,2,1,0:T(8,128)(2,1)S(1)}, u32[]{:S(2)}, u32[]{:S(2)}) collective-permute-start(bf16[2,16,8,768]{3,2,1,0:T(8,128)(2,1)} %get-tuple-element.53), channel_id=1, source_target_pairs={{0,12},{2,14},{4,8},{6,10},{8,4},{10,6},{12,0},{14,2},{16,28},{18,... | collective-permute-start | bytes 1179656 | tf_op jit(solution)/shard_map/ppermute | solution.py:329
  310.1 40.4 %collective-permute-start.23 = (bf16[2,16,8,768]{3,2,1,0:T(8,128)(2,1)}, bf16[2,16,8,768]{3,2,1,0:T(8,128)(2,1)}, u32[]{:S(2)}, u32[]{:S(2)}) collective-permute-start(bf16[2,16,8,768]{3,2,1,0:T(8,128)(2,1)} %get-tuple-element.54), channel_id=1, source_target_pairs={{0,24},{2,26},{4,28},{6,30},{8,16},{10,18},{12,20},{14,22},{16,8},... | collective-permute-start | bytes 1179656 | tf_op jit(solution)/shard_map/ppermute | solution.py:329
  310.1 40.4 %collective-permute-start.24 = (bf16[2,16,8,768]{3,2,1,0:T(8,128)(2,1)}, bf16[2,16,8,768]{3,2,1,0:T(8,128)(2,1)}, u32[]{:S(2)}, u32[]{:S(2)}) collective-permute-start(bf16[2,16,8,768]{3,2,1,0:T(8,128)(2,1)} %get-tuple-element.55), channel_id=1, source_target_pairs={{0,8},{2,10},{4,12},{6,14},{8,0},{10,2},{12,4},{14,6},{16,24},{18,... | collective-permute-start | bytes 1179656 | tf_op jit(solution)/shard_map/ppermute | solution.py:329
  325.1 44.1 %collective-permute-start.25 = (bf16[2,16,8,768]{3,2,1,0:T(8,128)(2,1)}, bf16[2,16,8,768]{3,2,1,0:T(8,128)(2,1)}, u32[]{:S(2)}, u32[]{:S(2)}) collective-permute-start(bf16[2,16,8,768]{3,2,1,0:T(8,128)(2,1)} %get-tuple-element.56), channel_id=1, source_target_pairs={{0,20},{2,22},{4,16},{6,18},{8,28},{10,30},{12,24},{14,26},{16,4},... | collective-permute-start | bytes 1179656 | tf_op jit(solution)/shard_map/ppermute | solution.py:329
  327.1 44.9 %collective-permute-start.19 = (bf16[2,16,8,768]{3,2,1,0:T(8,128)(2,1)}, bf16[2,16,8,768]{3,2,1,0:T(8,128)(2,1)S(1)}, u32[]{:S(2)}, u32[]{:S(2)}) collective-permute-start(bf16[2,16,8,768]{3,2,1,0:T(8,128)(2,1)} %get-tuple-element.50), channel_id=1, source_target_pairs={{0,4},{2,6},{4,0},{6,2},{8,12},{10,14},{12,8},{14,10},{16,20},{18,... | collective-permute-start | bytes 1179656 | tf_op jit(solution)/shard_map/ppermute | solution.py:329
  328.8 46.8 %collective-permute-start.20 = (bf16[2,16,8,768]{3,2,1,0:T(8,128)(2,1)}, bf16[2,16,8,768]{3,2,1,0:T(8,128)(2,1)S(1)}, u32[]{:S(2)}, u32[]{:S(2)}) collective-permute-start(bf16[2,16,8,768]{3,2,1,0:T(8,128)(2,1)} %get-tuple-element.51), channel_id=1, source_target_pairs={{0,16},{2,18},{4,20},{6,22},{8,24},{10,26},{12,28},{14,30},{16,0},... | collective-permute-start | bytes 1179656 | tf_op jit(solution)/shard_map/ppermute | solution.py:329
  (50 other events, 938.7 us)

commit v4 on v3

--- a/solution.py
+++ b/solution.py
@@ -210,8 +210,8 @@
     for k in range(share):
         matrices[1 + rank * share + k] = own_ref[k]
         matrices[1 + (1 - rank) * share + k] = opposite_ref[k]
-    for k, edge in zip((0, 2 * share + 1), edges):
-        matrices[k] = edge[0]
+    for k, edge in enumerate(edges):
+        matrices[((1 - rank) ^ k) * (2 * share + 1)] = edge[0]
     _, members, tiers, cells = other_ref.shape
     total = chips * 2 * members
     rows = members * tiers
@@ -377,11 +377,14 @@
     )
     weights = ensemble_weights(gram_matrix, right_side)
     opposite = lax.ppermute(weights, "level", flip)
-    before = lax.ppermute(jnp.where(tier_rank == 0, opposite, weights)[-1:], "region", up)
-    beyond = lax.ppermute(jnp.where(tier_rank == 0, weights, opposite)[:1], "region", down)
+    pairs = [(r * levels, (r - 1) % regions * levels) for r in range(regions)]
+    pairs += [(r * levels - 1, ((r % regions) + 1) * levels - 1) for r in range(1, regions + 1)]
+    edge = lax.dynamic_slice_in_dim(weights, tier_rank * (share - 1), 1, axis=0)
+    edge = lax.ppermute(edge, ("region", "level"), pairs)
+    edges = [edge, lax.ppermute(edge, "level", flip)]
 
     analysis = None
-    early_count = -(-2 * (chips - 1) // 7)
+    early_count = -(-(chips - 1) // 7)
     for half in range(HALVES):
         early = -(-(chips - 1) // 7) if half == 0 else 0
         pieces = []
@@ -391,8 +394,7 @@
         pieces = [swap(block, rank) for rank, block in enumerate(pieces)]
         other = hand(pieces)
         other = swap_core(other)
-        edges = [] if half == 0 else [before, beyond]
-        keep, give = transform(half, pieces, other, weights, opposite, edges)
+        keep, give = transform(half, pieces, other, weights, opposite, edges if half else [])
         got = swap_core(give)
         blocks = pack(keep, got)
         blocks = [swap(block, rank) for rank, block in enumerate(blocks)]

time: 381 us -> 381 us (level)
    ppermute x28, starting transfers between devices: 65.6 us -> 72.5 us  [swap(): return lax.ppermute(block, 'region', pairs)]
    ppermute x2, waiting for transfers between devices: 2.33 us -> 7.77 us  [the longest x1 4.58 us: analyse(): edge = lax.ppermute(edge, ('region', 'level'), pairs)]
    ppermute x28, waiting for transfers between devices: 141 us -> 137 us  [swap(): return lax.ppermute(block, 'region', pairs)]
    unnamed x80 -> x76, local copies, waits for them, and re-layouts: 11.6 us -> 8.45 us
  transfers between devices with their start and end apart: 44 -> 44, of which waited for: 19 -> 20; matrix products, arithmetic and copies ran while one was open for 9% -> 8% of each run, Pallas kernels for 14% -> 14%
where the time goes in v4:
time: 381 us; the launch traced here: 379 us
  waiting for transfers between devices  175 us (46%)
  starting transfers between devices  105 us (28%)
  Pallas kernels  56.5 us (15%)
  other arithmetic  15.1 us (4%)
  matrix products  14.7 us (4%)
  local copies, waits for them, and re-layouts  10.3 us (3%)
    ppermute x28, waiting for transfers between devices, swap(): return lax.ppermute(block, 'region', pairs)  137 us
    ppermute x28, starting transfers between devices, swap(): return lax.ppermute(block, 'region', pairs)  72.5 us
    pallas_call x10, Pallas kernels, moved(): pl.pallas_call(kernel, in_specs=[anywhere] * len(operands), out_specs=[an...  28.5 us
    pallas_call x2, Pallas kernels, transform(): pl.pallas_call(functools.partial(transform_kernel, first, chips), grid=(1...  15 us
    all_to_all x2, waiting for transfers between devices, spread(): lax.all_to_all(block, 'region', split_axis=0, concat_axis=0, tiled=True)  13.4 us
    pallas_call x1, Pallas kernels, gather_observed(): pl.pallas_call(gather_kernel, grid=(regions,), in_specs=[pl.BlockSpec((1,...  13.1 us
    all_to_all x2, starting transfers between devices, spread(): lax.all_to_all(block, 'region', split_axis=0, concat_axis=0, tiled=True)  13 us
    ppermute x4, starting transfers between devices, swap_core(): return lax.ppermute(block, 'region', [(i, i ^ 1) for i in range(regions)])  10.1 us
  transfers between devices with their start and end apart: 44, of which 20 were waited for; matrix products, arithmetic and copies ran while one was open for 8% of the time, Pallas kernels for 14%

profile of v4, /device:TPU:1, one launch (start us, length us, event | category | flops | bytes accessed | tf_op | source)
XLA Modules:
  0.0 378.9 jit_solution(12110138495724931334)
XLA Ops:
  5.9 6.5 %all-to-all-start = ((f32[16,1,512]{2,1,0:T(1,128)}), f32[16,1,512]{2,1,0:T(1,128)S(1)}, u32[]{:S(2)}, u32[]{:S(2)}) async-start(f32[16,1,512]{2,1,0:T(1,128)} %broadcast_in_dim.19), calls=%async_computation | async-start | bytes 65536 | tf_op jit(solution)/shard_map/all_to_all | solution.py:308
  14.2 4.1 %collective-permute-start.26 = (bf16[2,16,8,768]{3,2,1,0:T(8,128)(2,1)}, bf16[2,16,8,768]{3,2,1,0:T(8,128)(2,1)S(1)}, u32[]{:S(2)}, u32[]{:S(2)}) collective-permute-start(bf16[2,16,8,768]{3,2,1,0:T(8,128)(2,1)} %shard_map.68), channel_id=1, source_target_pairs={{0,28},{2,30},{4,24},{6,26},{8,20},{10,22},{12,16},{14,18},{16,12}... | collective-permute-start | bytes 1179656 | tf_op jit(solution)/shard_map/ppermute | solution.py:329
  18.3 3.1 shard_map.69
  23.4 3.5 shard_map.64
  29.5 13.1 %gather_observed.1 = bf16[2,16,16,256]{3,2,1,0:T(8,128)(2,1)} custom-call(s32[16,1,512]{2,1,0:T(1,128)} %get-tuple-element.91.cell_ref, s32[16,1,512]{2,1,0:T(1,128)} %get-tuple-element.90.level_ref, bf16[16,8,24576]{2,1,0:T(8,128)(2,1)} %prior_ref.5), custom_call_target="tpu_custom_call" | custom-call | tf_op jit(solution)/shard_map/gather_observed/pallas_call | solution.py:61
  60.4 30.2 %collective-permute-done.30.refs_4_ = bf16[2,16,8,768]{3,2,1,0:T(8,128)(2,1)S(1)} collective-permute-done((bf16[2,16,8,768]{3,2,1,0:T(8,128)(2,1)}, bf16[2,16,8,768]{3,2,1,0:T(8,128)(2,1)S(1)}, u32[]{:S(2)}, u32[]{:S(2)}) %collective-permute-start.30) | collective-permute-done | bytes 393248 | tf_op jit(solution)/shard_map/ppermute | solution.py:329
  94.0 6.6 %all-to-all-start.1 = ((bf16[16,16,256]{2,1,0:T(8,128)(2,1)}), bf16[16,16,256]{2,1,0:T(8,128)(2,1)S(1)}, u32[]{:S(2)}, u32[]{:S(2)}) async-start(bf16[16,16,256]{2,1,0:T(8,128)(2,1)} %fusion.22), calls=%async_computation.1 | async-start | bytes 262144 | tf_op jit(solution)/shard_map/all_to_all | solution.py:308
  100.5 6.6 %collective-permute-done.32.refs_6_ = bf16[2,16,8,768]{3,2,1,0:T(8,128)(2,1)S(1)} collective-permute-done((bf16[2,16,8,768]{3,2,1,0:T(8,128)(2,1)}, bf16[2,16,8,768]{3,2,1,0:T(8,128)(2,1)S(1)}, u32[]{:S(2)}, u32[]{:S(2)}) %collective-permute-start.32) | collective-permute-done | bytes 393248 | tf_op jit(solution)/shard_map/ppermute | solution.py:329
  108.5 19.1 %collective-permute-start.6 = (bf16[2,16,8,768]{3,2,1,0:T(8,128)(2,1)}, bf16[2,16,8,768]{3,2,1,0:T(8,128)(2,1)S(1)}, u32[]{:S(2)}, u32[]{:S(2)}) collective-permute-start(bf16[2,16,8,768]{3,2,1,0:T(8,128)(2,1)} %get-tuple-element.46), channel_id=1, source_target_pairs={{0,16},{2,18},{4,20},{6,22},{8,24},{10,26},{12,28},{14,30},{16,0},... | collective-permute-start | bytes 1179656 | tf_op jit(solution)/shard_map/ppermute | solution.py:329
  131.5 13.4 %all-to-all-done.1 = bf16[16,16,256]{2,1,0:T(8,128)(2,1)S(1)} async-done(((bf16[16,16,256]{2,1,0:T(8,128)(2,1)}), bf16[16,16,256]{2,1,0:T(8,128)(2,1)S(1)}, u32[]{:S(2)}, u32[]{:S(2)}) %all-to-all-start.1) | async-done | bytes 131104 | tf_op jit(solution)/shard_map/all_to_all | solution.py:308
  152.4 3.5 collective-permute-start.33
  155.9 4.6 %collective-permute-done.6.refs_6_ = bf16[2,16,8,768]{3,2,1,0:T(8,128)(2,1)S(1)} collective-permute-done((bf16[2,16,8,768]{3,2,1,0:T(8,128)(2,1)}, bf16[2,16,8,768]{3,2,1,0:T(8,128)(2,1)S(1)}, u32[]{:S(2)}, u32[]{:S(2)}) %collective-permute-start.6) | collective-permute-done | bytes 393248 | tf_op jit(solution)/shard_map/ppermute | solution.py:329
  170.1 5.6 %collective-permute-done.12 = bf16[256,512]{1,0:T(8,128)(2,1)S(1)} collective-permute-done((bf16[256,512]{1,0:T(8,128)(2,1)S(1)}, bf16[256,512]{1,0:T(8,128)(2,1)S(1)}, u32[]{:S(2)}, u32[]{:S(2)}) %collective-permute-start.12) | collective-permute-done | bytes 262176 | tf_op jit(solution)/shard_map/ppermute | solution.py:359
  193.9 8.3 %collective-permute-done.15.refs_10_ = bf16[3,256,256]{2,1,0:T(8,128)(2,1)S(1)} collective-permute-done((bf16[3,256,256]{2,1,0:T(8,128)(2,1)S(1)}, bf16[3,256,256]{2,1,0:T(8,128)(2,1)S(1)}, u32[]{:S(2)}, u32[]{:S(2)}) %collective-permute-start.15) | collective-permute-done | bytes 393248 | tf_op jit(solution)/shard_map/ppermute | solution.py:379
  202.9 7.5 %shard_map.71 = (bf16[8,16,8,768]{3,2,1,0:T(8,128)(2,1)}, bf16[8,16,8,768]{3,2,1,0:T(8,128)(2,1)}) custom-call(bf16[2,16,8,768]{3,2,1,0:T(8,128)(2,1)} %copy-done.10, bf16[2,16,8,768]{3,2,1,0:T(8,128)(2,1)} %copy-done.11, bf16[2,16,8,768]{3,2,1,0:T(8,128)(2,1)} %copy-done.12, bf16[2,16,8,768]{3,2,1,0:T(8,128)(2,1)} %copy-done.13, ...), custom_call_target="tpu_custom_call" | custom-call | tf_op jit(solution)/shard_map/pallas_call | solution.py:258
  212.7 4.6 %collective-permute-done.16.refs_11_ = bf16[1,256,256]{2,1,0:T(8,128)(2,1)S(1)} collective-permute-done((bf16[1,256,256]{2,1,0:T(8,128)(2,1)S(1)}, bf16[1,256,256]{2,1,0:T(8,128)(2,1)S(1)}, u32[]{:S(2)}, u32[]{:S(2)}) %collective-permute-start.16) | collective-permute-done | bytes 131104 | tf_op jit(solution)/shard_map/ppermute | solution.py:383
  217.9 3.2 collective-permute-done.17.refs_12_
  221.7 7.5 %shard_map.66 = (bf16[8,16,8,768]{3,2,1,0:T(8,128)(2,1)}, bf16[8,16,8,768]{3,2,1,0:T(8,128)(2,1)}) custom-call(bf16[2,16,8,768]{3,2,1,0:T(8,128)(2,1)} %copy-done.1, bf16[2,16,8,768]{3,2,1,0:T(8,128)(2,1)} %copy-done.2, bf16[2,16,8,768]{3,2,1,0:T(8,128)(2,1)} %copy-done.3, bf16[2,16,8,768]{3,2,1,0:T(8,128)(2,1)} %copy-done.4, ...), custom_call_target="tpu_custom_call" | custom-call | tf_op jit(solution)/shard_map/pallas_call | solution.py:258
  229.3 3.4 collective-permute-start.18
  233.8 3.5 shard_map.72
  243.7 3.5 shard_map.67
  247.2 3.9 %collective-permute-done.35.refs_0_ = bf16[2,16,8,768]{3,2,1,0:T(8,128)(2,1)S(1)} collective-permute-done((bf16[2,16,8,768]{3,2,1,0:T(8,128)(2,1)}, bf16[2,16,8,768]{3,2,1,0:T(8,128)(2,1)S(1)}, u32[]{:S(2)}, u32[]{:S(2)}) %collective-permute-start.35) | collective-permute-done | bytes 393248 | tf_op jit(solution)/shard_map/ppermute | solution.py:329
  251.0 9.6 %collective-permute-done.36.refs_1_ = bf16[2,16,8,768]{3,2,1,0:T(8,128)(2,1)S(1)} collective-permute-done((bf16[2,16,8,768]{3,2,1,0:T(8,128)(2,1)}, bf16[2,16,8,768]{3,2,1,0:T(8,128)(2,1)S(1)}, u32[]{:S(2)}, u32[]{:S(2)}) %collective-permute-start.36) | collective-permute-done | bytes 393248 | tf_op jit(solution)/shard_map/ppermute | solution.py:329
  263.3 7.0 %collective-permute-done.37.refs_2_ = bf16[2,16,8,768]{3,2,1,0:T(8,128)(2,1)S(1)} collective-permute-done((bf16[2,16,8,768]{3,2,1,0:T(8,128)(2,1)}, bf16[2,16,8,768]{3,2,1,0:T(8,128)(2,1)S(1)}, u32[]{:S(2)}, u32[]{:S(2)}) %collective-permute-start.37) | collective-permute-done | bytes 393248 | tf_op jit(solution)/shard_map/ppermute | solution.py:329
  270.3 4.6 %collective-permute-start.20 = (bf16[2,16,8,768]{3,2,1,0:T(8,128)(2,1)}, bf16[2,16,8,768]{3,2,1,0:T(8,128)(2,1)S(1)}, u32[]{:S(2)}, u32[]{:S(2)}) collective-permute-start(bf16[2,16,8,768]{3,2,1,0:T(8,128)(2,1)} %get-tuple-element.51), channel_id=1, source_target_pairs={{0,28},{2,30},{4,24},{6,26},{8,20},{10,22},{12,16},{14,18},{16,12}... | collective-permute-start | bytes 1179656 | tf_op jit(solution)/shard_map/ppermute | solution.py:329
  277.5 4.1 %collective-permute-start.21 = (bf16[2,16,8,768]{3,2,1,0:T(8,128)(2,1)}, bf16[2,16,8,768]{3,2,1,0:T(8,128)(2,1)S(1)}, u32[]{:S(2)}, u32[]{:S(2)}) collective-permute-start(bf16[2,16,8,768]{3,2,1,0:T(8,128)(2,1)} %get-tuple-element.52), channel_id=1, source_target_pairs={{0,12},{2,14},{4,8},{6,10},{8,4},{10,6},{12,0},{14,2},{16,28},{18,... | collective-permute-start | bytes 1179656 | tf_op jit(solution)/shard_map/ppermute | solution.py:329
  281.6 29.4 %collective-permute-done.39.refs_4_ = bf16[2,16,8,768]{3,2,1,0:T(8,128)(2,1)S(1)} collective-permute-done((bf16[2,16,8,768]{3,2,1,0:T(8,128)(2,1)}, bf16[2,16,8,768]{3,2,1,0:T(8,128)(2,1)S(1)}, u32[]{:S(2)}, u32[]{:S(2)}) %collective-permute-start.39) | collective-permute-done | bytes 393248 | tf_op jit(solution)/shard_map/ppermute | solution.py:329
  311.0 14.5 %collective-permute-done.41.refs_6_ = bf16[2,16,8,768]{3,2,1,0:T(8,128)(2,1)S(1)} collective-permute-done((bf16[2,16,8,768]{3,2,1,0:T(8,128)(2,1)}, bf16[2,16,8,768]{3,2,1,0:T(8,128)(2,1)S(1)}, u32[]{:S(2)}, u32[]{:S(2)}) %collective-permute-start.41) | collective-permute-done | bytes 393248 | tf_op jit(solution)/shard_map/ppermute | solution.py:329
  328.9 16.1 %collective-permute-start.19 = (bf16[2,16,8,768]{3,2,1,0:T(8,128)(2,1)}, bf16[2,16,8,768]{3,2,1,0:T(8,128)(2,1)S(1)}, u32[]{:S(2)}, u32[]{:S(2)}) collective-permute-start(bf16[2,16,8,768]{3,2,1,0:T(8,128)(2,1)} %get-tuple-element.50), channel_id=1, source_target_pairs={{0,16},{2,18},{4,20},{6,22},{8,24},{10,26},{12,28},{14,30},{16,0},... | collective-permute-start | bytes 1179656 | tf_op jit(solution)/shard_map/ppermute | solution.py:329
  345.1 3.5 shard_map.73.refs_7_
  348.6 21.5 %collective-permute-done.24.refs_4_ = bf16[2,16,8,768]{3,2,1,0:T(8,128)(2,1)} collective-permute-done((bf16[2,16,8,768]{3,2,1,0:T(8,128)(2,1)}, bf16[2,16,8,768]{3,2,1,0:T(8,128)(2,1)}, u32[]{:S(2)}, u32[]{:S(2)}) %collective-permute-start.24) | collective-permute-done | bytes 393248 | tf_op jit(solution)/shard_map/ppermute | solution.py:329
  373.1 3.1 collective-permute-done.19.refs_0_
  (201 shorter events, 98.6 us)
Async XLA Ops:
  2.0 25.6 %collective-permute-start.13 = (f32[2,512]{1,0:T(2,128)S(1)}, f32[2,512]{1,0:T(2,128)S(1)}, u32[]{:S(2)}, u32[]{:S(2)}) collective-permute-start(f32[2,512]{1,0:T(2,128)S(1)} %pad_maximum_fusion.1), channel_id=1, source_target_pairs={{0,2},{2,4},{4,6},{6,8},{8,10},{10,12},{12,14},{14,16},{16,18},{18... | collective-permute-start | bytes 12296 | tf_op jit(solution)/shard_map/ppermute | solution.py:342
  4.6 38.9 %collective-permute-start.14 = (f32[2,512]{1,0:T(2,128)S(1)}, f32[2,512]{1,0:T(2,128)S(1)}, u32[]{:S(2)}, u32[]{:S(2)}) collective-permute-start(f32[2,512]{1,0:T(2,128)S(1)} %pad_maximum_fusion.1), channel_id=1, source_target_pairs={{2,0},{4,2},{6,4},{8,6},{10,8},{12,10},{14,12},{16,14},{18,16},{20... | collective-permute-start | bytes 12296 | tf_op jit(solution)/shard_map/ppermute | solution.py:342
  5.9 22.7 %all-to-all-start = ((f32[16,1,512]{2,1,0:T(1,128)}), f32[16,1,512]{2,1,0:T(1,128)S(1)}, u32[]{:S(2)}, u32[]{:S(2)}) async-start(f32[16,1,512]{2,1,0:T(1,128)} %broadcast_in_dim.19), calls=%async_computation | async-start | bytes 65536 | tf_op jit(solution)/shard_map/all_to_all | solution.py:308
  14.2 35.9 %collective-permute-start.26 = (bf16[2,16,8,768]{3,2,1,0:T(8,128)(2,1)}, bf16[2,16,8,768]{3,2,1,0:T(8,128)(2,1)S(1)}, u32[]{:S(2)}, u32[]{:S(2)}) collective-permute-start(bf16[2,16,8,768]{3,2,1,0:T(8,128)(2,1)} %shard_map.68), channel_id=1, source_target_pairs={{0,28},{2,30},{4,24},{6,26},{8,20},{10,22},{12,16},{14,18},{16,12}... | collective-permute-start | bytes 1179656 | tf_op jit(solution)/shard_map/ppermute | solution.py:329
  21.4 30.9 %collective-permute-start.27 = (bf16[2,16,8,768]{3,2,1,0:T(8,128)(2,1)}, bf16[2,16,8,768]{3,2,1,0:T(8,128)(2,1)S(1)}, u32[]{:S(2)}, u32[]{:S(2)}) collective-permute-start(bf16[2,16,8,768]{3,2,1,0:T(8,128)(2,1)} %get-tuple-element.58), channel_id=1, source_target_pairs={{0,12},{2,14},{4,8},{6,10},{8,4},{10,6},{12,0},{14,2},{16,28},{18,... | collective-permute-start | bytes 1179656 | tf_op jit(solution)/shard_map/ppermute | solution.py:329
  21.5 31.1 %collective-permute-start.28 = (bf16[2,16,8,768]{3,2,1,0:T(8,128)(2,1)}, bf16[2,16,8,768]{3,2,1,0:T(8,128)(2,1)S(1)}, u32[]{:S(2)}, u32[]{:S(2)}) collective-permute-start(bf16[2,16,8,768]{3,2,1,0:T(8,128)(2,1)} %get-tuple-element.59), channel_id=1, source_target_pairs={{0,24},{2,26},{4,28},{6,30},{8,16},{10,18},{12,20},{14,22},{16,8},... | collective-permute-start | bytes 1179656 | tf_op jit(solution)/shard_map/ppermute | solution.py:329
  27.6 30.6 %collective-permute-start.29 = (bf16[2,16,8,768]{3,2,1,0:T(8,128)(2,1)}, bf16[2,16,8,768]{3,2,1,0:T(8,128)(2,1)S(1)}, u32[]{:S(2)}, u32[]{:S(2)}) collective-permute-start(bf16[2,16,8,768]{3,2,1,0:T(8,128)(2,1)} %get-tuple-element.60), channel_id=1, source_target_pairs={{0,8},{2,10},{4,12},{6,14},{8,0},{10,2},{12,4},{14,6},{16,24},{18,... | collective-permute-start | bytes 1179656 | tf_op jit(solution)/shard_map/ppermute | solution.py:329
  47.7 42.9 %collective-permute-start.30 = (bf16[2,16,8,768]{3,2,1,0:T(8,128)(2,1)}, bf16[2,16,8,768]{3,2,1,0:T(8,128)(2,1)S(1)}, u32[]{:S(2)}, u32[]{:S(2)}) collective-permute-start(bf16[2,16,8,768]{3,2,1,0:T(8,128)(2,1)} %get-tuple-element.61), channel_id=1, source_target_pairs={{0,20},{2,22},{4,16},{6,18},{8,28},{10,30},{12,24},{14,26},{16,4},... | collective-permute-start | bytes 1179656 | tf_op jit(solution)/shard_map/ppermute | solution.py:329
  50.1 42.1 %collective-permute-start.31 = (bf16[2,16,8,768]{3,2,1,0:T(8,128)(2,1)S(1)}, bf16[2,16,8,768]{3,2,1,0:T(8,128)(2,1)S(1)}, u32[]{:S(2)}, u32[]{:S(2)}) collective-permute-start(bf16[2,16,8,768]{3,2,1,0:T(8,128)(2,1)S(1)} %copy-done.35), channel_id=1, source_target_pairs={{0,4},{2,6},{4,0},{6,2},{8,12},{10,14},{12,8},{14,10},{16,20},{18,... | collective-permute-start | bytes 1179656 | tf_op jit(solution)/shard_map/ppermute | solution.py:329
  52.3 54.8 %collective-permute-start.32 = (bf16[2,16,8,768]{3,2,1,0:T(8,128)(2,1)}, bf16[2,16,8,768]{3,2,1,0:T(8,128)(2,1)S(1)}, u32[]{:S(2)}, u32[]{:S(2)}) collective-permute-start(bf16[2,16,8,768]{3,2,1,0:T(8,128)(2,1)} %get-tuple-element.63), channel_id=1, source_target_pairs={{0,16},{2,18},{4,20},{6,22},{8,24},{10,26},{12,28},{14,30},{16,0},... | collective-permute-start | bytes 1179656 | tf_op jit(solution)/shard_map/ppermute | solution.py:329
  53.1 54.0 %collective-permute-start = (bf16[2,16,8,768]{3,2,1,0:T(8,128)(2,1)}, bf16[2,16,8,768]{3,2,1,0:T(8,128)(2,1)S(1)}, u32[]{:S(2)}, u32[]{:S(2)}) collective-permute-start(bf16[2,16,8,768]{3,2,1,0:T(8,128)(2,1)} %get-tuple-element.40), channel_id=1, source_target_pairs={{0,28},{2,30},{4,24},{6,26},{8,20},{10,22},{12,16},{14,18},{16,12}... | collective-permute-start | bytes 1179656 | tf_op jit(solution)/shard_map/ppermute | solution.py:329
  58.2 50.3 %collective-permute-start.1 = (bf16[2,16,8,768]{3,2,1,0:T(8,128)(2,1)}, bf16[2,16,8,768]{3,2,1,0:T(8,128)(2,1)S(1)}, u32[]{:S(2)}, u32[]{:S(2)}) collective-permute-start(bf16[2,16,8,768]{3,2,1,0:T(8,128)(2,1)} %get-tuple-element.41), channel_id=1, source_target_pairs={{0,12},{2,14},{4,8},{6,10},{8,4},{10,6},{12,0},{14,2},{16,28},{18,... | collective-permute-start | bytes 1179656 | tf_op jit(solution)/shard_map/ppermute | solution.py:329
  90.6 40.9 %collective-permute-start.2 = (bf16[2,16,8,768]{3,2,1,0:T(8,128)(2,1)}, bf16[2,16,8,768]{3,2,1,0:T(8,128)(2,1)S(1)}, u32[]{:S(2)}, u32[]{:S(2)}) collective-permute-start(bf16[2,16,8,768]{3,2,1,0:T(8,128)(2,1)} %get-tuple-element.42), channel_id=1, source_target_pairs={{0,24},{2,26},{4,28},{6,30},{8,16},{10,18},{12,20},{14,22},{16,8},... | collective-permute-start | bytes 1179656 | tf_op jit(solution)/shard_map/ppermute | solution.py:329
  92.2 52.6 %collective-permute-start.3 = (bf16[2,16,8,768]{3,2,1,0:T(8,128)(2,1)}, bf16[2,16,8,768]{3,2,1,0:T(8,128)(2,1)S(1)}, u32[]{:S(2)}, u32[]{:S(2)}) collective-permute-start(bf16[2,16,8,768]{3,2,1,0:T(8,128)(2,1)} %get-tuple-element.43), channel_id=1, source_target_pairs={{0,8},{2,10},{4,12},{6,14},{8,0},{10,2},{12,4},{14,6},{16,24},{18,... | collective-permute-start | bytes 1179656 | tf_op jit(solution)/shard_map/ppermute | solution.py:329
  94.0 50.9 %all-to-all-start.1 = ((bf16[16,16,256]{2,1,0:T(8,128)(2,1)}), bf16[16,16,256]{2,1,0:T(8,128)(2,1)S(1)}, u32[]{:S(2)}, u32[]{:S(2)}) async-start(bf16[16,16,256]{2,1,0:T(8,128)(2,1)} %fusion.22), calls=%async_computation.1 | async-start | bytes 262144 | tf_op jit(solution)/shard_map/all_to_all | solution.py:308
  107.1 45.3 %collective-permute-start.4 = (bf16[2,16,8,768]{3,2,1,0:T(8,128)(2,1)}, bf16[2,16,8,768]{3,2,1,0:T(8,128)(2,1)S(1)}, u32[]{:S(2)}, u32[]{:S(2)}) collective-permute-start(bf16[2,16,8,768]{3,2,1,0:T(8,128)(2,1)} %get-tuple-element.44), channel_id=1, source_target_pairs={{0,20},{2,22},{4,16},{6,18},{8,28},{10,30},{12,24},{14,26},{16,4},... | collective-permute-start | bytes 1179656 | tf_op jit(solution)/shard_map/ppermute | solution.py:329
  107.8 48.1 %collective-permute-start.5 = (bf16[2,16,8,768]{3,2,1,0:T(8,128)(2,1)}, bf16[2,16,8,768]{3,2,1,0:T(8,128)(2,1)S(1)}, u32[]{:S(2)}, u32[]{:S(2)}) collective-permute-start(bf16[2,16,8,768]{3,2,1,0:T(8,128)(2,1)} %get-tuple-element.45), channel_id=1, source_target_pairs={{0,4},{2,6},{4,0},{6,2},{8,12},{10,14},{12,8},{14,10},{16,20},{18,... | collective-permute-start | bytes 1179656 | tf_op jit(solution)/shard_map/ppermute | solution.py:329
  108.5 52.0 %collective-permute-start.6 = (bf16[2,16,8,768]{3,2,1,0:T(8,128)(2,1)}, bf16[2,16,8,768]{3,2,1,0:T(8,128)(2,1)S(1)}, u32[]{:S(2)}, u32[]{:S(2)}) collective-permute-start(bf16[2,16,8,768]{3,2,1,0:T(8,128)(2,1)} %get-tuple-element.46), channel_id=1, source_target_pairs={{0,16},{2,18},{4,20},{6,22},{8,24},{10,26},{12,28},{14,30},{16,0},... | collective-permute-start | bytes 1179656 | tf_op jit(solution)/shard_map/ppermute | solution.py:329
  152.4 49.7 %collective-permute-start.33 = (bf16[8,16,8,768]{3,2,1,0:T(8,128)(2,1)}, bf16[8,16,8,768]{3,2,1,0:T(8,128)(2,1)}, u32[]{:S(2)}, u32[]{:S(2)}) collective-permute-start(bf16[8,16,8,768]{3,2,1,0:T(8,128)(2,1)} %shard_map.70), channel_id=1, source_target_pairs={{0,2},{2,0},{4,6},{6,4},{8,10},{10,8},{12,14},{14,12},{16,18},{18,... | collective-permute-start | bytes 4718600 | tf_op jit(solution)/shard_map/ppermute | solution.py:332
  163.7 57.3 %collective-permute-start.7 = (bf16[8,16,8,768]{3,2,1,0:T(8,128)(2,1)}, bf16[8,16,8,768]{3,2,1,0:T(8,128)(2,1)}, u32[]{:S(2)}, u32[]{:S(2)}) collective-permute-start(bf16[8,16,8,768]{3,2,1,0:T(8,128)(2,1)} %shard_map.65), channel_id=1, source_target_pairs={{0,2},{2,0},{4,6},{6,4},{8,10},{10,8},{12,14},{14,12},{16,18},{18,... | collective-permute-start | bytes 4718600 | tf_op jit(solution)/shard_map/ppermute | solution.py:332
  239.4 31.0 %collective-permute-start.37 = (bf16[2,16,8,768]{3,2,1,0:T(8,128)(2,1)}, bf16[2,16,8,768]{3,2,1,0:T(8,128)(2,1)S(1)}, u32[]{:S(2)}, u32[]{:S(2)}) collective-permute-start(bf16[2,16,8,768]{3,2,1,0:T(8,128)(2,1)} %get-tuple-element.69), channel_id=1, source_target_pairs={{0,24},{2,26},{4,28},{6,30},{8,16},{10,18},{12,20},{14,22},{16,8},... | collective-permute-start | bytes 1179656 | tf_op jit(solution)/shard_map/ppermute | solution.py:329
  240.3 37.2 %collective-permute-start.38 = (bf16[2,16,8,768]{3,2,1,0:T(8,128)(2,1)}, bf16[2,16,8,768]{3,2,1,0:T(8,128)(2,1)S(1)}, u32[]{:S(2)}, u32[]{:S(2)}) collective-permute-start(bf16[2,16,8,768]{3,2,1,0:T(8,128)(2,1)} %get-tuple-element.70), channel_id=1, source_target_pairs={{0,8},{2,10},{4,12},{6,14},{8,0},{10,2},{12,4},{14,6},{16,24},{18,... | collective-permute-start | bytes 1179656 | tf_op jit(solution)/shard_map/ppermute | solution.py:329
  242.1 68.8 %collective-permute-start.39 = (bf16[2,16,8,768]{3,2,1,0:T(8,128)(2,1)}, bf16[2,16,8,768]{3,2,1,0:T(8,128)(2,1)S(1)}, u32[]{:S(2)}, u32[]{:S(2)}) collective-permute-start(bf16[2,16,8,768]{3,2,1,0:T(8,128)(2,1)} %get-tuple-element.71), channel_id=1, source_target_pairs={{0,20},{2,22},{4,16},{6,18},{8,28},{10,30},{12,24},{14,26},{16,4},... | collective-permute-start | bytes 1179656 | tf_op jit(solution)/shard_map/ppermute | solution.py:329
  251.0 59.9 %collective-permute-start.40 = (bf16[2,16,8,768]{3,2,1,0:T(8,128)(2,1)}, bf16[2,16,8,768]{3,2,1,0:T(8,128)(2,1)S(1)}, u32[]{:S(2)}, u32[]{:S(2)}) collective-permute-start(bf16[2,16,8,768]{3,2,1,0:T(8,128)(2,1)} %get-tuple-element.72), channel_id=1, source_target_pairs={{0,4},{2,6},{4,0},{6,2},{8,12},{10,14},{12,8},{14,10},{16,20},{18,... | collective-permute-start | bytes 1179656 | tf_op jit(solution)/shard_map/ppermute | solution.py:329
  260.6 64.9 %collective-permute-start.41 = (bf16[2,16,8,768]{3,2,1,0:T(8,128)(2,1)}, bf16[2,16,8,768]{3,2,1,0:T(8,128)(2,1)S(1)}, u32[]{:S(2)}, u32[]{:S(2)}) collective-permute-start(bf16[2,16,8,768]{3,2,1,0:T(8,128)(2,1)} %get-tuple-element.73), channel_id=1, source_target_pairs={{0,16},{2,18},{4,20},{6,22},{8,24},{10,26},{12,28},{14,30},{16,0},... | collective-permute-start | bytes 1179656 | tf_op jit(solution)/shard_map/ppermute | solution.py:329
  270.3 56.9 %collective-permute-start.20 = (bf16[2,16,8,768]{3,2,1,0:T(8,128)(2,1)}, bf16[2,16,8,768]{3,2,1,0:T(8,128)(2,1)S(1)}, u32[]{:S(2)}, u32[]{:S(2)}) collective-permute-start(bf16[2,16,8,768]{3,2,1,0:T(8,128)(2,1)} %get-tuple-element.51), channel_id=1, source_target_pairs={{0,28},{2,30},{4,24},{6,26},{8,20},{10,22},{12,16},{14,18},{16,12}... | collective-permute-start | bytes 1179656 | tf_op jit(solution)/shard_map/ppermute | solution.py:329
  277.5 50.7 %collective-permute-start.21 = (bf16[2,16,8,768]{3,2,1,0:T(8,128)(2,1)}, bf16[2,16,8,768]{3,2,1,0:T(8,128)(2,1)S(1)}, u32[]{:S(2)}, u32[]{:S(2)}) collective-permute-start(bf16[2,16,8,768]{3,2,1,0:T(8,128)(2,1)} %get-tuple-element.52), channel_id=1, source_target_pairs={{0,12},{2,14},{4,8},{6,10},{8,4},{10,6},{12,0},{14,2},{16,28},{18,... | collective-permute-start | bytes 1179656 | tf_op jit(solution)/shard_map/ppermute | solution.py:329
  310.9 37.7 %collective-permute-start.22 = (bf16[2,16,8,768]{3,2,1,0:T(8,128)(2,1)}, bf16[2,16,8,768]{3,2,1,0:T(8,128)(2,1)}, u32[]{:S(2)}, u32[]{:S(2)}) collective-permute-start(bf16[2,16,8,768]{3,2,1,0:T(8,128)(2,1)} %get-tuple-element.53), channel_id=1, source_target_pairs={{0,24},{2,26},{4,28},{6,30},{8,16},{10,18},{12,20},{14,22},{16,8},... | collective-permute-start | bytes 1179656 | tf_op jit(solution)/shard_map/ppermute | solution.py:329
  311.0 37.7 %collective-permute-start.23 = (bf16[2,16,8,768]{3,2,1,0:T(8,128)(2,1)}, bf16[2,16,8,768]{3,2,1,0:T(8,128)(2,1)}, u32[]{:S(2)}, u32[]{:S(2)}) collective-permute-start(bf16[2,16,8,768]{3,2,1,0:T(8,128)(2,1)} %get-tuple-element.54), channel_id=1, source_target_pairs={{0,8},{2,10},{4,12},{6,14},{8,0},{10,2},{12,4},{14,6},{16,24},{18,... | collective-permute-start | bytes 1179656 | tf_op jit(solution)/shard_map/ppermute | solution.py:329
  325.6 44.5 %collective-permute-start.24 = (bf16[2,16,8,768]{3,2,1,0:T(8,128)(2,1)}, bf16[2,16,8,768]{3,2,1,0:T(8,128)(2,1)}, u32[]{:S(2)}, u32[]{:S(2)}) collective-permute-start(bf16[2,16,8,768]{3,2,1,0:T(8,128)(2,1)} %get-tuple-element.55), channel_id=1, source_target_pairs={{0,20},{2,22},{4,16},{6,18},{8,28},{10,30},{12,24},{14,26},{16,4},... | collective-permute-start | bytes 1179656 | tf_op jit(solution)/shard_map/ppermute | solution.py:329
  327.2 42.9 %collective-permute-start.25 = (bf16[2,16,8,768]{3,2,1,0:T(8,128)(2,1)}, bf16[2,16,8,768]{3,2,1,0:T(8,128)(2,1)}, u32[]{:S(2)}, u32[]{:S(2)}) collective-permute-start(bf16[2,16,8,768]{3,2,1,0:T(8,128)(2,1)} %get-tuple-element.56), channel_id=1, source_target_pairs={{0,4},{2,6},{4,0},{6,2},{8,12},{10,14},{12,8},{14,10},{16,20},{18,... | collective-permute-start | bytes 1179656 | tf_op jit(solution)/shard_map/ppermute | solution.py:329
  328.9 47.3 %collective-permute-start.19 = (bf16[2,16,8,768]{3,2,1,0:T(8,128)(2,1)}, bf16[2,16,8,768]{3,2,1,0:T(8,128)(2,1)S(1)}, u32[]{:S(2)}, u32[]{:S(2)}) collective-permute-start(bf16[2,16,8,768]{3,2,1,0:T(8,128)(2,1)} %get-tuple-element.50), channel_id=1, source_target_pairs={{0,16},{2,18},{4,20},{6,22},{8,24},{10,26},{12,28},{14,30},{16,0},... | collective-permute-start | bytes 1179656 | tf_op jit(solution)/shard_map/ppermute | solution.py:329
  (48 other events, 938.0 us)

commit v5 on v4

--- a/solution.py
+++ b/solution.py
@@ -403,7 +403,17 @@
         shape = prior_samples.shape
         analysis = join(half, blocks, shape, analysis, rest, regions)
         if late:
-            analysis = join(half, blocks, shape, analysis, late, regions)
+            core, partners = standing(regions)
+            for rank in late:
+                for side in range(2):
+                    first = (partners[rank] * 2 + (core ^ side)) * grid_sites
+                    for lane, cell, count in spans(half, blocks[rank].shape[-1]):
+                        analysis = lax.dynamic_update_slice_in_dim(
+                            analysis,
+                            blocks[rank][side, :, :, lane : lane + count],
+                            first + cell,
+                            axis=2,
+                        )
     return analysis
 
 

time: 381 us -> 379 us (level)
    unnamed x76 -> x74, local copies, waits for them, and re-layouts: 8.45 us -> 6.13 us
    pallas_call x10 -> x9, Pallas kernels: 28.5 us -> 26.8 us  [moved(): pl.pallas_call(kernel, in_specs=[anywhere] * len(operands), out_specs=[an...]
  transfers between devices with their start and end apart: 44 -> 44, of which waited for: 20 -> 19; matrix products, arithmetic and copies ran while one was open for 8% -> 9% of each run, Pallas kernels for 14% -> 15%
where the time goes in v5:
time: 379 us; the launch traced here: 377 us
  waiting for transfers between devices  176 us (46%)
  starting transfers between devices  104 us (27%)
  Pallas kernels  54.8 us (14%)
  other arithmetic  15 us (4%)
  matrix products  14.7 us (4%)
  local copies, waits for them, and re-layouts  10.6 us (3%)
    ppermute x28, waiting for transfers between devices, swap(): return lax.ppermute(block, 'region', pairs)  139 us
    ppermute x28, starting transfers between devices, swap(): return lax.ppermute(block, 'region', pairs)  71.4 us
    pallas_call x9, Pallas kernels, moved(): pl.pallas_call(kernel, in_specs=[anywhere] * len(operands), out_specs=[an...  26.8 us
    all_to_all x2, starting transfers between devices, spread(): lax.all_to_all(block, 'region', split_axis=0, concat_axis=0, tiled=True)  16.4 us
    pallas_call x2, Pallas kernels, transform(): pl.pallas_call(functools.partial(transform_kernel, first, chips), grid=(1...  15 us
    pallas_call x1, Pallas kernels, gather_observed(): pl.pallas_call(gather_kernel, grid=(regions,), in_specs=[pl.BlockSpec((1,...  13.1 us
    all_to_all x2, waiting for transfers between devices, spread(): lax.all_to_all(block, 'region', split_axis=0, concat_axis=0, tiled=True)  12.3 us
    ppermute x1, waiting for transfers between devices, analyse(): opposite = lax.ppermute(weights, 'level', flip)  8.27 us
  transfers between devices with their start and end apart: 44, of which 19 were waited for; matrix products, arithmetic and copies ran while one was open for 9% of the time, Pallas kernels for 15%

profile of v5, /device:TPU:1, one launch (start us, length us, event | category | flops | bytes accessed | tf_op | source)
XLA Modules:
  0.0 376.7 jit_solution(13793564368428244237)
XLA Ops:
  5.9 6.5 %all-to-all-start = ((f32[16,1,512]{2,1,0:T(1,128)}), f32[16,1,512]{2,1,0:T(1,128)S(1)}, u32[]{:S(2)}, u32[]{:S(2)}) async-start(f32[16,1,512]{2,1,0:T(1,128)} %broadcast_in_dim.19), calls=%async_computation | async-start | bytes 65536 | tf_op jit(solution)/shard_map/all_to_all | solution.py:308
  12.4 3.1 shard_map.69
  23.3 3.6 shard_map.64
  29.7 13.1 %gather_observed.1 = bf16[2,16,16,256]{3,2,1,0:T(8,128)(2,1)} custom-call(s32[16,1,512]{2,1,0:T(1,128)} %get-tuple-element.91.cell_ref, s32[16,1,512]{2,1,0:T(1,128)} %get-tuple-element.90.level_ref, bf16[16,8,24576]{2,1,0:T(8,128)(2,1)} %prior_ref.5), custom_call_target="tpu_custom_call" | custom-call | tf_op jit(solution)/shard_map/gather_observed/pallas_call | solution.py:61
  52.5 3.2 collective-permute-start
  58.6 34.5 %collective-permute-done.31.refs_6_ = bf16[2,16,8,768]{3,2,1,0:T(8,128)(2,1)S(1)} collective-permute-done((bf16[2,16,8,768]{3,2,1,0:T(8,128)(2,1)}, bf16[2,16,8,768]{3,2,1,0:T(8,128)(2,1)S(1)}, u32[]{:S(2)}, u32[]{:S(2)}) %collective-permute-start.31) | collective-permute-done | bytes 393248 | tf_op jit(solution)/shard_map/ppermute | solution.py:329
  94.8 10.0 %all-to-all-start.1 = ((bf16[16,16,256]{2,1,0:T(8,128)(2,1)}), bf16[16,16,256]{2,1,0:T(8,128)(2,1)S(1)}, u32[]{:S(2)}, u32[]{:S(2)}) async-start(bf16[16,16,256]{2,1,0:T(8,128)(2,1)} %fusion.24), calls=%async_computation.1 | async-start | bytes 262144 | tf_op jit(solution)/shard_map/all_to_all | solution.py:308
  104.8 3.2 collective-permute-start.4
  108.4 17.4 %collective-permute-start.6 = (bf16[2,16,8,768]{3,2,1,0:T(8,128)(2,1)}, bf16[2,16,8,768]{3,2,1,0:T(8,128)(2,1)S(1)}, u32[]{:S(2)}, u32[]{:S(2)}) collective-permute-start(bf16[2,16,8,768]{3,2,1,0:T(8,128)(2,1)} %get-tuple-element.46), channel_id=1, source_target_pairs={{0,16},{2,18},{4,20},{6,22},{8,24},{10,26},{12,28},{14,30},{16,0},... | collective-permute-start | bytes 1179656 | tf_op jit(solution)/shard_map/ppermute | solution.py:329
  129.6 12.3 %all-to-all-done.1 = bf16[16,16,256]{2,1,0:T(8,128)(2,1)S(1)} async-done(((bf16[16,16,256]{2,1,0:T(8,128)(2,1)}), bf16[16,16,256]{2,1,0:T(8,128)(2,1)S(1)}, u32[]{:S(2)}, u32[]{:S(2)}) %all-to-all-start.1) | async-done | bytes 131104 | tf_op jit(solution)/shard_map/all_to_all | solution.py:308
  147.4 4.8 %collective-permute-done.4.refs_4_ = bf16[2,16,8,768]{3,2,1,0:T(8,128)(2,1)S(1)} collective-permute-done((bf16[2,16,8,768]{3,2,1,0:T(8,128)(2,1)}, bf16[2,16,8,768]{3,2,1,0:T(8,128)(2,1)S(1)}, u32[]{:S(2)}, u32[]{:S(2)}) %collective-permute-start.4) | collective-permute-done | bytes 393248 | tf_op jit(solution)/shard_map/ppermute | solution.py:329
  152.8 6.6 %collective-permute-done.6.refs_6_ = bf16[2,16,8,768]{3,2,1,0:T(8,128)(2,1)S(1)} collective-permute-done((bf16[2,16,8,768]{3,2,1,0:T(8,128)(2,1)}, bf16[2,16,8,768]{3,2,1,0:T(8,128)(2,1)S(1)}, u32[]{:S(2)}, u32[]{:S(2)}) %collective-permute-start.6) | collective-permute-done | bytes 393248 | tf_op jit(solution)/shard_map/ppermute | solution.py:329
  168.2 5.6 %collective-permute-done.12 = bf16[256,512]{1,0:T(8,128)(2,1)S(1)} collective-permute-done((bf16[256,512]{1,0:T(8,128)(2,1)S(1)}, bf16[256,512]{1,0:T(8,128)(2,1)S(1)}, u32[]{:S(2)}, u32[]{:S(2)}) %collective-permute-start.12) | collective-permute-done | bytes 262176 | tf_op jit(solution)/shard_map/ppermute | solution.py:359
  191.5 8.3 %collective-permute-done.15.refs_10_ = bf16[3,256,256]{2,1,0:T(8,128)(2,1)S(1)} collective-permute-done((bf16[3,256,256]{2,1,0:T(8,128)(2,1)S(1)}, bf16[3,256,256]{2,1,0:T(8,128)(2,1)S(1)}, u32[]{:S(2)}, u32[]{:S(2)}) %collective-permute-start.15) | collective-permute-done | bytes 393248 | tf_op jit(solution)/shard_map/ppermute | solution.py:379
  200.5 7.4 %shard_map.71 = (bf16[8,16,8,768]{3,2,1,0:T(8,128)(2,1)}, bf16[8,16,8,768]{3,2,1,0:T(8,128)(2,1)}) custom-call(bf16[2,16,8,768]{3,2,1,0:T(8,128)(2,1)} %copy-done.16, bf16[2,16,8,768]{3,2,1,0:T(8,128)(2,1)} %copy-done.10, bf16[2,16,8,768]{3,2,1,0:T(8,128)(2,1)} %copy-done.11, bf16[2,16,8,768]{3,2,1,0:T(8,128)(2,1)} %copy-done.12, ...), custom_call_target="tpu_custom_call" | custom-call | tf_op jit(solution)/shard_map/pallas_call | solution.py:258
  210.3 4.4 %collective-permute-done.16.refs_11_ = bf16[1,256,256]{2,1,0:T(8,128)(2,1)S(1)} collective-permute-done((bf16[1,256,256]{2,1,0:T(8,128)(2,1)S(1)}, bf16[1,256,256]{2,1,0:T(8,128)(2,1)S(1)}, u32[]{:S(2)}, u32[]{:S(2)}) %collective-permute-start.16) | collective-permute-done | bytes 131104 | tf_op jit(solution)/shard_map/ppermute | solution.py:383
  215.1 3.4 collective-permute-done.17.refs_12_
  219.2 7.5 %shard_map.66 = (bf16[8,16,8,768]{3,2,1,0:T(8,128)(2,1)}, bf16[8,16,8,768]{3,2,1,0:T(8,128)(2,1)}) custom-call(bf16[2,16,8,768]{3,2,1,0:T(8,128)(2,1)} %copy-done.1, bf16[2,16,8,768]{3,2,1,0:T(8,128)(2,1)} %copy-done.2, bf16[2,16,8,768]{3,2,1,0:T(8,128)(2,1)} %copy-done.3, bf16[2,16,8,768]{3,2,1,0:T(8,128)(2,1)} %copy-done.4, ...), custom_call_target="tpu_custom_call" | custom-call | tf_op jit(solution)/shard_map/pallas_call | solution.py:258
  226.7 3.6 collective-permute-start.18
  231.4 3.5 shard_map.72
  241.6 3.5 shard_map.67
  245.0 3.6 collective-permute-done.34.refs_0_
  248.6 10.1 %collective-permute-done.35.refs_1_ = bf16[2,16,8,768]{3,2,1,0:T(8,128)(2,1)S(1)} collective-permute-done((bf16[2,16,8,768]{3,2,1,0:T(8,128)(2,1)}, bf16[2,16,8,768]{3,2,1,0:T(8,128)(2,1)S(1)}, u32[]{:S(2)}, u32[]{:S(2)}) %collective-permute-start.35) | collective-permute-done | bytes 393248 | tf_op jit(solution)/shard_map/ppermute | solution.py:329
  260.6 7.1 %collective-permute-done.36.refs_2_ = bf16[2,16,8,768]{3,2,1,0:T(8,128)(2,1)S(1)} collective-permute-done((bf16[2,16,8,768]{3,2,1,0:T(8,128)(2,1)}, bf16[2,16,8,768]{3,2,1,0:T(8,128)(2,1)S(1)}, u32[]{:S(2)}, u32[]{:S(2)}) %collective-permute-start.36) | collective-permute-done | bytes 393248 | tf_op jit(solution)/shard_map/ppermute | solution.py:329
  267.7 5.0 %collective-permute-start.19 = (bf16[2,16,8,768]{3,2,1,0:T(8,128)(2,1)}, bf16[2,16,8,768]{3,2,1,0:T(8,128)(2,1)S(1)}, u32[]{:S(2)}, u32[]{:S(2)}) collective-permute-start(bf16[2,16,8,768]{3,2,1,0:T(8,128)(2,1)} %get-tuple-element.50), channel_id=1, source_target_pairs={{0,28},{2,30},{4,24},{6,26},{8,20},{10,22},{12,16},{14,18},{16,12}... | collective-permute-start | bytes 1179656 | tf_op jit(solution)/shard_map/ppermute | solution.py:329
  275.6 3.7 collective-permute-start.20
  279.4 29.1 %collective-permute-done.38.refs_4_ = bf16[2,16,8,768]{3,2,1,0:T(8,128)(2,1)S(1)} collective-permute-done((bf16[2,16,8,768]{3,2,1,0:T(8,128)(2,1)}, bf16[2,16,8,768]{3,2,1,0:T(8,128)(2,1)S(1)}, u32[]{:S(2)}, u32[]{:S(2)}) %collective-permute-start.38) | collective-permute-done | bytes 393248 | tf_op jit(solution)/shard_map/ppermute | solution.py:329
  308.6 14.9 %collective-permute-done.40.refs_6_ = bf16[2,16,8,768]{3,2,1,0:T(8,128)(2,1)S(1)} collective-permute-done((bf16[2,16,8,768]{3,2,1,0:T(8,128)(2,1)}, bf16[2,16,8,768]{3,2,1,0:T(8,128)(2,1)S(1)}, u32[]{:S(2)}, u32[]{:S(2)}) %collective-permute-start.40) | collective-permute-done | bytes 393248 | tf_op jit(solution)/shard_map/ppermute | solution.py:329
  326.5 16.1 %collective-permute-start.41 = (bf16[2,16,8,768]{3,2,1,0:T(8,128)(2,1)}, bf16[2,16,8,768]{3,2,1,0:T(8,128)(2,1)S(1)}, u32[]{:S(2)}, u32[]{:S(2)}) collective-permute-start(bf16[2,16,8,768]{3,2,1,0:T(8,128)(2,1)} %get-tuple-element.74), channel_id=1, source_target_pairs={{0,16},{2,18},{4,20},{6,22},{8,24},{10,26},{12,28},{14,30},{16,0},... | collective-permute-start | bytes 1179656 | tf_op jit(solution)/shard_map/ppermute | solution.py:329
  342.7 3.5 shard_map.73.refs_7_
  346.2 21.4 %collective-permute-done.23.refs_4_ = bf16[2,16,8,768]{3,2,1,0:T(8,128)(2,1)} collective-permute-done((bf16[2,16,8,768]{3,2,1,0:T(8,128)(2,1)}, bf16[2,16,8,768]{3,2,1,0:T(8,128)(2,1)}, u32[]{:S(2)}, u32[]{:S(2)}) %collective-permute-start.23) | collective-permute-done | bytes 393248 | tf_op jit(solution)/shard_map/ppermute | solution.py:329
  370.7 3.4 collective-permute-done.41
  (202 shorter events, 91.3 us)
Async XLA Ops:
  2.0 25.5 %collective-permute-start.13 = (f32[2,512]{1,0:T(2,128)S(1)}, f32[2,512]{1,0:T(2,128)S(1)}, u32[]{:S(2)}, u32[]{:S(2)}) collective-permute-start(f32[2,512]{1,0:T(2,128)S(1)} %pad_maximum_fusion.1), channel_id=1, source_target_pairs={{0,2},{2,4},{4,6},{6,8},{8,10},{10,12},{12,14},{14,16},{16,18},{18... | collective-permute-start | bytes 12296 | tf_op jit(solution)/shard_map/ppermute | solution.py:342
  4.6 39.1 %collective-permute-start.14 = (f32[2,512]{1,0:T(2,128)S(1)}, f32[2,512]{1,0:T(2,128)S(1)}, u32[]{:S(2)}, u32[]{:S(2)}) collective-permute-start(f32[2,512]{1,0:T(2,128)S(1)} %pad_maximum_fusion.1), channel_id=1, source_target_pairs={{2,0},{4,2},{6,4},{8,6},{10,8},{12,10},{14,12},{16,14},{18,16},{20... | collective-permute-start | bytes 12296 | tf_op jit(solution)/shard_map/ppermute | solution.py:342
  5.9 22.9 %all-to-all-start = ((f32[16,1,512]{2,1,0:T(1,128)}), f32[16,1,512]{2,1,0:T(1,128)S(1)}, u32[]{:S(2)}, u32[]{:S(2)}) async-start(f32[16,1,512]{2,1,0:T(1,128)} %broadcast_in_dim.19), calls=%async_computation | async-start | bytes 65536 | tf_op jit(solution)/shard_map/all_to_all | solution.py:308
  15.5 33.6 %collective-permute-start.26 = (bf16[2,16,8,768]{3,2,1,0:T(8,128)(2,1)}, bf16[2,16,8,768]{3,2,1,0:T(8,128)(2,1)S(1)}, u32[]{:S(2)}, u32[]{:S(2)}) collective-permute-start(bf16[2,16,8,768]{3,2,1,0:T(8,128)(2,1)} %get-tuple-element.57), channel_id=1, source_target_pairs={{0,12},{2,14},{4,8},{6,10},{8,4},{10,6},{12,0},{14,2},{16,28},{18,... | collective-permute-start | bytes 1179656 | tf_op jit(solution)/shard_map/ppermute | solution.py:329
  17.8 33.6 %collective-permute-start.27 = (bf16[2,16,8,768]{3,2,1,0:T(8,128)(2,1)}, bf16[2,16,8,768]{3,2,1,0:T(8,128)(2,1)S(1)}, u32[]{:S(2)}, u32[]{:S(2)}) collective-permute-start(bf16[2,16,8,768]{3,2,1,0:T(8,128)(2,1)} %get-tuple-element.58), channel_id=1, source_target_pairs={{0,24},{2,26},{4,28},{6,30},{8,16},{10,18},{12,20},{14,22},{16,8},... | collective-permute-start | bytes 1179656 | tf_op jit(solution)/shard_map/ppermute | solution.py:329
  19.9 32.6 %collective-permute-start.28 = (bf16[2,16,8,768]{3,2,1,0:T(8,128)(2,1)}, bf16[2,16,8,768]{3,2,1,0:T(8,128)(2,1)S(1)}, u32[]{:S(2)}, u32[]{:S(2)}) collective-permute-start(bf16[2,16,8,768]{3,2,1,0:T(8,128)(2,1)} %get-tuple-element.59), channel_id=1, source_target_pairs={{0,8},{2,10},{4,12},{6,14},{8,0},{10,2},{12,4},{14,6},{16,24},{18,... | collective-permute-start | bytes 1179656 | tf_op jit(solution)/shard_map/ppermute | solution.py:329
  27.6 28.2 %collective-permute-start.29 = (bf16[2,16,8,768]{3,2,1,0:T(8,128)(2,1)}, bf16[2,16,8,768]{3,2,1,0:T(8,128)(2,1)S(1)}, u32[]{:S(2)}, u32[]{:S(2)}) collective-permute-start(bf16[2,16,8,768]{3,2,1,0:T(8,128)(2,1)} %get-tuple-element.60), channel_id=1, source_target_pairs={{0,20},{2,22},{4,16},{6,18},{8,28},{10,30},{12,24},{14,26},{16,4},... | collective-permute-start | bytes 1179656 | tf_op jit(solution)/shard_map/ppermute | solution.py:329
  49.1 44.0 %collective-permute-start.31 = (bf16[2,16,8,768]{3,2,1,0:T(8,128)(2,1)}, bf16[2,16,8,768]{3,2,1,0:T(8,128)(2,1)S(1)}, u32[]{:S(2)}, u32[]{:S(2)}) collective-permute-start(bf16[2,16,8,768]{3,2,1,0:T(8,128)(2,1)} %get-tuple-element.62), channel_id=1, source_target_pairs={{0,16},{2,18},{4,20},{6,22},{8,24},{10,26},{12,28},{14,30},{16,0},... | collective-permute-start | bytes 1179656 | tf_op jit(solution)/shard_map/ppermute | solution.py:329
  51.5 53.3 %collective-permute-start.25 = (bf16[2,16,8,768]{3,2,1,0:T(8,128)(2,1)S(1)}, bf16[2,16,8,768]{3,2,1,0:T(8,128)(2,1)S(1)}, u32[]{:S(2)}, u32[]{:S(2)}) collective-permute-start(bf16[2,16,8,768]{3,2,1,0:T(8,128)(2,1)S(1)} %copy-done.25), channel_id=1, source_target_pairs={{0,28},{2,30},{4,24},{6,26},{8,20},{10,22},{12,16},{14,18},{16,12}... | collective-permute-start | bytes 1179656 | tf_op jit(solution)/shard_map/ppermute | solution.py:329
  52.5 55.5 %collective-permute-start = (bf16[2,16,8,768]{3,2,1,0:T(8,128)(2,1)}, bf16[2,16,8,768]{3,2,1,0:T(8,128)(2,1)S(1)}, u32[]{:S(2)}, u32[]{:S(2)}) collective-permute-start(bf16[2,16,8,768]{3,2,1,0:T(8,128)(2,1)} %get-tuple-element.40), channel_id=1, source_target_pairs={{0,28},{2,30},{4,24},{6,26},{8,20},{10,22},{12,16},{14,18},{16,12}... | collective-permute-start | bytes 1179656 | tf_op jit(solution)/shard_map/ppermute | solution.py:329
  55.8 52.6 %collective-permute-start.1 = (bf16[2,16,8,768]{3,2,1,0:T(8,128)(2,1)}, bf16[2,16,8,768]{3,2,1,0:T(8,128)(2,1)S(1)}, u32[]{:S(2)}, u32[]{:S(2)}) collective-permute-start(bf16[2,16,8,768]{3,2,1,0:T(8,128)(2,1)} %get-tuple-element.41), channel_id=1, source_target_pairs={{0,12},{2,14},{4,8},{6,10},{8,4},{10,6},{12,0},{14,2},{16,28},{18,... | collective-permute-start | bytes 1179656 | tf_op jit(solution)/shard_map/ppermute | solution.py:329
  56.5 73.0 %collective-permute-start.2 = (bf16[2,16,8,768]{3,2,1,0:T(8,128)(2,1)}, bf16[2,16,8,768]{3,2,1,0:T(8,128)(2,1)S(1)}, u32[]{:S(2)}, u32[]{:S(2)}) collective-permute-start(bf16[2,16,8,768]{3,2,1,0:T(8,128)(2,1)} %get-tuple-element.42), channel_id=1, source_target_pairs={{0,24},{2,26},{4,28},{6,30},{8,16},{10,18},{12,20},{14,22},{16,8},... | collective-permute-start | bytes 1179656 | tf_op jit(solution)/shard_map/ppermute | solution.py:329
  93.1 50.5 %collective-permute-start.3 = (bf16[2,16,8,768]{3,2,1,0:T(8,128)(2,1)}, bf16[2,16,8,768]{3,2,1,0:T(8,128)(2,1)S(1)}, u32[]{:S(2)}, u32[]{:S(2)}) collective-permute-start(bf16[2,16,8,768]{3,2,1,0:T(8,128)(2,1)} %get-tuple-element.43), channel_id=1, source_target_pairs={{0,8},{2,10},{4,12},{6,14},{8,0},{10,2},{12,4},{14,6},{16,24},{18,... | collective-permute-start | bytes 1179656 | tf_op jit(solution)/shard_map/ppermute | solution.py:329
  94.8 47.1 %all-to-all-start.1 = ((bf16[16,16,256]{2,1,0:T(8,128)(2,1)}), bf16[16,16,256]{2,1,0:T(8,128)(2,1)S(1)}, u32[]{:S(2)}, u32[]{:S(2)}) async-start(bf16[16,16,256]{2,1,0:T(8,128)(2,1)} %fusion.24), calls=%async_computation.1 | async-start | bytes 262144 | tf_op jit(solution)/shard_map/all_to_all | solution.py:308
  104.8 47.4 %collective-permute-start.4 = (bf16[2,16,8,768]{3,2,1,0:T(8,128)(2,1)}, bf16[2,16,8,768]{3,2,1,0:T(8,128)(2,1)S(1)}, u32[]{:S(2)}, u32[]{:S(2)}) collective-permute-start(bf16[2,16,8,768]{3,2,1,0:T(8,128)(2,1)} %get-tuple-element.44), channel_id=1, source_target_pairs={{0,20},{2,22},{4,16},{6,18},{8,28},{10,30},{12,24},{14,26},{16,4},... | collective-permute-start | bytes 1179656 | tf_op jit(solution)/shard_map/ppermute | solution.py:329
  108.0 44.8 %collective-permute-start.5 = (bf16[2,16,8,768]{3,2,1,0:T(8,128)(2,1)}, bf16[2,16,8,768]{3,2,1,0:T(8,128)(2,1)S(1)}, u32[]{:S(2)}, u32[]{:S(2)}) collective-permute-start(bf16[2,16,8,768]{3,2,1,0:T(8,128)(2,1)} %get-tuple-element.45), channel_id=1, source_target_pairs={{0,4},{2,6},{4,0},{6,2},{8,12},{10,14},{12,8},{14,10},{16,20},{18,... | collective-permute-start | bytes 1179656 | tf_op jit(solution)/shard_map/ppermute | solution.py:329
  108.4 51.0 %collective-permute-start.6 = (bf16[2,16,8,768]{3,2,1,0:T(8,128)(2,1)}, bf16[2,16,8,768]{3,2,1,0:T(8,128)(2,1)S(1)}, u32[]{:S(2)}, u32[]{:S(2)}) collective-permute-start(bf16[2,16,8,768]{3,2,1,0:T(8,128)(2,1)} %get-tuple-element.46), channel_id=1, source_target_pairs={{0,16},{2,18},{4,20},{6,22},{8,24},{10,26},{12,28},{14,30},{16,0},... | collective-permute-start | bytes 1179656 | tf_op jit(solution)/shard_map/ppermute | solution.py:329
  141.9 22.7 %collective-permute-start.9 = (bf16[256,256]{1,0:T(8,128)(2,1)S(1)}, bf16[256,256]{1,0:T(8,128)(2,1)}, u32[]{:S(2)}, u32[]{:S(2)}) collective-permute-start(bf16[256,256]{1,0:T(8,128)(2,1)S(1)} %bitcast.127), channel_id=1, source_target_pairs={{0,2},{2,4},{4,6},{6,8},{8,10},{10,12},{12,14},{14,16},{16,18},{18... | collective-permute-start | bytes 393224 | tf_op jit(solution)/shard_map/ppermute | solution.py:355
  152.2 47.6 %collective-permute-start.32 = (bf16[8,16,8,768]{3,2,1,0:T(8,128)(2,1)}, bf16[8,16,8,768]{3,2,1,0:T(8,128)(2,1)}, u32[]{:S(2)}, u32[]{:S(2)}) collective-permute-start(bf16[8,16,8,768]{3,2,1,0:T(8,128)(2,1)} %shard_map.70), channel_id=1, source_target_pairs={{0,2},{2,0},{4,6},{6,4},{8,10},{10,8},{12,14},{14,12},{16,18},{18,... | collective-permute-start | bytes 4718600 | tf_op jit(solution)/shard_map/ppermute | solution.py:332
  162.6 55.9 %collective-permute-start.7 = (bf16[8,16,8,768]{3,2,1,0:T(8,128)(2,1)}, bf16[8,16,8,768]{3,2,1,0:T(8,128)(2,1)}, u32[]{:S(2)}, u32[]{:S(2)}) collective-permute-start(bf16[8,16,8,768]{3,2,1,0:T(8,128)(2,1)} %shard_map.65), channel_id=1, source_target_pairs={{0,2},{2,0},{4,6},{6,4},{8,10},{10,8},{12,14},{14,12},{16,18},{18,... | collective-permute-start | bytes 4718600 | tf_op jit(solution)/shard_map/ppermute | solution.py:332
  237.3 30.4 %collective-permute-start.36 = (bf16[2,16,8,768]{3,2,1,0:T(8,128)(2,1)}, bf16[2,16,8,768]{3,2,1,0:T(8,128)(2,1)S(1)}, u32[]{:S(2)}, u32[]{:S(2)}) collective-permute-start(bf16[2,16,8,768]{3,2,1,0:T(8,128)(2,1)} %get-tuple-element.68), channel_id=1, source_target_pairs={{0,24},{2,26},{4,28},{6,30},{8,16},{10,18},{12,20},{14,22},{16,8},... | collective-permute-start | bytes 1179656 | tf_op jit(solution)/shard_map/ppermute | solution.py:329
  237.6 38.0 %collective-permute-start.37 = (bf16[2,16,8,768]{3,2,1,0:T(8,128)(2,1)}, bf16[2,16,8,768]{3,2,1,0:T(8,128)(2,1)S(1)}, u32[]{:S(2)}, u32[]{:S(2)}) collective-permute-start(bf16[2,16,8,768]{3,2,1,0:T(8,128)(2,1)} %get-tuple-element.69), channel_id=1, source_target_pairs={{0,8},{2,10},{4,12},{6,14},{8,0},{10,2},{12,4},{14,6},{16,24},{18,... | collective-permute-start | bytes 1179656 | tf_op jit(solution)/shard_map/ppermute | solution.py:329
  239.7 68.8 %collective-permute-start.38 = (bf16[2,16,8,768]{3,2,1,0:T(8,128)(2,1)}, bf16[2,16,8,768]{3,2,1,0:T(8,128)(2,1)S(1)}, u32[]{:S(2)}, u32[]{:S(2)}) collective-permute-start(bf16[2,16,8,768]{3,2,1,0:T(8,128)(2,1)} %get-tuple-element.70), channel_id=1, source_target_pairs={{0,20},{2,22},{4,16},{6,18},{8,28},{10,30},{12,24},{14,26},{16,4},... | collective-permute-start | bytes 1179656 | tf_op jit(solution)/shard_map/ppermute | solution.py:329
  248.6 59.9 %collective-permute-start.39 = (bf16[2,16,8,768]{3,2,1,0:T(8,128)(2,1)}, bf16[2,16,8,768]{3,2,1,0:T(8,128)(2,1)S(1)}, u32[]{:S(2)}, u32[]{:S(2)}) collective-permute-start(bf16[2,16,8,768]{3,2,1,0:T(8,128)(2,1)} %get-tuple-element.71), channel_id=1, source_target_pairs={{0,4},{2,6},{4,0},{6,2},{8,12},{10,14},{12,8},{14,10},{16,20},{18,... | collective-permute-start | bytes 1179656 | tf_op jit(solution)/shard_map/ppermute | solution.py:329
  258.7 64.8 %collective-permute-start.40 = (bf16[2,16,8,768]{3,2,1,0:T(8,128)(2,1)}, bf16[2,16,8,768]{3,2,1,0:T(8,128)(2,1)S(1)}, u32[]{:S(2)}, u32[]{:S(2)}) collective-permute-start(bf16[2,16,8,768]{3,2,1,0:T(8,128)(2,1)} %get-tuple-element.72), channel_id=1, source_target_pairs={{0,16},{2,18},{4,20},{6,22},{8,24},{10,26},{12,28},{14,30},{16,0},... | collective-permute-start | bytes 1179656 | tf_op jit(solution)/shard_map/ppermute | solution.py:329
  267.7 57.0 %collective-permute-start.19 = (bf16[2,16,8,768]{3,2,1,0:T(8,128)(2,1)}, bf16[2,16,8,768]{3,2,1,0:T(8,128)(2,1)S(1)}, u32[]{:S(2)}, u32[]{:S(2)}) collective-permute-start(bf16[2,16,8,768]{3,2,1,0:T(8,128)(2,1)} %get-tuple-element.50), channel_id=1, source_target_pairs={{0,28},{2,30},{4,24},{6,26},{8,20},{10,22},{12,16},{14,18},{16,12}... | collective-permute-start | bytes 1179656 | tf_op jit(solution)/shard_map/ppermute | solution.py:329
  275.6 50.1 %collective-permute-start.20 = (bf16[2,16,8,768]{3,2,1,0:T(8,128)(2,1)}, bf16[2,16,8,768]{3,2,1,0:T(8,128)(2,1)S(1)}, u32[]{:S(2)}, u32[]{:S(2)}) collective-permute-start(bf16[2,16,8,768]{3,2,1,0:T(8,128)(2,1)} %get-tuple-element.51), channel_id=1, source_target_pairs={{0,12},{2,14},{4,8},{6,10},{8,4},{10,6},{12,0},{14,2},{16,28},{18,... | collective-permute-start | bytes 1179656 | tf_op jit(solution)/shard_map/ppermute | solution.py:329
  308.5 37.7 %collective-permute-start.21 = (bf16[2,16,8,768]{3,2,1,0:T(8,128)(2,1)}, bf16[2,16,8,768]{3,2,1,0:T(8,128)(2,1)}, u32[]{:S(2)}, u32[]{:S(2)}) collective-permute-start(bf16[2,16,8,768]{3,2,1,0:T(8,128)(2,1)} %get-tuple-element.52), channel_id=1, source_target_pairs={{0,24},{2,26},{4,28},{6,30},{8,16},{10,18},{12,20},{14,22},{16,8},... | collective-permute-start | bytes 1179656 | tf_op jit(solution)/shard_map/ppermute | solution.py:329
  308.5 37.7 %collective-permute-start.22 = (bf16[2,16,8,768]{3,2,1,0:T(8,128)(2,1)}, bf16[2,16,8,768]{3,2,1,0:T(8,128)(2,1)}, u32[]{:S(2)}, u32[]{:S(2)}) collective-permute-start(bf16[2,16,8,768]{3,2,1,0:T(8,128)(2,1)} %get-tuple-element.53), channel_id=1, source_target_pairs={{0,8},{2,10},{4,12},{6,14},{8,0},{10,2},{12,4},{14,6},{16,24},{18,... | collective-permute-start | bytes 1179656 | tf_op jit(solution)/shard_map/ppermute | solution.py:329
  323.5 44.1 %collective-permute-start.23 = (bf16[2,16,8,768]{3,2,1,0:T(8,128)(2,1)}, bf16[2,16,8,768]{3,2,1,0:T(8,128)(2,1)}, u32[]{:S(2)}, u32[]{:S(2)}) collective-permute-start(bf16[2,16,8,768]{3,2,1,0:T(8,128)(2,1)} %get-tuple-element.54), channel_id=1, source_target_pairs={{0,20},{2,22},{4,16},{6,18},{8,28},{10,30},{12,24},{14,26},{16,4},... | collective-permute-start | bytes 1179656 | tf_op jit(solution)/shard_map/ppermute | solution.py:329
  324.8 42.9 %collective-permute-start.24 = (bf16[2,16,8,768]{3,2,1,0:T(8,128)(2,1)}, bf16[2,16,8,768]{3,2,1,0:T(8,128)(2,1)}, u32[]{:S(2)}, u32[]{:S(2)}) collective-permute-start(bf16[2,16,8,768]{3,2,1,0:T(8,128)(2,1)} %get-tuple-element.55), channel_id=1, source_target_pairs={{0,4},{2,6},{4,0},{6,2},{8,12},{10,14},{12,8},{14,10},{16,20},{18,... | collective-permute-start | bytes 1179656 | tf_op jit(solution)/shard_map/ppermute | solution.py:329
  326.5 47.6 %collective-permute-start.41 = (bf16[2,16,8,768]{3,2,1,0:T(8,128)(2,1)}, bf16[2,16,8,768]{3,2,1,0:T(8,128)(2,1)S(1)}, u32[]{:S(2)}, u32[]{:S(2)}) collective-permute-start(bf16[2,16,8,768]{3,2,1,0:T(8,128)(2,1)} %get-tuple-element.74), channel_id=1, source_target_pairs={{0,16},{2,18},{4,20},{6,22},{8,24},{10,26},{12,28},{14,30},{16,0},... | collective-permute-start | bytes 1179656 | tf_op jit(solution)/shard_map/ppermute | solution.py:329
  (47 other events, 942.9 us)
